TPU v7x, 32 devices: a whole 2x2x4 slice. The times are simulated.
32 devices in a mesh: lon: 4 (over y, x), lat: 4 (over z), comp: 2 (over core).
Axes of the slice: x: 2, y: 2, z: 4, core: 2. Of those that a mesh axis runs over, the one named last changes fastest.
Arguments:
- ocean_state: float32 [4, 80, 32, 1024], P(None, None, 'lon', ('lat', 'comp')), may hold values from -6 to 6
- level_count: int32 [32, 1024], P('lon', ('lat', 'comp')), may hold values from 0 to 80, as said below
- mix_rate: float32 [80, 32, 1024], P(None, 'lon', ('lat', 'comp')), may hold values from 0.05 to 5
- atmos_flux: bfloat16 [8, 16, 4, 256], P(('lat', 'comp'), 'lon'), may hold values from -6 to 6
- remap_weight: bfloat16 [8, 16, 256, 128], P(('lat', 'comp'), 'lon'), may hold values from -0.375 to 0.375
- remap_target: int32 [8, 16], P(('lat', 'comp'), 'lon'), may hold values from 0 to 3, as said below
- remap_slot: int32 [8, 16], P(('lat', 'comp'), 'lon'), may hold values from 0 to 7
Outputs:
- ocean_next: float32 [4, 80, 32, 1024], P(None, None, 'lon', ('lat', 'comp'))
Inputs may be any that keep to these rules, and one draw needn't show every extreme that they name: `level_count`: 0 marks a land column. `remap_target`: among the blocks of one device each longitude tile index appears exactly 1 times.
All inputs are finite; a program needn't handle non-finite values.
Results may differ from a plain program's by a relative error of at most 0.0003.
Values sent between devices are 32-bit elements; how exact they have to be, the bound alone decides.
No kernel may reach another device: no remote copies, remote signals or barrier semaphores. Data moves between devices by JAX's collectives and lax.ppermute only.
A program may use at most 128 MiB of HBM per device.

v0:
```python
import jax
import jax.numpy as jnp
from jax import lax
from jax.sharding import PartitionSpec as P

SUBSTEPS = 2


DIFFUSE = 0.2
VISCOUS = 0.2
ADVECTION = 0.5
THERMAL = 0.2
HALINE = 0.15
GRAVITY = 0.05
CORIOLIS = 0.3
SURFACE_GAIN = (0.5, 0.4, 0.6, 0.6)


def with_halo(block, sides, width, periodic):
    for axis, dim in sides:
        count = lax.axis_size(axis)
        forward = [(i, i + 1) for i in range(count - 1)]
        if periodic:
            forward.append((count - 1, 0))
        backward = [(target, source) for source, target in forward]
        low = lax.ppermute(
            lax.slice_in_dim(block, block.shape[dim] - width, None, axis=dim), axis, forward
        )
        high = lax.ppermute(lax.slice_in_dim(block, 0, width, axis=dim), axis, backward)
        block = jnp.concatenate([low, block, high], axis=dim)
    return block


def centre_of(values):
    return values[..., 1:-1, 1:-1]


def east_of(values):
    return values[..., 2:, 1:-1]


def west_of(values):
    return values[..., :-2, 1:-1]


def north_of(values):
    return values[..., 1:-1, 2:]


def south_of(values):
    return values[..., 1:-1, :-2]


def laplace(values, wet_padded):
    middle = centre_of(values)
    total = east_of(wet_padded) * (east_of(values) - middle)
    total = total + west_of(wet_padded) * (west_of(values) - middle)
    total = total + north_of(wet_padded) * (north_of(values) - middle)
    total = total + south_of(wet_padded) * (south_of(values) - middle)
    return total


def vertical_mix(tendency, rate, wet_mask):
    level_total = tendency.shape[1]
    coupling = rate[:-1] * wet_mask[:-1] * wet_mask[1:]
    zero_level = jnp.zeros_like(rate[:1])
    upper = jnp.concatenate([coupling, zero_level], axis=0)
    lower = jnp.concatenate([zero_level, coupling], axis=0)
    diagonal = 1.0 + upper + lower
    ratio_list = []
    value_list = []
    prev_ratio = jnp.zeros_like(rate[0])
    prev_value = jnp.zeros_like(tendency[:, 0])
    for level_at in range(level_total):
        pivot = diagonal[level_at] + lower[level_at] * prev_ratio
        prev_ratio = -upper[level_at] / pivot
        prev_value = (tendency[:, level_at] + lower[level_at] * prev_value) / pivot
        ratio_list.append(prev_ratio)
        value_list.append(prev_value)
    following = prev_value
    solved = [following]
    for level_at in range(level_total - 2, -1, -1):
        following = value_list[level_at] - ratio_list[level_at] * following
        solved.append(following)
    return jnp.stack(solved[::-1], axis=1)


def baroclinic(state_padded, rate_padded, count_padded, forcing, first_row, lat_total):
    level_total = state_padded.shape[1]
    level_ids = jnp.arange(level_total, dtype=jnp.int32).astype(jnp.float32)[:, None, None]
    wet_padded = (level_ids < count_padded[None]).astype(jnp.float32)
    masked = state_padded * wet_padded[None]
    wet_mask = centre_of(wet_padded)
    tracers = masked[:2]
    u_padded = masked[2]
    v_padded = masked[3]
    u_middle = centre_of(u_padded)
    v_middle = centre_of(v_padded)
    carried = u_middle * (east_of(tracers) - west_of(tracers)) + v_middle * (
        north_of(tracers) - south_of(tracers)
    )
    tracer_next = (
        centre_of(tracers) + DIFFUSE * laplace(tracers, wet_padded) - 0.5 * ADVECTION * carried
    )
    density = HALINE * masked[1] - THERMAL * masked[0]
    pressure = GRAVITY * jnp.cumsum(density, axis=0) * wet_padded
    force_x = 0.5 * (east_of(pressure) - west_of(pressure))
    force_y = 0.5 * (north_of(pressure) - south_of(pressure))
    row_count = wet_mask.shape[-1]
    row_ids = (first_row + jnp.arange(row_count, dtype=jnp.int32)).astype(jnp.float32)
    rotation = CORIOLIS * (2.0 * (row_ids + 0.5) / lat_total - 1.0)
    u_next = u_middle + VISCOUS * laplace(u_padded, wet_padded) + rotation * v_middle - force_x
    v_next = v_middle + VISCOUS * laplace(v_padded, wet_padded) - rotation * u_middle - force_y
    updated = jnp.stack([tracer_next[0], tracer_next[1], u_next, v_next])
    gains = jnp.array(SURFACE_GAIN, dtype=jnp.float32)[:, None, None]
    surface = updated[:, 0] + gains * forcing
    updated = jnp.concatenate([surface[:, None], updated[:, 1:]], axis=1) * wet_mask[None]
    return vertical_mix(updated, centre_of(rate_padded), wet_mask) * wet_mask[None]


def edge_cells(values, margin):
    rows_done = with_halo(values, ((("lat", "comp"), 2),), margin, False)
    return with_halo(rows_done, (("lon", 1),), margin, True)


def remap_forcing(flux_block, weight_block, target_tile, slot_index, lon_dev):
    partial_value = jnp.einsum(
        "bfc,bco->bfo", flux_block, weight_block, preferred_element_type=jnp.float32
    )
    block_total, flux_total, lat_dev = partial_value.shape
    flat_part = partial_value.reshape(block_total, flux_total * lat_dev)
    column = target_tile * lon_dev + slot_index
    row_ids = jnp.arange(lon_dev * lax.axis_size("lon"), dtype=jnp.int32)
    select = (row_ids[:, None] == column[None, :]).astype(jnp.float32)
    local_sum = lax.psum_scatter(
        jnp.dot(select, flat_part, precision=lax.Precision.HIGHEST),
        "lon",
        scatter_dimension=0,
        tiled=True,
    )
    return jnp.transpose(local_sum.reshape(lon_dev, flux_total, lat_dev), (1, 0, 2))


def local(ocean_state, level_count, mix_rate, atmos_flux, remap_weight, remap_target, remap_slot):
    field_total, level_total, lon_dev, lat_dev = ocean_state.shape
    lat_total = lat_dev * lax.axis_size("lat") * lax.axis_size("comp")
    first_row = (lax.axis_index("lat") * lax.axis_size("comp") + lax.axis_index("comp")) * lat_dev
    forcing = remap_forcing(atmos_flux[0], remap_weight[0], remap_target[0], remap_slot[0], lon_dev)
    state_rows = field_total * level_total
    state_flat = ocean_state.reshape(state_rows, lon_dev, lat_dev)
    count_row = level_count.astype(jnp.float32)[None]
    state = ocean_state
    bundle = jnp.concatenate([state_flat, count_row], axis=0)
    padded = edge_cells(bundle, 1)
    count_padded = padded[state_rows]
    rate_padded = jnp.pad(mix_rate, ((0, 0), (1, 1), (1, 1)))
    for step_index in range(SUBSTEPS):
        if step_index > 0:
            fields_padded = edge_cells(state.reshape(state_rows, lon_dev, lat_dev), 1)
        else:
            fields_padded = padded[:state_rows]
        state_padded = fields_padded.reshape(field_total, level_total, lon_dev + 2, lat_dev + 2)
        state = baroclinic(state_padded, rate_padded, count_padded, forcing, first_row, lat_total)
    return state


def solution(mesh):
    placed = (
        P(None, None, "lon", ("lat", "comp")),
        P("lon", ("lat", "comp")),
        P(None, "lon", ("lat", "comp")),
        P(("lat", "comp"), "lon", None, None),
        P(("lat", "comp"), "lon", None, None),
        P(("lat", "comp"), "lon"),
        P(("lat", "comp"), "lon"),
    )
    return jax.shard_map(
        local,
        mesh=mesh,
        in_specs=placed,
        out_specs=P(None, None, "lon", ("lat", "comp")),
        check_vma=False,
    )
```

profile of v0, /device:TPU:0, one launch (start us, length us, event | category | flops | bytes accessed | tf_op | source)
XLA Modules:
  0.0 174.2 jit_solution(5556423072964168187)
XLA Ops:
  6.5 0.7 convert_bitcast_fusion
  7.3 2.3 %slice_maximum_fusion = (f32[321,8,1]{2,1,0:T(8,128)S(1)}, f32[321,8,1]{2,1,0:T(8,128)S(1)}) fusion(f32[1,8,128]{2,1,0:T(8,128)S(1)} %convert_bitcast_fusion, f32[320,8,128]{2,1,0:T(8,128)} %bitcast.4711), kind=kLoop, calls=%fused_computation.8 | loop fusion | flops 5136 | bytes 1335360 | tf_op jit(solution)/shard_map/concatenate | solution.py:153
  10.2 1.3 collective-permute-start.1
  12.0 3.0 %collective-permute-start = (f32[321,8,1]{0,1,2:T(8,128)S(1)}, f32[321,8,1]{0,1,2:T(8,128)S(1)}, u32[]{:S(2)}, u32[]{:S(2)}) collective-permute-start(f32[321,8,1]{0,1,2:T(8,128)S(1)} %copy.1036), channel_id=1, source_target_pairs={{0,1},{1,2},{2,3},{3,4},{4,5},{5,6},{6,7},{8,9},{9,10},{10,11},{11... | collective-permute-start | bytes 30824 | tf_op jit(solution)/shard_map/ppermute | solution.py:26
  15.3 0.8 fusion.411
  17.3 4.8 %pad_maximum_fusion.6 = (f32[321,1,130]{2,1,0:T(1,128)}, f32[321,1,130]{2,1,0:T(1,128)}) fusion(f32[321,8,1]{2,1,0:T(8,128)S(1)} %copy.1039, f32[321,8,1]{2,1,0:T(8,128)S(1)} %copy.1038, f32[1,8,128]{2,1,0:T(8,128)S(1)} %convert_bitcast_fusion, f32[320,8,128]{2,1,0:T(8,128)} %bitcast.4712), kind=kLoop, calls=%fused_computation.216 | loop fusion | flops 250380 | bytes 1669200 | tf_op jit(solution)/shard_map/slice | solution.py:27
  22.1 3.9 %collective-permute-start.3 = (f32[321,1,130]{2,1,0:T(1,128)}, f32[321,1,130]{2,1,0:T(1,128)S(1)}, u32[]{:S(2)}, u32[]{:S(2)}) collective-permute-start(f32[321,1,130]{2,1,0:T(1,128)} %get-tuple-element.321), channel_id=1, source_target_pairs={{8,0},{16,8},{24,16},{0,24},{9,1},{17,9},{25,17},{1,25},{10,2},{18... | collective-permute-start | bytes 500768 | tf_op jit(solution)/shard_map/ppermute | solution.py:29
  27.3 7.1 %collective-permute-done.3 = f32[321,1,130]{2,1,0:T(1,128)S(1)} collective-permute-done((f32[321,1,130]{2,1,0:T(1,128)}, f32[321,1,130]{2,1,0:T(1,128)S(1)}, u32[]{:S(2)}, u32[]{:S(2)}) %collective-permute-start.3) | collective-permute-done | bytes 166952 | tf_op jit(solution)/shard_map/ppermute | solution.py:29
  34.5 7.9 %collective-permute-done.2 = f32[321,1,130]{2,1,0:T(1,128)S(1)} collective-permute-done((f32[321,1,130]{2,1,0:T(1,128)}, f32[321,1,130]{2,1,0:T(1,128)S(1)}, u32[]{:S(2)}, u32[]{:S(2)}) %collective-permute-start.2) | collective-permute-done | bytes 166952 | tf_op jit(solution)/shard_map/ppermute | solution.py:26
  42.4 5.3 %pad_maximum_fusion = f32[321,10,130]{2,1,0:T(8,128)S(1)} fusion(f32[321,1,130]{2,1,0:T(1,128)S(1)} %collective-permute-done.3, f32[321,8,1]{2,1,0:T(8,128)S(1)} %copy.1039, f32[1,8,128]{2,1,0:T(8,128)} %copy-done.142, f32[320,8,128]{2,1,0:T(8,128)} %bitcast.4713, f32[321,8,1]{2,1,0:T(8,128)S(1)} %copy.1038, f32[321,1,130]{2,1,0:T(1,128)S(1)} %collective-permute-done.2), kind=kLoop, calls=%fused_computation | loop fusion | flops 2086500 | bytes 3338400 | tf_op jit(solution)/shard_map/concatenate | solution.py:30
  48.3 0.7 copy-done.2
  49.3 0.8 broadcast_multiply_fusion.1
  50.7 1.6 fusion.790
  52.2 1.8 %fusion.789 = (f32[80,8,128]{2,1,0:T(8,128)S(1)}, f32[1,80,8,128]{3,2,0,1:T(8,128)}, f32[80,8,128]{2,1,0:T(8,128)S(1)}, f32[80,8,128]{2,1,0:T(8,128)S(1)}, f32[8...) fusion(f32[80,10,130]{2,1,0:T(8,128)S(1)} %compare_convert_fusion, ...), kind=kLoop, calls=%fused_computation.1538 | loop fusion | flops 1474560 | bytes 6554112 | tf_op jit(solution)/shard_map/slice | solution.py:35
  54.0 0.8 fusion.786
  55.5 0.7 slice_bitcast_fusion.71
  56.8 0.6 slice_bitcast_fusion.120
  58.4 0.7 slice_bitcast_fusion.67
  88.4 0.6 fusion.421
  89.1 0.6 fusion.429
  89.7 0.6 fusion.418
  91.5 0.9 fusion.83
  93.4 1.1 fusion.369
  94.9 1.9 %constant_dynamic-update-slice_fusion.79 = (f32[4,80,8,128]{3,2,1,0:T(8,128)S(1)}, f32[4,8,128]{2,1,0:T(8,128)S(1)}, f32[4,8,128]{2,1,0:T(8,128)S(1)}, f32[4,8,1...) fusion(f32[8,128]{1,0:T(8,128)S(1)} %get-tuple-element.461, ...), kind=kLoop, calls=%fused_computation.132 | loop fusion | flops 1437695 | bytes 2899968
  96.9 0.7 constant_dynamic-update-slice_fusion.78
  97.6 0.7 constant_dynamic-update-slice_fusion.76
  98.3 0.7 constant_dynamic-update-slice_fusion.74
  99.0 0.7 constant_dynamic-update-slice_fusion.72
  99.7 0.7 constant_dynamic-update-slice_fusion.70
  100.4 0.7 constant_dynamic-update-slice_fusion.68
  101.0 0.7 constant_dynamic-update-slice_fusion.66
  101.7 0.7 constant_dynamic-update-slice_fusion.64
  102.6 2.4 %constant_dynamic-update-slice_fusion.62 = (f32[4,80,8,128]{3,2,1,0:T(8,128)S(1)}, f32[4,1,8,128]{3,2,0,1:T(8,128)S(1)}, f32[4,1,8,128]{3,2,0,1:T(8,128)S(1)}, f...) fusion(f32[4,80,8,128]{3,2,1,0:T(8,128)S(1)} %constant_dynamic-, ...), kind=kLoop, calls=%fused_computation.115 | loop fusion | flops 1482752 | bytes 2641920
  105.9 1.9 %fusion.788 = (f32[320,8,1]{2,1,0:T(8,128)}, f32[320,8,1]{2,1,0:T(8,128)}) fusion(f32[320,8,128]{2,1,0:T(8,128)S(1)} %bitcast.4715), kind=kLoop, calls=%fused_computation.1537 | loop fusion | bytes 40960 | tf_op jit(solution)/shard_map/slice | solution.py:27
  107.8 2.4 %copy.1385 = f32[320,8,1]{0,1,2:T(8,128)} copy(f32[320,8,1]{2,1,0:T(8,128)} %get-tuple-element.332) | data formatting | bytes 20480
  110.2 1.5 collective-permute-start.5
  111.7 2.4 %copy.1384 = f32[320,8,1]{0,1,2:T(8,128)} copy(f32[320,8,1]{2,1,0:T(8,128)} %get-tuple-element.331) | data formatting | bytes 20480
  114.1 3.6 %collective-permute-start.4 = (f32[320,8,1]{0,1,2:T(8,128)}, f32[320,8,1]{0,1,2:T(8,128)}, u32[]{:S(2)}, u32[]{:S(2)}) collective-permute-start(f32[320,8,1]{0,1,2:T(8,128)} %copy.1384), channel_id=1, source_target_pairs={{0,1},{1,2},{2,3},{3,4},{4,5},{5,6},{6,7},{8,9},{9,10},{10,11},{11... | collective-permute-start | bytes 30728 | tf_op jit(solution)/shard_map/ppermute | solution.py:26
  117.7 1.7 copy.1130
  119.5 0.8 copy.1131
  120.3 0.7 copy.1129
  121.0 1.1 pad_maximum_fusion.9
  122.1 1.5 collective-permute-start.7
  124.2 5.9 %collective-permute-done.7 = f32[320,1,130]{0,2,1:T(8,128)S(1)} collective-permute-done((f32[320,1,130]{0,2,1:T(8,128)S(1)}, f32[320,1,130]{0,2,1:T(8,128)S(1)}, u32[]{:S(2)}, u32[]{:S(2)}) %collective-permute-start.7) | collective-permute-done | bytes 166432 | tf_op jit(solution)/shard_map/ppermute | solution.py:29
  130.1 3.4 %collective-permute-done.6 = f32[320,1,130]{0,2,1:T(8,128)S(1)} collective-permute-done((f32[320,1,130]{0,2,1:T(8,128)S(1)}, f32[320,1,130]{0,2,1:T(8,128)S(1)}, u32[]{:S(2)}, u32[]{:S(2)}) %collective-permute-start.6) | collective-permute-done | bytes 166432 | tf_op jit(solution)/shard_map/ppermute | solution.py:26
  133.5 1.5 pad_maximum_fusion.1
  135.0 6.7 %copy.1132 = f32[320,10,130]{2,1,0:T(8,128)} copy(f32[320,10,130]{0,2,1:T(8,128)} %pad_maximum_fusion.1) | data formatting | bytes 3328000 | tf_op jit(solution)/shard_map/concatenate | solution.py:30
  141.7 3.3 %broadcast_multiply_fusion = f32[4,80,10,130]{3,2,1,0:T(8,128)S(1)} fusion(f32[4,80,10,130]{3,2,1,0:T(8,128)} %bitcast.4710, f32[80,10,130]{2,1,0:T(8,128)S(1)} %compare_convert_fusion), kind=kLoop, calls=%fused_computation.1 | loop fusion | flops 416000 | bytes 3744000 | tf_op jit(solution)/shard_map/mul | solution.py:92
  146.0 0.9 fusion.29
  146.8 0.9 fusion.787
  147.8 0.7 fusion.785
  150.0 0.8 fusion.81
  151.9 1.1 fusion.156
  153.3 2.0 %constant_dynamic-update-slice_fusion.159 = (f32[4,80,8,128]{3,2,1,0:T(8,128)S(1)}, f32[4,8,128]{2,1,0:T(8,128)S(1)}, f32[4,8,128]{2,1,0:T(8,128)S(1)}, f32[4,8,...) fusion(f32[8,128]{1,0:T(8,128)} %copy-done.148, ...), kind=kLoop, calls=%fused_computation.212 | loop fusion | flops 1437695 | bytes 2899968
  155.4 0.7 constant_dynamic-update-slice_fusion.158
  156.1 0.7 constant_dynamic-update-slice_fusion.156
  156.8 0.7 constant_dynamic-update-slice_fusion.154
  157.4 0.7 constant_dynamic-update-slice_fusion.152
  158.1 0.7 constant_dynamic-update-slice_fusion.150
  158.8 0.7 constant_dynamic-update-slice_fusion.148
  159.5 0.7 constant_dynamic-update-slice_fusion.146
  160.2 0.7 constant_dynamic-update-slice_fusion.144
  161.0 4.4 %constant_dynamic-update-slice_fusion.142 = (f32[4,80,8,128]{3,2,1,0:T(8,128)S(1)}, f32[4,1,8,128]{3,2,0,1:T(8,128)S(1)}, f32[4,1,8,128]{3,2,0,1:T(8,128)S(1)}, ...) fusion(f32[4,80,8,128]{3,2,1,0:T(8,128)S(1)} %constant_dynamic-, ...), kind=kLoop, calls=%fused_computation.195 | loop fusion | flops 1482752 | bytes 2641920
  166.2 1.2 broadcast_multiply_fusion.3
  (550 shorter events, 42.6 us)
Async XLA Ops:
  6.5 8.5 %copy-start = (bf16[1,4,256,128]{3,2,1,0:T(8,128)(2,1)S(1)}, bf16[1,4,256,128]{3,2,1,0:T(8,128)(2,1)}, u32[]{:S(2)}) copy-start(bf16[1,4,256,128]{3,2,1,0:T(8,128)(2,1)} %param.13) | copy-start | bytes 786436
  6.5 85.0 %all-reduce.5.cloned.1.call-start = ((), (), s32[]{:S(2)}) async-start(), calls=%async_computation | async-start | bytes 131072
  7.3 10.0 %copy-start.142 = (f32[1,8,128]{2,1,0:T(8,128)}, f32[1,8,128]{2,1,0:T(8,128)S(1)}, u32[]{:S(2)}) copy-start(f32[1,8,128]{2,1,0:T(8,128)S(1)} %convert_bitcast_fusion) | copy-start | bytes 12292
  9.6 5.5 %copy-start.152 = (bf16[1,4,4,256]{3,2,1,0:T(4,128)(2,1)S(1)}, bf16[1,4,4,256]{3,2,1,0:T(4,128)(2,1)}, u32[]{:S(2)}) copy-start(bf16[1,4,4,256]{3,2,1,0:T(4,128)(2,1)} %param.12) | copy-start | bytes 24580
  9.6 5.6 %copy-start.159 = (s32[1,4]{1,0:T(1,128)S(1)}, s32[1,4]{1,0:T(1,128)}, u32[]{:S(2)}) copy-start(s32[1,4]{1,0:T(1,128)} %param.15) | copy-start | bytes 52
  9.6 5.6 %copy-start.160 = (s32[1,4]{1,0:T(1,128)S(1)}, s32[1,4]{1,0:T(1,128)}, u32[]{:S(2)}) copy-start(s32[1,4]{1,0:T(1,128)} %param.14) | copy-start | bytes 52
  10.2 5.9 %collective-permute-start.1 = (f32[321,8,1]{0,1,2:T(8,128)S(1)}, f32[321,8,1]{0,1,2:T(8,128)S(1)}, u32[]{:S(2)}, u32[]{:S(2)}) collective-permute-start(f32[321,8,1]{0,1,2:T(8,128)S(1)} %copy.1037), channel_id=1, source_target_pairs={{1,0},{2,1},{3,2},{4,3},{5,4},{6,5},{7,6},{9,8},{10,9},{11,10},{12... | collective-permute-start | bytes 30824 | tf_op jit(solution)/shard_map/ppermute | solution.py:29
  12.0 4.6 %collective-permute-start = (f32[321,8,1]{0,1,2:T(8,128)S(1)}, f32[321,8,1]{0,1,2:T(8,128)S(1)}, u32[]{:S(2)}, u32[]{:S(2)}) collective-permute-start(f32[321,8,1]{0,1,2:T(8,128)S(1)} %copy.1036), channel_id=1, source_target_pairs={{0,1},{1,2},{2,3},{3,4},{4,5},{5,6},{6,7},{8,9},{9,10},{10,11},{11... | collective-permute-start | bytes 30824 | tf_op jit(solution)/shard_map/ppermute | solution.py:26
  17.3 8.8 %copy-start.161 = (u32[32]{0:T(128)S(1)}, u32[32]{0:T(128)}, u32[]{:S(2)}) copy-start(u32[32]{0:T(128)} %constant.61) | copy-start | bytes 388
  22.1 12.3 %collective-permute-start.3 = (f32[321,1,130]{2,1,0:T(1,128)}, f32[321,1,130]{2,1,0:T(1,128)S(1)}, u32[]{:S(2)}, u32[]{:S(2)}) collective-permute-start(f32[321,1,130]{2,1,0:T(1,128)} %get-tuple-element.321), channel_id=1, source_target_pairs={{8,0},{16,8},{24,16},{0,24},{9,1},{17,9},{25,17},{1,25},{10,2},{18... | collective-permute-start | bytes 500768 | tf_op jit(solution)/shard_map/ppermute | solution.py:29
  26.1 16.3 %collective-permute-start.2 = (f32[321,1,130]{2,1,0:T(1,128)}, f32[321,1,130]{2,1,0:T(1,128)S(1)}, u32[]{:S(2)}, u32[]{:S(2)}) collective-permute-start(f32[321,1,130]{2,1,0:T(1,128)} %get-tuple-element.320), channel_id=1, source_target_pairs={{0,8},{8,16},{16,24},{24,0},{1,9},{9,17},{17,25},{25,1},{2,10},{10... | collective-permute-start | bytes 500768 | tf_op jit(solution)/shard_map/ppermute | solution.py:26
  26.1 24.0 %copy-start.155 = (f32[80]{0:T(128)}, f32[80]{0:T(128)S(1)}, u32[]{:S(2)}) copy-start(f32[80]{0:T(128)S(1)} %iota_convert_fusion) | copy-start | bytes 964
  27.3 24.9 %copy-start.153 = (f32[128]{0:T(128)}, f32[128]{0:T(128)S(1)}, u32[]{:S(2)}) copy-start(f32[128]{0:T(128)S(1)} %add_multiply_fusion) | copy-start | bytes 1540
  54.0 36.3 %copy-start.4 = (f32[80,8,128]{2,1,0:T(8,128)}, f32[80,8,128]{2,1,0:T(8,128)S(1)}, u32[]{:S(2)}) copy-start(f32[80,8,128]{2,1,0:T(8,128)S(1)} %get-tuple-element.337) | copy-start | bytes 983044
  54.0 36.3 %copy-start.6 = (f32[80,8,128]{2,1,0:T(8,128)}, f32[80,8,128]{2,1,0:T(8,128)S(1)}, u32[]{:S(2)}) copy-start(f32[80,8,128]{2,1,0:T(8,128)S(1)} %get-tuple-element.338) | copy-start | bytes 983044
  54.0 36.3 %copy-start.8 = (f32[80,8,128]{2,1,0:T(8,128)}, f32[80,8,128]{2,1,0:T(8,128)S(1)}, u32[]{:S(2)}) copy-start(f32[80,8,128]{2,1,0:T(8,128)S(1)} %get-tuple-element.339) | copy-start | bytes 983044
  58.4 32.5 %copy-start.35 = (f32[8,128]{1,0:T(8,128)}, f32[8,128]{1,0:T(8,128)S(1)}, u32[]{:S(2)}) copy-start(f32[8,128]{1,0:T(8,128)S(1)} %get-tuple-element.238) | copy-start | bytes 12292
  59.7 23.9 %copy-start.38 = (f32[1,8,128]{2,1,0:T(8,128)}, f32[1,8,128]{2,1,0:T(8,128)S(1)}, u32[]{:S(2)}) copy-start(f32[1,8,128]{2,1,0:T(8,128)S(1)} %get-tuple-element.165) | copy-start | bytes 12292
  60.3 26.8 %copy-start.41 = (f32[1,8,128]{2,1,0:T(8,128)}, f32[1,8,128]{2,1,0:T(8,128)S(1)}, u32[]{:S(2)}) copy-start(f32[1,8,128]{2,1,0:T(8,128)S(1)} %get-tuple-element.168) | copy-start | bytes 12292
  61.0 17.1 %copy-start.44 = (f32[1,8,128]{2,1,0:T(8,128)}, f32[1,8,128]{2,1,0:T(8,128)S(1)}, u32[]{:S(2)}) copy-start(f32[1,8,128]{2,1,0:T(8,128)S(1)} %get-tuple-element.171) | copy-start | bytes 12292
  61.6 24.4 %copy-start.47 = (f32[1,8,128]{2,1,0:T(8,128)}, f32[1,8,128]{2,1,0:T(8,128)S(1)}, u32[]{:S(2)}) copy-start(f32[1,8,128]{2,1,0:T(8,128)S(1)} %get-tuple-element.174) | copy-start | bytes 12292
  62.2 23.2 %copy-start.50 = (f32[1,8,128]{2,1,0:T(8,128)}, f32[1,8,128]{2,1,0:T(8,128)S(1)}, u32[]{:S(2)}) copy-start(f32[1,8,128]{2,1,0:T(8,128)S(1)} %get-tuple-element.177) | copy-start | bytes 12292
  62.8 28.0 %copy-start.53 = (f32[1,8,128]{2,1,0:T(8,128)}, f32[1,8,128]{2,1,0:T(8,128)S(1)}, u32[]{:S(2)}) copy-start(f32[1,8,128]{2,1,0:T(8,128)S(1)} %get-tuple-element.180) | copy-start | bytes 12292
  63.4 27.4 %copy-start.59 = (f32[1,8,128]{2,1,0:T(8,128)}, f32[1,8,128]{2,1,0:T(8,128)S(1)}, u32[]{:S(2)}) copy-start(f32[1,8,128]{2,1,0:T(8,128)S(1)} %get-tuple-element.183) | copy-start | bytes 12292
  77.4 12.9 %copy-start.77 = (f32[1,8,128]{2,1,0:T(8,128)}, f32[1,8,128]{2,1,0:T(8,128)S(1)}, u32[]{:S(2)}) copy-start(f32[1,8,128]{2,1,0:T(8,128)S(1)} %get-tuple-element.230) | copy-start | bytes 12292
  84.2 21.4 %copy-start.13 = (f32[8,128]{1,0:T(8,128)}, f32[8,128]{1,0:T(8,128)S(1)}, u32[]{:S(2)}) copy-start(f32[8,128]{1,0:T(8,128)S(1)} %get-tuple-element.267) | copy-start | bytes 12292
  93.2 12.1 %copy-start.80 = (f32[8,128]{1,0:T(8,128)}, f32[8,128]{1,0:T(8,128)S(1)}, u32[]{:S(2)}) copy-start(f32[8,128]{1,0:T(8,128)S(1)} %get-tuple-element.235) | copy-start | bytes 12292
  93.3 9.2 %copy-start.138 = (f32[8,128]{1,0:T(8,128)}, f32[8,128]{1,0:T(8,128)S(1)}, u32[]{:S(2)}) copy-start(f32[8,128]{1,0:T(8,128)S(1)} %get-tuple-element.458) | copy-start | bytes 12292
  93.3 9.2 %copy-start.139 = (f32[8,128]{1,0:T(8,128)}, f32[8,128]{1,0:T(8,128)S(1)}, u32[]{:S(2)}) copy-start(f32[8,128]{1,0:T(8,128)S(1)} %get-tuple-element.459) | copy-start | bytes 12292
  93.3 9.2 %copy-start.140 = (f32[8,128]{1,0:T(8,128)}, f32[8,128]{1,0:T(8,128)S(1)}, u32[]{:S(2)}) copy-start(f32[8,128]{1,0:T(8,128)S(1)} %get-tuple-element.462) | copy-start | bytes 12292
  93.3 9.2 %copy-start.141 = (f32[8,128]{1,0:T(8,128)}, f32[8,128]{1,0:T(8,128)S(1)}, u32[]{:S(2)}) copy-start(f32[8,128]{1,0:T(8,128)S(1)} %get-tuple-element.463) | copy-start | bytes 12292
  94.8 7.7 %copy-start.112 = (f32[8,128]{1,0:T(8,128)S(1)}, f32[8,128]{1,0:T(8,128)}, u32[]{:S(2)}) copy-start(f32[8,128]{1,0:T(8,128)} %get-tuple-element.207) | copy-start | bytes 12292
  94.8 7.7 %copy-start.114 = (f32[8,128]{1,0:T(8,128)S(1)}, f32[8,128]{1,0:T(8,128)}, u32[]{:S(2)}) copy-start(f32[8,128]{1,0:T(8,128)} %get-tuple-element.211) | copy-start | bytes 12292
  94.8 7.7 %copy-start.116 = (f32[8,128]{1,0:T(8,128)S(1)}, f32[8,128]{1,0:T(8,128)}, u32[]{:S(2)}) copy-start(f32[8,128]{1,0:T(8,128)} %get-tuple-element.215) | copy-start | bytes 12292
  94.8 7.7 %copy-start.118 = (f32[8,128]{1,0:T(8,128)S(1)}, f32[8,128]{1,0:T(8,128)}, u32[]{:S(2)}) copy-start(f32[8,128]{1,0:T(8,128)} %get-tuple-element.219) | copy-start | bytes 12292
  94.8 7.7 %copy-start.120 = (f32[8,128]{1,0:T(8,128)S(1)}, f32[8,128]{1,0:T(8,128)}, u32[]{:S(2)}) copy-start(f32[8,128]{1,0:T(8,128)} %get-tuple-element.223) | copy-start | bytes 12292
  94.8 7.7 %copy-start.122 = (f32[8,128]{1,0:T(8,128)S(1)}, f32[8,128]{1,0:T(8,128)}, u32[]{:S(2)}) copy-start(f32[8,128]{1,0:T(8,128)} %get-tuple-element.227) | copy-start | bytes 12292
  94.8 7.7 %copy-start.124 = (f32[8,128]{1,0:T(8,128)S(1)}, f32[8,128]{1,0:T(8,128)}, u32[]{:S(2)}) copy-start(f32[8,128]{1,0:T(8,128)} %get-tuple-element.231) | copy-start | bytes 12292
  94.8 7.7 %copy-start.126 = (f32[8,128]{1,0:T(8,128)S(1)}, f32[8,128]{1,0:T(8,128)}, u32[]{:S(2)}) copy-start(f32[8,128]{1,0:T(8,128)} %get-tuple-element.233) | copy-start | bytes 12292
  94.9 7.7 %copy-start.128 = (f32[8,128]{1,0:T(8,128)S(1)}, f32[8,128]{1,0:T(8,128)}, u32[]{:S(2)}) copy-start(f32[8,128]{1,0:T(8,128)} %get-tuple-element.385) | copy-start | bytes 12292
  94.9 7.7 %copy-start.130 = (f32[8,128]{1,0:T(8,128)S(1)}, f32[8,128]{1,0:T(8,128)}, u32[]{:S(2)}) copy-start(f32[8,128]{1,0:T(8,128)} %get-tuple-element.386) | copy-start | bytes 12292
  94.9 7.7 %copy-start.132 = (f32[8,128]{1,0:T(8,128)S(1)}, f32[8,128]{1,0:T(8,128)}, u32[]{:S(2)}) copy-start(f32[8,128]{1,0:T(8,128)} %get-tuple-element.387) | copy-start | bytes 12292
  94.9 7.7 %copy-start.134 = (f32[8,128]{1,0:T(8,128)S(1)}, f32[8,128]{1,0:T(8,128)}, u32[]{:S(2)}) copy-start(f32[8,128]{1,0:T(8,128)} %get-tuple-element.388) | copy-start | bytes 12292
  94.9 7.7 %copy-start.136 = (f32[8,128]{1,0:T(8,128)S(1)}, f32[8,128]{1,0:T(8,128)}, u32[]{:S(2)}) copy-start(f32[8,128]{1,0:T(8,128)} %get-tuple-element.389) | copy-start | bytes 12292
  94.9 7.7 %copy-start.137 = (f32[8,128]{1,0:T(8,128)S(1)}, f32[8,128]{1,0:T(8,128)}, u32[]{:S(2)}) copy-start(f32[8,128]{1,0:T(8,128)} %get-tuple-element.390) | copy-start | bytes 12292
  110.2 9.2 %collective-permute-start.5 = (f32[320,8,1]{0,1,2:T(8,128)}, f32[320,8,1]{0,1,2:T(8,128)}, u32[]{:S(2)}, u32[]{:S(2)}) collective-permute-start(f32[320,8,1]{0,1,2:T(8,128)} %copy.1385), channel_id=1, source_target_pairs={{1,0},{2,1},{3,2},{4,3},{5,4},{6,5},{7,6},{9,8},{10,9},{11,10},{12... | collective-permute-start | bytes 30728 | tf_op jit(solution)/shard_map/ppermute | solution.py:29
  114.1 6.2 %collective-permute-start.4 = (f32[320,8,1]{0,1,2:T(8,128)}, f32[320,8,1]{0,1,2:T(8,128)}, u32[]{:S(2)}, u32[]{:S(2)}) collective-permute-start(f32[320,8,1]{0,1,2:T(8,128)} %copy.1384), channel_id=1, source_target_pairs={{0,1},{1,2},{2,3},{3,4},{4,5},{5,6},{6,7},{8,9},{9,10},{10,11},{11... | collective-permute-start | bytes 30728 | tf_op jit(solution)/shard_map/ppermute | solution.py:26
  119.4 14.1 %copy-start.3 = (f32[320,8,128]{0,2,1:T(8,128)S(1)}, f32[320,8,128]{0,2,1:T(8,128)}, u32[]{:S(2)}) copy-start(f32[320,8,128]{0,2,1:T(8,128)} %copy.1130) | copy-start | bytes 3932164
  122.1 8.0 %collective-permute-start.7 = (f32[320,1,130]{0,2,1:T(8,128)S(1)}, f32[320,1,130]{0,2,1:T(8,128)S(1)}, u32[]{:S(2)}, u32[]{:S(2)}) collective-permute-start(f32[320,1,130]{0,2,1:T(8,128)S(1)} %get-tuple-element.323), channel_id=1, source_target_pairs={{8,0},{16,8},{24,16},{0,24},{9,1},{17,9},{25,17},{1,25},{10,2},{18... | collective-permute-start | bytes 499208 | tf_op jit(solution)/shard_map/ppermute | solution.py:29
  123.6 9.9 %collective-permute-start.6 = (f32[320,1,130]{0,2,1:T(8,128)S(1)}, f32[320,1,130]{0,2,1:T(8,128)S(1)}, u32[]{:S(2)}, u32[]{:S(2)}) collective-permute-start(f32[320,1,130]{0,2,1:T(8,128)S(1)} %get-tuple-element.322), channel_id=1, source_target_pairs={{0,8},{8,16},{16,24},{24,0},{1,9},{9,17},{17,25},{25,1},{2,10},{10... | collective-permute-start | bytes 499208 | tf_op jit(solution)/shard_map/ppermute | solution.py:26
  153.2 7.7 %copy-start.109 = (f32[8,128]{1,0:T(8,128)S(1)}, f32[8,128]{1,0:T(8,128)}, u32[]{:S(2)}) copy-start(f32[8,128]{1,0:T(8,128)} %get-tuple-element.199) | copy-start | bytes 12292
  153.2 7.7 %copy-start.111 = (f32[8,128]{1,0:T(8,128)S(1)}, f32[8,128]{1,0:T(8,128)}, u32[]{:S(2)}) copy-start(f32[8,128]{1,0:T(8,128)} %get-tuple-element.203) | copy-start | bytes 12292
  153.2 7.7 %copy-start.113 = (f32[8,128]{1,0:T(8,128)S(1)}, f32[8,128]{1,0:T(8,128)}, u32[]{:S(2)}) copy-start(f32[8,128]{1,0:T(8,128)} %get-tuple-element.207) | copy-start | bytes 12292
  153.2 7.7 %copy-start.115 = (f32[8,128]{1,0:T(8,128)S(1)}, f32[8,128]{1,0:T(8,128)}, u32[]{:S(2)}) copy-start(f32[8,128]{1,0:T(8,128)} %get-tuple-element.211) | copy-start | bytes 12292
  153.2 7.7 %copy-start.117 = (f32[8,128]{1,0:T(8,128)S(1)}, f32[8,128]{1,0:T(8,128)}, u32[]{:S(2)}) copy-start(f32[8,128]{1,0:T(8,128)} %get-tuple-element.215) | copy-start | bytes 12292
  153.3 7.7 %copy-start.119 = (f32[8,128]{1,0:T(8,128)S(1)}, f32[8,128]{1,0:T(8,128)}, u32[]{:S(2)}) copy-start(f32[8,128]{1,0:T(8,128)} %get-tuple-element.219) | copy-start | bytes 12292
  153.3 7.7 %copy-start.121 = (f32[8,128]{1,0:T(8,128)S(1)}, f32[8,128]{1,0:T(8,128)}, u32[]{:S(2)}) copy-start(f32[8,128]{1,0:T(8,128)} %get-tuple-element.223) | copy-start | bytes 12292
  153.3 7.7 %copy-start.123 = (f32[8,128]{1,0:T(8,128)S(1)}, f32[8,128]{1,0:T(8,128)}, u32[]{:S(2)}) copy-start(f32[8,128]{1,0:T(8,128)} %get-tuple-element.227) | copy-start | bytes 12292
  153.3 7.7 %copy-start.125 = (f32[8,128]{1,0:T(8,128)S(1)}, f32[8,128]{1,0:T(8,128)}, u32[]{:S(2)}) copy-start(f32[8,128]{1,0:T(8,128)} %get-tuple-element.231) | copy-start | bytes 12292
  153.3 7.7 %copy-start.127 = (f32[8,128]{1,0:T(8,128)S(1)}, f32[8,128]{1,0:T(8,128)}, u32[]{:S(2)}) copy-start(f32[8,128]{1,0:T(8,128)} %get-tuple-element.233) | copy-start | bytes 12292
  153.3 7.7 %copy-start.129 = (f32[8,128]{1,0:T(8,128)S(1)}, f32[8,128]{1,0:T(8,128)}, u32[]{:S(2)}) copy-start(f32[8,128]{1,0:T(8,128)} %get-tuple-element.385) | copy-start | bytes 12292
  153.3 7.7 %copy-start.131 = (f32[8,128]{1,0:T(8,128)S(1)}, f32[8,128]{1,0:T(8,128)}, u32[]{:S(2)}) copy-start(f32[8,128]{1,0:T(8,128)} %get-tuple-element.386) | copy-start | bytes 12292
  153.3 7.7 %copy-start.133 = (f32[8,128]{1,0:T(8,128)S(1)}, f32[8,128]{1,0:T(8,128)}, u32[]{:S(2)}) copy-start(f32[8,128]{1,0:T(8,128)} %get-tuple-element.387) | copy-start | bytes 12292
  153.3 7.7 %copy-start.135 = (f32[8,128]{1,0:T(8,128)S(1)}, f32[8,128]{1,0:T(8,128)}, u32[]{:S(2)}) copy-start(f32[8,128]{1,0:T(8,128)} %get-tuple-element.388) | copy-start | bytes 12292
  (107 other events, 148.7 us)
Sparse Core Ops, SparseCore 0:
  16.2 44.6 all-reduce.4
where the time goes:
time: 176 us; the launch traced here: 174 us
  other arithmetic  87.5 us (50%)
  local copies, waits for them, and re-layouts  28.7 us (16%)
  waiting for transfers between devices  24.4 us (14%)
  between operations  17.2 us (10%)
  starting transfers between devices  15.5 us (9%)
    unnamed x80, other arithmetic  22.1 us
    mul x34, other arithmetic, vertical_mix(): following = value_list[level_at] - ratio_list[level_at] * following  20.1 us
    ppermute x4, waiting for transfers between devices, with_halo(): lax.ppermute(lax.slice_in_dim(block, 0, width, axis=dim), axis, backward)  13 us
    div x19, other arithmetic, vertical_mix(): prev_ratio = -upper[level_at] / pivot  11.4 us
    ppermute x4, waiting for transfers between devices, with_halo(): lax.ppermute(lax.slice_in_dim(block, block.shape[dim] - width, None, axis...  11.4 us
    unnamed x405, local copies, waits for them, and re-layouts  9.32 us
    ppermute x4, starting transfers between devices, with_halo(): lax.ppermute(lax.slice_in_dim(block, 0, width, axis=dim), axis, backward)  8.2 us
    ppermute x4, starting transfers between devices, with_halo(): lax.ppermute(lax.slice_in_dim(block, block.shape[dim] - width, None, axis...  7.26 us
  transfers between devices with their start and end apart: 9, of which 4 were waited for; matrix products, arithmetic and copies ran while one was open for 35% of the time, Pallas kernels for 0%

commit v1 on v0

v1 whole, which is shorter than its diff:
```python
import jax
import jax.numpy as jnp
from jax import lax
from jax.experimental import pallas as pl
from jax.experimental.pallas import tpu as pltpu
from jax.sharding import PartitionSpec as P

SUBSTEPS = 2

DIFFUSE = 0.2
VISCOUS = 0.2
ADVECTION = 0.5
THERMAL = 0.2
HALINE = 0.15
GRAVITY = 0.05
CORIOLIS = 0.3
SURFACE_GAIN = (0.5, 0.4, 0.6, 0.6)

FIELDS = 4
SUB = 8
LANE = 128
PAIRS = LANE // 2
GROUP = PAIRS // FIELDS
EXTRA = 8
SLOT_ROW = 4
COUNT_ROW = 5
LAT_AXES = ("lat", "comp")

VMEM_SPEC = pl.BlockSpec(memory_space=pltpu.VMEM)
SMEM_SPEC = pl.BlockSpec(memory_space=pltpu.SMEM)


def sublane_ids():
    return lax.broadcasted_iota(jnp.int32, (SUB, LANE), 0)


def lane_ids():
    return lax.broadcasted_iota(jnp.int32, (SUB, LANE), 1)


def spread(row):
    return jnp.broadcast_to(row, (SUB, LANE))


def tile_at(ref, index):
    return ref[pl.ds(pl.multiple_of(index * SUB, SUB), SUB), :]


def put_tile(ref, index, value):
    ref[pl.ds(pl.multiple_of(index * SUB, SUB), SUB), :] = value


def row_at(ref, index):
    return spread(ref[pl.ds(index, 1), :])


def pack_kernel(levels, lon_total, x_ref, count_ref, flux_ref, weight_ref, target_ref, slot_ref,
                east_ref, west_ref, edge_ref, parts_ref):
    me = lax.axis_index("lon")
    sub = sublane_ids()
    pair = lane_ids() // 2
    count = count_ref[...]
    rows = FIELDS * levels

    for out_ref, column in ((east_ref, SUB - 1), (west_ref, 0)):
        depth = spread(count[column:column + 1, :])
        for field in range(FIELDS):
            for start in range(0, levels, SUB):
                row = field * levels + start
                value = x_ref[pl.ds(row * SUB + column, SUB, stride=SUB), :]
                out_ref[pl.ds(row, SUB), :] = jnp.where(start + sub < depth, value, 0.0)

    blocks = flux_ref.shape[0]
    for block in range(blocks):
        partial = jnp.dot(flux_ref[block], weight_ref[block], preferred_element_type=jnp.float32)
        slot = slot_ref[0, block].astype(jnp.float32)
        tile = jnp.concatenate([partial, jnp.full((SUB - FIELDS, LANE), slot, jnp.float32)], axis=0)
        shift = lax.rem(target_ref[0, block] - me + lon_total, lon_total)
        parts_ref[shift] = tile

    count_f = count.astype(jnp.float32)
    for out_ref, column, shift in ((east_ref, SUB - 1, 1), (west_ref, 0, lon_total - 1)):
        tile = parts_ref[shift]
        out_ref[pl.ds(rows, EXTRA), :] = jnp.where(
            sub == COUNT_ROW, spread(count_f[column:column + 1, :]), tile
        )

    def group_body(group, carry):
        packed = jnp.zeros((SUB, LANE), jnp.float32)
        for inner in range(GROUP):
            level = group * GROUP + inner
            wet = level < count
            for field in range(FIELDS):
                j = inner * FIELDS + field
                value = jnp.where(wet, tile_at(x_ref, field * levels + level), 0.0)
                packed = jnp.where(pair == j, pltpu.roll(value, 2 * j + 1, 1), packed)
        put_tile(edge_ref, group, packed)
        return carry

    lax.fori_loop(0, levels // GROUP, group_body, 0)
    put_tile(edge_ref, levels // GROUP, pltpu.roll(count_f, 1, 1))


def factor_kernel(levels, rate_ref, count_ref, gain_ref, down_ref, up_ref):
    count = count_ref[...]

    def level_body(level, carry):
        lower, prev = carry
        upper = jnp.where(level + 1 < count, rate_ref[level], 0.0)
        upper = jnp.where(level < levels - 1, upper, 0.0)
        pivot = 1.0 + upper + lower - lower * prev
        inverse = 1.0 / pivot
        ratio = upper * inverse
        gain_ref[level] = jnp.where(level < count, inverse, 0.0)
        down_ref[level] = lower * inverse
        up_ref[level] = ratio
        return upper, ratio

    zero = jnp.zeros((SUB, LANE), jnp.float32)
    lax.fori_loop(0, levels, level_body, (zero, zero), unroll=8)


def step_body(levels, first, final, x_ref, depth, depths, gain_ref, down_ref, up_ref,
              from_west, from_east, from_south, from_north, forcing, out_ref, east_ref, west_ref,
              edge_ref, merged_ref):
    sub = sublane_ids()
    lane = lane_ids()
    pair = lane // 2
    groups = levels // GROUP
    lat_dev = LANE
    first_row = (lax.axis_index("lat") * lax.axis_size("comp") + lax.axis_index("comp")) * lat_dev
    lat_total = lat_dev * lax.axis_size("lat") * lax.axis_size("comp")
    row_ids = (first_row + lane).astype(jnp.float32)
    rotation = CORIOLIS * (2.0 * (row_ids + 0.5) / lat_total - 1.0)
    depth_e, depth_w, depth_n, depth_s = depths
    even = lane % 2 == 0
    for group in range(groups):
        merged_ref[group] = jnp.where(even, tile_at(from_south, group), tile_at(from_north, group))

    thermal = THERMAL / HALINE
    push = 0.5 * GRAVITY * HALINE
    zero = jnp.zeros((SUB, LANE), jnp.float32)

    def forward_level(level, inner, halo, carry, surface):
        sum_e, sum_w, sum_n, sum_s, *prev = carry
        here, east, west, north, south = [], [], [], [], []
        for field in range(FIELDS):
            row = field * levels + level
            value = tile_at(x_ref, row)
            if first:
                value = jnp.where(level < depth, value, 0.0)
            j = inner * FIELDS + field
            side = pltpu.roll(halo, (LANE - 1 - 2 * j) % LANE, 1)
            here.append(value)
            east.append(jnp.where(sub == SUB - 1, row_at(from_east, row), pltpu.roll(value, SUB - 1, 0)))
            west.append(jnp.where(sub == 0, row_at(from_west, row), pltpu.roll(value, 1, 0)))
            north.append(pltpu.roll(jnp.where(lane == 0, side, value), LANE - 1, 1))
            south.append(pltpu.roll(jnp.where(lane == LANE - 1, side, value), 1, 1))
        wet_e, wet_w, wet_n, wet_s = level < depth_e, level < depth_w, level < depth_n, level < depth_s
        keep = 1.0 - (
            (jnp.where(wet_e, DIFFUSE, 0.0) + jnp.where(wet_w, DIFFUSE, 0.0))
            + (jnp.where(wet_n, DIFFUSE, 0.0) + jnp.where(wet_s, DIFFUSE, 0.0))
        )
        sum_e = sum_e + (east[1] - thermal * east[0])
        sum_w = sum_w + (west[1] - thermal * west[0])
        sum_n = sum_n + (north[1] - thermal * north[0])
        sum_s = sum_s + (south[1] - thermal * south[0])
        force_x = push * (jnp.where(wet_e, sum_e, 0.0) - jnp.where(wet_w, sum_w, 0.0))
        force_y = push * (jnp.where(wet_n, sum_n, 0.0) - jnp.where(wet_s, sum_s, 0.0))
        u, v = here[2], here[3]
        u_part = (0.5 * ADVECTION) * u
        v_part = (0.5 * ADVECTION) * v
        explicit = []
        for field in range(FIELDS):
            spread_sum = (east[field] + west[field]) + (north[field] + south[field])
            value = keep * here[field] + DIFFUSE * spread_sum
            if field < 2:
                value = value - (
                    u_part * (east[field] - west[field]) + v_part * (north[field] - south[field])
                )
            elif field == 2:
                value = value + (rotation * v - force_x)
            else:
                value = value - (rotation * u + force_y)
            if surface:
                value = value + SURFACE_GAIN[field] * forcing[field]
            explicit.append(value)
        gain = gain_ref[level]
        down = down_ref[level]
        done = []
        for field in range(FIELDS):
            value = explicit[field] * gain + down * prev[field]
            put_tile(out_ref, field * levels + level, value)
            done.append(value)
        return (sum_e, sum_w, sum_n, sum_s, *done)

    carry = (zero,) * 8
    halo = merged_ref[0]
    for inner in range(GROUP):
        carry = forward_level(inner, inner, halo, carry, inner == 0)

    def forward_group(group, carry):
        halo = merged_ref[group]
        for inner in range(GROUP):
            carry = forward_level(group * GROUP + inner, inner, halo, carry, False)
        return carry

    carry = lax.fori_loop(1, groups, forward_group, carry)

    def backward_group(step, following):
        group = groups - 1 - step
        packed = zero
        for inner in range(GROUP - 1, -1, -1):
            level = group * GROUP + inner
            ratio = up_ref[level]
            now = []
            for field in range(FIELDS):
                value = tile_at(out_ref, field * levels + level) + ratio * following[field]
                put_tile(out_ref, field * levels + level, value)
                now.append(value)
                if not final:
                    j = inner * FIELDS + field
                    packed = jnp.where(pair == j, pltpu.roll(value, 2 * j + 1, 1), packed)
            following = tuple(now)
        if not final:
            put_tile(edge_ref, group, packed)
        return following

    lax.fori_loop(0, groups, backward_group, (zero,) * FIELDS)
    if not final:
        rows = FIELDS * levels
        for out_col, column in ((east_ref, SUB - 1), (west_ref, 0)):
            for row in range(0, rows, SUB):
                out_col[pl.ds(row, SUB), :] = out_ref[pl.ds(row * SUB + column, SUB, stride=SUB), :]


def first_kernel(levels, lon_total, x_ref, count_ref, gain_ref, down_ref, up_ref, west_in, east_in,
                 south_in, north_in, parts_ref, *rest):
    others = rest[:lon_total - 3]
    out_ref, east_ref, west_ref, edge_ref, depth_ref, merged_ref = rest[lon_total - 3:]
    sub = sublane_ids()
    lane = lane_ids()
    rows = FIELDS * levels
    depth = count_ref[...]
    count_f = depth.astype(jnp.float32)
    extra_w = west_in[pl.ds(rows, EXTRA), :]
    extra_e = east_in[pl.ds(rows, EXTRA), :]
    groups = levels // GROUP
    side_s = tile_at(south_in, groups)
    side_n = tile_at(north_in, groups)
    depth_e = jnp.where(sub == SUB - 1, spread(extra_e[COUNT_ROW:COUNT_ROW + 1]), pltpu.roll(count_f, SUB - 1, 0))
    depth_w = jnp.where(sub == 0, spread(extra_w[COUNT_ROW:COUNT_ROW + 1]), pltpu.roll(count_f, 1, 0))
    depth_n = pltpu.roll(jnp.where(lane == 0, pltpu.roll(side_n, LANE - 1, 1), count_f), LANE - 1, 1)
    depth_s = pltpu.roll(jnp.where(lane == LANE - 1, pltpu.roll(side_s, LANE - 1, 1), count_f), 1, 1)
    depths = []
    for at, value in enumerate((depth_e, depth_w, depth_n, depth_s)):
        value = value.astype(jnp.int32)
        put_tile(depth_ref, at, value)
        depths.append(value)
    forcing = [jnp.zeros((SUB, LANE), jnp.float32)] * FIELDS
    for tile in [parts_ref[0], extra_w, extra_e] + [other[...] for other in others]:
        mine = sub == spread(tile[SLOT_ROW:SLOT_ROW + 1]).astype(jnp.int32)
        for field in range(FIELDS):
            forcing[field] = forcing[field] + jnp.where(mine, spread(tile[field:field + 1]), 0.0)
    step_body(levels, True, False, x_ref, depth, depths, gain_ref, down_ref, up_ref, west_in, east_in,
              south_in, north_in, forcing, out_ref, east_ref, west_ref, edge_ref, merged_ref)
    put_tile(edge_ref, groups, jnp.zeros((SUB, LANE), jnp.float32))


def second_kernel(levels, lon_total, x_ref, gain_ref, down_ref, up_ref, west_in, east_in, south_in, north_in,
                  depth_ref, extra_w_ref, extra_e_ref, parts_ref, *rest):
    others = rest[:lon_total - 3]
    out_ref, merged_ref = rest[lon_total - 3:]
    sub = sublane_ids()
    rows = FIELDS * levels
    extra_w = extra_w_ref[pl.ds(rows, EXTRA), :]
    extra_e = extra_e_ref[pl.ds(rows, EXTRA), :]
    depths = [tile_at(depth_ref, at) for at in range(4)]
    forcing = [jnp.zeros((SUB, LANE), jnp.float32)] * FIELDS
    for tile in [parts_ref[0], extra_w, extra_e] + [other[...] for other in others]:
        mine = sub == spread(tile[SLOT_ROW:SLOT_ROW + 1]).astype(jnp.int32)
        for field in range(FIELDS):
            forcing[field] = forcing[field] + jnp.where(mine, spread(tile[field:field + 1]), 0.0)
    step_body(levels, False, True, x_ref, None, depths, gain_ref, down_ref, up_ref, west_in, east_in,
              south_in, north_in, forcing, out_ref, None, None, None, merged_ref)


def call(kernel, outs, args, specs=None, scratch=()):
    return pl.pallas_call(
        kernel,
        out_shape=[jax.ShapeDtypeStruct(shape, dtype) for shape, dtype in outs],
        in_specs=specs or [VMEM_SPEC] * len(args),
        out_specs=[VMEM_SPEC] * len(outs),
        scratch_shapes=list(scratch),
    )(*args)


def shift_by(value, axis, amount, periodic):
    count = lax.axis_size(axis)
    if periodic:
        pairs = [(i, (i + amount) % count) for i in range(count)]
    else:
        pairs = [(i, i + amount) for i in range(count) if 0 <= i + amount < count]
    return lax.ppermute(value, axis, pairs)


def bind(kernel, *head):
    def bound(*refs):
        return kernel(*head, *refs)
    bound.__name__ = kernel.__name__
    return bound


def local(ocean_state, level_count, mix_rate, atmos_flux, remap_weight, remap_target, remap_slot):
    field_total, levels, lon_dev, lat_dev = ocean_state.shape
    lon_total = lax.axis_size("lon")
    rows = field_total * levels
    groups = levels // GROUP
    f32 = jnp.float32
    x = ocean_state.reshape(rows * lon_dev, lat_dev)
    message = ((rows + EXTRA, lat_dev), f32)
    edges = (((groups + 1) * SUB, lat_dev), f32)
    table = ((levels, lon_dev, lat_dev), f32)

    east, west, edge, parts = call(
        bind(pack_kernel, levels, lon_total),
        [message, message, edges, ((lon_total, SUB, lat_dev), f32)],
        (x, level_count, atmos_flux[0], remap_weight[0], remap_target, remap_slot),
        [VMEM_SPEC] * 4 + [SMEM_SPEC] * 2,
    )
    from_west = shift_by(east, "lon", 1, True)
    from_east = shift_by(west, "lon", -1, True)
    from_south = shift_by(edge, LAT_AXES, 1, False)
    from_north = shift_by(edge, LAT_AXES, -1, False)
    others = [shift_by(parts[s], "lon", s, True) for s in range(2, lon_total - 1)]
    gain, down, up = call(bind(factor_kernel, levels), [table] * 3, (mix_rate, level_count))
    scratch = [pltpu.VMEM((groups, SUB, LANE), f32)]
    next_message = ((rows, lat_dev), f32)
    state, east, west, edge, depths = call(
        bind(first_kernel, levels, lon_total),
        [((rows * lon_dev, lat_dev), f32), next_message, next_message, edges, ((4 * SUB, LANE), jnp.int32)],
        (x, level_count, gain, down, up, from_west, from_east, from_south, from_north, parts, *others),
        scratch=scratch,
    )
    second_west = shift_by(east, "lon", 1, True)
    second_east = shift_by(west, "lon", -1, True)
    second_south = shift_by(edge, LAT_AXES, 1, False)
    second_north = shift_by(edge, LAT_AXES, -1, False)
    (state,) = call(
        bind(second_kernel, levels, lon_total),
        [((rows * lon_dev, lat_dev), f32)],
        (state, gain, down, up, second_west, second_east, second_south, second_north, depths,
         from_west, from_east, parts, *others),
        scratch=scratch,
    )
    return state.reshape(ocean_state.shape)


def solution(mesh):
    placed = (
        P(None, None, "lon", LAT_AXES),
        P("lon", LAT_AXES),
        P(None, "lon", LAT_AXES),
        P(LAT_AXES, "lon", None, None),
        P(LAT_AXES, "lon", None, None),
        P(LAT_AXES, "lon"),
        P(LAT_AXES, "lon"),
    )
    return jax.shard_map(
        local,
        mesh=mesh,
        in_specs=placed,
        out_specs=P(None, None, "lon", LAT_AXES),
        check_vma=False,
    )
```

time: 176 us -> 49.8 us (0.28)
  other arithmetic: 87.5 us -> 0 us
  local copies, waits for them, and re-layouts: 28.7 us -> 2.01 us
  Pallas kernels: 0 us -> 23.6 us
  waiting for transfers between devices: 24.4 us -> 6.21 us
  between operations: 17.2 us -> 0.12 us
  starting transfers between devices: 15.5 us -> 17.5 us
    mul x43 -> x0, other arithmetic: 26.3 us -> none  [the longest x34 20.1 us: vertical_mix(): following = value_list[level_at] - ratio_list[level_at] * following]
    pallas_call x0 -> x4, Pallas kernels: none -> 23.6 us  [call(): pl.pallas_call(kernel, out_shape=[jax.ShapeDtypeStruct(shape, dtype) for...]
    unnamed x80 -> x0, other arithmetic: 22.1 us -> none
    ppermute x8 -> x9, waiting for transfers between devices: 24.4 us -> 6.21 us  [shift_by(): return lax.ppermute(value, axis, pairs)]
    div x21 -> x0, other arithmetic: 13.5 us -> none  [the longest x19 11.4 us: vertical_mix(): prev_ratio = -upper[level_at] / pivot]
    slice x5 -> x0, other arithmetic: 10.2 us -> none  [the longest x2 5.91 us: with_halo(): lax.slice_in_dim(block, block.shape[dim] - width, None, axis=dim)]
    concatenate x3 -> x0, other arithmetic: 9.11 us -> none  [the longest x2 6.8 us: with_halo(): block = jnp.concatenate([low, block, high], axis=dim)]
    unnamed x405 -> x18, local copies, waits for them, and re-layouts: 9.32 us -> 1.33 us
  transfers between devices with their start and end apart: 9 -> 9, of which waited for: 4 -> 3; matrix products, arithmetic and copies ran while one was open for 35% -> 1% of each run, Pallas kernels for 0% -> 5%
where the time goes in v1:
time: 49.8 us; the launch traced here: 49.5 us
  Pallas kernels  23.6 us (47%)
  starting transfers between devices  17.5 us (35%)
  waiting for transfers between devices  6.21 us (12%)
  local copies, waits for them, and re-layouts  2.01 us (4%)
    pallas_call x4, Pallas kernels, call(): pl.pallas_call(kernel, out_shape=[jax.ShapeDtypeStruct(shape, dtype) for...  23.6 us
    ppermute x9, starting transfers between devices, shift_by(): return lax.ppermute(value, axis, pairs)  17.5 us
    ppermute x9, waiting for transfers between devices, shift_by(): return lax.ppermute(value, axis, pairs)  6.21 us
    unnamed x18, local copies, waits for them, and re-layouts  1.33 us
  transfers between devices with their start and end apart: 9, of which 3 were waited for; matrix products, arithmetic and copies ran while one was open for 1% of the time, Pallas kernels for 5%

profile of v1, /device:TPU:0, one launch (start us, length us, event | category | flops | bytes accessed | tf_op | source)
XLA Modules:
  0.0 49.5 jit_solution(8665997950340169756)
XLA Ops:
  0.0 2.9 %shard_map.74 = (f32[328,128]{1,0:T(8,128)}, f32[328,128]{1,0:T(8,128)}, f32[48,128]{1,0:T(8,128)}, f32[4,8,128]{2,1,0:T(8,128)}) custom-call(f32[2560,128]{1,0:T(8,128)} %bitcast.6, s32[8,128]{1,0:T(8,128)} %refs_1_.5, bf16[4,4,256]{2,1,0:T(4,128)(2,1)} %bitcast.9, bf16[4,256,128]{2,1,0:T(8,128)(2,1)} %bitcast.8, s32[1,4]{1,0:T(1,128)} %refs_4_.1, ...), custom_call_target="tpu_custom_call" | custom-call | tf_op jit(solution)/shard_map/pallas_call | solution.py:289
  2.9 1.3 %collective-permute-start.3 = (f32[48,128]{1,0:T(8,128)}, f32[48,128]{1,0:T(8,128)S(1)}, u32[]{:S(2)}, u32[]{:S(2)}) collective-permute-start(f32[48,128]{1,0:T(8,128)} %get-tuple-element.22), channel_id=1, source_target_pairs={{1,0},{2,1},{3,2},{4,3},{5,4},{6,5},{7,6},{9,8},{10,9},{11,10},{12... | collective-permute-start | bytes 73736 | tf_op jit(solution)/shard_map/ppermute | solution.py:304
  4.2 3.0 %collective-permute-start.2 = (f32[48,128]{1,0:T(8,128)}, f32[48,128]{1,0:T(8,128)S(1)}, u32[]{:S(2)}, u32[]{:S(2)}) collective-permute-start(f32[48,128]{1,0:T(8,128)} %get-tuple-element.22), channel_id=1, source_target_pairs={{0,1},{1,2},{2,3},{3,4},{4,5},{5,6},{6,7},{8,9},{9,10},{10,11},{11... | collective-permute-start | bytes 73736 | tf_op jit(solution)/shard_map/ppermute | solution.py:304
  7.2 3.0 %collective-permute-start = (f32[328,128]{1,0:T(8,128)}, f32[328,128]{1,0:T(8,128)S(1)}, u32[]{:S(2)}, u32[]{:S(2)}) collective-permute-start(f32[328,128]{1,0:T(8,128)} %get-tuple-element.20), channel_id=1, source_target_pairs={{0,8},{8,16},{16,24},{24,0},{1,9},{9,17},{17,25},{25,1},{2,10},{10... | collective-permute-start | bytes 503816 | tf_op jit(solution)/shard_map/ppermute | solution.py:304
  10.2 1.0 %collective-permute-start.1 = (f32[328,128]{1,0:T(8,128)}, f32[328,128]{1,0:T(8,128)S(1)}, u32[]{:S(2)}, u32[]{:S(2)}) collective-permute-start(f32[328,128]{1,0:T(8,128)} %get-tuple-element.21), channel_id=1, source_target_pairs={{0,24},{8,0},{16,8},{24,16},{1,25},{9,1},{17,9},{25,17},{2,26},{10... | collective-permute-start | bytes 503816 | tf_op jit(solution)/shard_map/ppermute | solution.py:304
  11.2 0.7 %slice_bitcast_fusion = f32[8,128]{1,0:T(8,128)S(1)} fusion(f32[4,8,128]{2,1,0:T(8,128)} %get-tuple-element.23.refs_9_.refs_11_), kind=kLoop, calls=%fused_computation | loop fusion | bytes 8192 | tf_op jit(solution)/shard_map/squeeze | solution.py:335
  11.9 1.9 %collective-permute-start.4 = (f32[8,128]{1,0:T(8,128)S(1)}, f32[8,128]{1,0:T(8,128)S(1)}, u32[]{:S(2)}, u32[]{:S(2)}) collective-permute-start(f32[8,128]{1,0:T(8,128)S(1)} %slice_bitcast_fusion), channel_id=1, source_target_pairs={{0,16},{8,24},{16,0},{24,8},{1,17},{9,25},{17,1},{25,9},{2,18},{10... | collective-permute-start | bytes 12296 | tf_op jit(solution)/shard_map/ppermute | solution.py:304
  13.8 2.7 %shard_map.73 = (f32[80,8,128]{2,1,0:T(8,128)}, f32[80,8,128]{2,1,0:T(8,128)}, f32[80,8,128]{2,1,0:T(8,128)}) custom-call(f32[80,8,128]{2,1,0:T(8,128)} %refs_0_.1, s32[8,128]{1,0:T(8,128)} %refs_1_.5), custom_call_target="tpu_custom_call" | custom-call | tf_op jit(solution)/shard_map/pallas_call | solution.py:289
  16.6 0.0 collective-permute-done.4.refs_10_.refs_12_
  16.6 0.0 copy-start.8
  16.6 0.0 collective-permute-done.3.refs_8_
  16.6 0.0 copy-start.4
  16.6 0.0 collective-permute-done.2.refs_7_
  16.6 0.0 copy-start.5
  16.6 0.0 collective-permute-done.refs_5_.refs_9_
  16.6 0.0 copy-start
  16.6 3.8 %collective-permute-done.1.refs_6_.refs_10_ = f32[328,128]{1,0:T(8,128)S(1)} collective-permute-done((f32[328,128]{1,0:T(8,128)}, f32[328,128]{1,0:T(8,128)S(1)}, u32[]{:S(2)}, u32[]{:S(2)}) %collective-permute-start.1) | collective-permute-done | bytes 167968 | tf_op jit(solution)/shard_map/ppermute | solution.py:304
  20.4 0.0 copy-start.1
  20.4 0.0 copy-done.8
  20.4 0.0 copy-done.4
  20.4 0.0 copy-done.5
  20.4 0.0 copy-done
  20.4 0.6 %copy-done.1 = f32[328,128]{1,0:T(8,128)} copy-done((f32[328,128]{1,0:T(8,128)}, f32[328,128]{1,0:T(8,128)S(1)}, u32[]{:S(2)}) %copy-start.1) | copy-done | bytes 167960
  21.1 9.3 %shard_map.75 = (f32[2560,128]{1,0:T(8,128)}, f32[320,128]{1,0:T(8,128)}, f32[320,128]{1,0:T(8,128)}, f32[48,128]{1,0:T(8,128)}, s32[32,128]{1,0:T(8,128)}) custom-call(f32[2560,128]{1,0:T(8,128)} %bitcast.7, s32[8,128]{1,0:T(8,128)} %refs_1_.5, f32[80,8,128]{2,1,0:T(8,128)} %get-tuple-element.17.refs_2_.refs_1_, ...), custom_call_target="tpu_custom_call" | custom-call | tf_op jit(solution)/shard_map/pallas_call | solution.py:289
  30.4 1.5 %collective-permute-start.5 = (f32[320,128]{1,0:T(8,128)}, f32[320,128]{1,0:T(8,128)S(1)}, u32[]{:S(2)}, u32[]{:S(2)}) collective-permute-start(f32[320,128]{1,0:T(8,128)} %get-tuple-element.25), channel_id=1, source_target_pairs={{0,8},{8,16},{16,24},{24,0},{1,9},{9,17},{17,25},{25,1},{2,10},{10... | collective-permute-start | bytes 491528 | tf_op jit(solution)/shard_map/ppermute | solution.py:304
  31.9 1.4 %collective-permute-start.6 = (f32[320,128]{1,0:T(8,128)}, f32[320,128]{1,0:T(8,128)S(1)}, u32[]{:S(2)}, u32[]{:S(2)}) collective-permute-start(f32[320,128]{1,0:T(8,128)} %get-tuple-element.26), channel_id=1, source_target_pairs={{0,24},{8,0},{16,8},{24,16},{1,25},{9,1},{17,9},{25,17},{2,26},{10... | collective-permute-start | bytes 491528 | tf_op jit(solution)/shard_map/ppermute | solution.py:304
  33.3 1.3 %collective-permute-start.8 = (f32[48,128]{1,0:T(8,128)}, f32[48,128]{1,0:T(8,128)S(1)}, u32[]{:S(2)}, u32[]{:S(2)}) collective-permute-start(f32[48,128]{1,0:T(8,128)} %get-tuple-element.27), channel_id=1, source_target_pairs={{1,0},{2,1},{3,2},{4,3},{5,4},{6,5},{7,6},{9,8},{10,9},{11,10},{12... | collective-permute-start | bytes 73736 | tf_op jit(solution)/shard_map/ppermute | solution.py:304
  34.6 3.0 %collective-permute-start.7 = (f32[48,128]{1,0:T(8,128)}, f32[48,128]{1,0:T(8,128)S(1)}, u32[]{:S(2)}, u32[]{:S(2)}) collective-permute-start(f32[48,128]{1,0:T(8,128)} %get-tuple-element.27), channel_id=1, source_target_pairs={{0,1},{1,2},{2,3},{3,4},{4,5},{5,6},{6,7},{8,9},{9,10},{10,11},{11... | collective-permute-start | bytes 73736 | tf_op jit(solution)/shard_map/ppermute | solution.py:304
  37.6 0.0 collective-permute-done.8.refs_7_
  37.7 0.0 copy-start.6
  37.7 1.0 %collective-permute-done.7.refs_6_ = f32[48,128]{1,0:T(8,128)S(1)} collective-permute-done((f32[48,128]{1,0:T(8,128)}, f32[48,128]{1,0:T(8,128)S(1)}, u32[]{:S(2)}, u32[]{:S(2)}) %collective-permute-start.7) | collective-permute-done | bytes 24608 | tf_op jit(solution)/shard_map/ppermute | solution.py:304
  38.7 0.0 copy-start.7
  38.7 0.0 collective-permute-done.5.refs_4_
  38.7 0.0 copy-start.2
  38.7 1.4 %collective-permute-done.6.refs_5_ = f32[320,128]{1,0:T(8,128)S(1)} collective-permute-done((f32[320,128]{1,0:T(8,128)}, f32[320,128]{1,0:T(8,128)S(1)}, u32[]{:S(2)}, u32[]{:S(2)}) %collective-permute-start.6) | collective-permute-done | bytes 163872 | tf_op jit(solution)/shard_map/ppermute | solution.py:304
  40.1 0.0 copy-start.3
  40.1 0.0 copy-done.6
  40.1 0.0 copy-done.7
  40.1 0.0 copy-done.2
  40.1 0.6 %copy-done.3 = f32[320,128]{1,0:T(8,128)} copy-done((f32[320,128]{1,0:T(8,128)}, f32[320,128]{1,0:T(8,128)S(1)}, u32[]{:S(2)}) %copy-start.3) | copy-done | bytes 163864
  40.7 8.8 %shard_map.76 = f32[2560,128]{1,0:T(8,128)} custom-call(f32[2560,128]{1,0:T(8,128)} %get-tuple-element.24.refs_0_, f32[80,8,128]{2,1,0:T(8,128)} %get-tuple-element.17.refs_2_.refs_1_, f32[80,8,128]{2,1,0:T(8,128)} %get-tuple-element.18.refs_3_.refs_2_, f32[80,8,128]{2,1,0:T(8,128)} %get-tuple-element.19.refs_4_.refs_3_, f32[320,128]{1,0:T(8,128)} %copy-done.2, ...), custom_call_target="tpu_custom_call" | custom-call | tf_op jit(solution)/shard_map/pallas_call | solution.py:289
Async XLA Ops:
  2.9 13.7 %collective-permute-start.3 = (f32[48,128]{1,0:T(8,128)}, f32[48,128]{1,0:T(8,128)S(1)}, u32[]{:S(2)}, u32[]{:S(2)}) collective-permute-start(f32[48,128]{1,0:T(8,128)} %get-tuple-element.22), channel_id=1, source_target_pairs={{1,0},{2,1},{3,2},{4,3},{5,4},{6,5},{7,6},{9,8},{10,9},{11,10},{12... | collective-permute-start | bytes 73736 | tf_op jit(solution)/shard_map/ppermute | solution.py:304
  4.2 12.4 %collective-permute-start.2 = (f32[48,128]{1,0:T(8,128)}, f32[48,128]{1,0:T(8,128)S(1)}, u32[]{:S(2)}, u32[]{:S(2)}) collective-permute-start(f32[48,128]{1,0:T(8,128)} %get-tuple-element.22), channel_id=1, source_target_pairs={{0,1},{1,2},{2,3},{3,4},{4,5},{5,6},{6,7},{8,9},{9,10},{10,11},{11... | collective-permute-start | bytes 73736 | tf_op jit(solution)/shard_map/ppermute | solution.py:304
  7.2 9.4 %collective-permute-start = (f32[328,128]{1,0:T(8,128)}, f32[328,128]{1,0:T(8,128)S(1)}, u32[]{:S(2)}, u32[]{:S(2)}) collective-permute-start(f32[328,128]{1,0:T(8,128)} %get-tuple-element.20), channel_id=1, source_target_pairs={{0,8},{8,16},{16,24},{24,0},{1,9},{9,17},{17,25},{25,1},{2,10},{10... | collective-permute-start | bytes 503816 | tf_op jit(solution)/shard_map/ppermute | solution.py:304
  10.2 10.2 %collective-permute-start.1 = (f32[328,128]{1,0:T(8,128)}, f32[328,128]{1,0:T(8,128)S(1)}, u32[]{:S(2)}, u32[]{:S(2)}) collective-permute-start(f32[328,128]{1,0:T(8,128)} %get-tuple-element.21), channel_id=1, source_target_pairs={{0,24},{8,0},{16,8},{24,16},{1,25},{9,1},{17,9},{25,17},{2,26},{10... | collective-permute-start | bytes 503816 | tf_op jit(solution)/shard_map/ppermute | solution.py:304
  11.9 4.7 %collective-permute-start.4 = (f32[8,128]{1,0:T(8,128)S(1)}, f32[8,128]{1,0:T(8,128)S(1)}, u32[]{:S(2)}, u32[]{:S(2)}) collective-permute-start(f32[8,128]{1,0:T(8,128)S(1)} %slice_bitcast_fusion), channel_id=1, source_target_pairs={{0,16},{8,24},{16,0},{24,8},{1,17},{9,25},{17,1},{25,9},{2,18},{10... | collective-permute-start | bytes 12296 | tf_op jit(solution)/shard_map/ppermute | solution.py:304
  16.6 3.9 %copy-start.8 = (f32[8,128]{1,0:T(8,128)}, f32[8,128]{1,0:T(8,128)S(1)}, u32[]{:S(2)}) copy-start(f32[8,128]{1,0:T(8,128)S(1)} %collective-permute-done.4.refs_10_.refs_12_) | copy-start | bytes 12292
  16.6 3.9 %copy-start.4 = (f32[48,128]{1,0:T(8,128)}, f32[48,128]{1,0:T(8,128)S(1)}, u32[]{:S(2)}) copy-start(f32[48,128]{1,0:T(8,128)S(1)} %collective-permute-done.3.refs_8_) | copy-start | bytes 73732
  16.6 3.8 %copy-start.5 = (f32[48,128]{1,0:T(8,128)}, f32[48,128]{1,0:T(8,128)S(1)}, u32[]{:S(2)}) copy-start(f32[48,128]{1,0:T(8,128)S(1)} %collective-permute-done.2.refs_7_) | copy-start | bytes 73732
  16.6 3.8 %copy-start = (f32[328,128]{1,0:T(8,128)}, f32[328,128]{1,0:T(8,128)S(1)}, u32[]{:S(2)}) copy-start(f32[328,128]{1,0:T(8,128)S(1)} %collective-permute-done.refs_5_.refs_9_) | copy-start | bytes 503812
  20.4 0.7 %copy-start.1 = (f32[328,128]{1,0:T(8,128)}, f32[328,128]{1,0:T(8,128)S(1)}, u32[]{:S(2)}) copy-start(f32[328,128]{1,0:T(8,128)S(1)} %collective-permute-done.1.refs_6_.refs_10_) | copy-start | bytes 503812
  30.4 8.3 %collective-permute-start.5 = (f32[320,128]{1,0:T(8,128)}, f32[320,128]{1,0:T(8,128)S(1)}, u32[]{:S(2)}, u32[]{:S(2)}) collective-permute-start(f32[320,128]{1,0:T(8,128)} %get-tuple-element.25), channel_id=1, source_target_pairs={{0,8},{8,16},{16,24},{24,0},{1,9},{9,17},{17,25},{25,1},{2,10},{10... | collective-permute-start | bytes 491528 | tf_op jit(solution)/shard_map/ppermute | solution.py:304
  31.9 8.2 %collective-permute-start.6 = (f32[320,128]{1,0:T(8,128)}, f32[320,128]{1,0:T(8,128)S(1)}, u32[]{:S(2)}, u32[]{:S(2)}) collective-permute-start(f32[320,128]{1,0:T(8,128)} %get-tuple-element.26), channel_id=1, source_target_pairs={{0,24},{8,0},{16,8},{24,16},{1,25},{9,1},{17,9},{25,17},{2,26},{10... | collective-permute-start | bytes 491528 | tf_op jit(solution)/shard_map/ppermute | solution.py:304
  33.3 4.3 %collective-permute-start.8 = (f32[48,128]{1,0:T(8,128)}, f32[48,128]{1,0:T(8,128)S(1)}, u32[]{:S(2)}, u32[]{:S(2)}) collective-permute-start(f32[48,128]{1,0:T(8,128)} %get-tuple-element.27), channel_id=1, source_target_pairs={{1,0},{2,1},{3,2},{4,3},{5,4},{6,5},{7,6},{9,8},{10,9},{11,10},{12... | collective-permute-start | bytes 73736 | tf_op jit(solution)/shard_map/ppermute | solution.py:304
  34.6 4.1 %collective-permute-start.7 = (f32[48,128]{1,0:T(8,128)}, f32[48,128]{1,0:T(8,128)S(1)}, u32[]{:S(2)}, u32[]{:S(2)}) collective-permute-start(f32[48,128]{1,0:T(8,128)} %get-tuple-element.27), channel_id=1, source_target_pairs={{0,1},{1,2},{2,3},{3,4},{4,5},{5,6},{6,7},{8,9},{9,10},{10,11},{11... | collective-permute-start | bytes 73736 | tf_op jit(solution)/shard_map/ppermute | solution.py:304
  37.7 2.4 %copy-start.6 = (f32[48,128]{1,0:T(8,128)}, f32[48,128]{1,0:T(8,128)S(1)}, u32[]{:S(2)}) copy-start(f32[48,128]{1,0:T(8,128)S(1)} %collective-permute-done.8.refs_7_) | copy-start | bytes 73732
  38.7 1.4 %copy-start.7 = (f32[48,128]{1,0:T(8,128)}, f32[48,128]{1,0:T(8,128)S(1)}, u32[]{:S(2)}) copy-start(f32[48,128]{1,0:T(8,128)S(1)} %collective-permute-done.7.refs_6_) | copy-start | bytes 73732
  38.7 1.4 %copy-start.2 = (f32[320,128]{1,0:T(8,128)}, f32[320,128]{1,0:T(8,128)S(1)}, u32[]{:S(2)}) copy-start(f32[320,128]{1,0:T(8,128)S(1)} %collective-permute-done.5.refs_4_) | copy-start | bytes 491524
  40.1 0.7 %copy-start.3 = (f32[320,128]{1,0:T(8,128)}, f32[320,128]{1,0:T(8,128)S(1)}, u32[]{:S(2)}) copy-start(f32[320,128]{1,0:T(8,128)S(1)} %collective-permute-done.6.refs_5_) | copy-start | bytes 491524

commit v2 on v1

--- a/solution.py
+++ b/solution.py
@@ -5,10 +5,8 @@
 from jax.experimental.pallas import tpu as pltpu
 from jax.sharding import PartitionSpec as P
 
-SUBSTEPS = 2
 
 DIFFUSE = 0.2
-VISCOUS = 0.2
 ADVECTION = 0.5
 THERMAL = 0.2
 HALINE = 0.15
@@ -27,6 +25,7 @@
 LAT_AXES = ("lat", "comp")
 
 VMEM_SPEC = pl.BlockSpec(memory_space=pltpu.VMEM)
+ANY_SPEC = pl.BlockSpec(memory_space=pl.ANY)
 SMEM_SPEC = pl.BlockSpec(memory_space=pltpu.SMEM)
 
 
@@ -42,6 +41,22 @@
     return jnp.broadcast_to(row, (SUB, LANE))
 
 
+def lat_place():
+    return lax.axis_index("lat") * lax.axis_size("comp") + lax.axis_index("comp")
+
+
+def lat_sides(swap_a, swap_b, index):
+    place = lat_place()
+    total = lax.axis_size("lat") * lax.axis_size("comp")
+    tile_a, tile_b = tile_at(swap_a, index), tile_at(swap_b, index)
+    evenly = place % 2 == 0
+    north = jnp.where(jnp.logical_and(place < total - 1, evenly), tile_a, 0.0)
+    north = jnp.where(jnp.logical_and(place < total - 1, jnp.logical_not(evenly)), tile_b, north)
+    south = jnp.where(jnp.logical_and(place > 0, evenly), tile_b, 0.0)
+    south = jnp.where(jnp.logical_and(place > 0, jnp.logical_not(evenly)), tile_a, south)
+    return south, north
+
+
 def tile_at(ref, index):
     return ref[pl.ds(pl.multiple_of(index * SUB, SUB), SUB), :]
 
@@ -55,10 +70,9 @@
 
 
 def pack_kernel(levels, lon_total, x_ref, count_ref, flux_ref, weight_ref, target_ref, slot_ref,
-                east_ref, west_ref, edge_ref, parts_ref):
+                east_ref, west_ref, parts_ref):
     me = lax.axis_index("lon")
     sub = sublane_ids()
-    pair = lane_ids() // 2
     count = count_ref[...]
     rows = FIELDS * levels
 
@@ -84,6 +98,13 @@
         out_ref[pl.ds(rows, EXTRA), :] = jnp.where(
             sub == COUNT_ROW, spread(count_f[column:column + 1, :]), tile
         )
+
+
+def edge_kernel(levels, x_ref, count_ref, after_ref, edge_ref):
+    del after_ref
+    pair = ((lane_ids() + 1) % LANE) // 2
+    count = count_ref[...]
+    count_f = count.astype(jnp.float32)
 
     def group_body(group, carry):
         packed = jnp.zeros((SUB, LANE), jnp.float32)
@@ -93,12 +114,12 @@
             for field in range(FIELDS):
                 j = inner * FIELDS + field
                 value = jnp.where(wet, tile_at(x_ref, field * levels + level), 0.0)
-                packed = jnp.where(pair == j, pltpu.roll(value, 2 * j + 1, 1), packed)
+                packed = jnp.where(pair == j, pltpu.roll(value, 2 * j, 1) if j else value, packed)
         put_tile(edge_ref, group, packed)
         return carry
 
     lax.fori_loop(0, levels // GROUP, group_body, 0)
-    put_tile(edge_ref, levels // GROUP, pltpu.roll(count_f, 1, 1))
+    put_tile(edge_ref, levels // GROUP, count_f)
 
 
 def factor_kernel(levels, rate_ref, count_ref, gain_ref, down_ref, up_ref):
@@ -121,21 +142,22 @@
 
 
 def step_body(levels, first, final, x_ref, depth, depths, gain_ref, down_ref, up_ref,
-              from_west, from_east, from_south, from_north, forcing, out_ref, east_ref, west_ref,
-              edge_ref, merged_ref):
+              from_west, from_east, swap_a, swap_b, forcing, out_ref, east_ref, west_ref,
+              edge_ref, merged_ref, result_ref=None, sem_ref=None):
     sub = sublane_ids()
     lane = lane_ids()
-    pair = lane // 2
+    pair = ((lane + 1) % LANE) // 2
     groups = levels // GROUP
     lat_dev = LANE
-    first_row = (lax.axis_index("lat") * lax.axis_size("comp") + lax.axis_index("comp")) * lat_dev
+    first_row = lat_place() * lat_dev
     lat_total = lat_dev * lax.axis_size("lat") * lax.axis_size("comp")
     row_ids = (first_row + lane).astype(jnp.float32)
     rotation = CORIOLIS * (2.0 * (row_ids + 0.5) / lat_total - 1.0)
     depth_e, depth_w, depth_n, depth_s = depths
     even = lane % 2 == 0
     for group in range(groups):
-        merged_ref[group] = jnp.where(even, tile_at(from_south, group), tile_at(from_north, group))
+        south, north = lat_sides(swap_a, swap_b, group)
+        merged_ref[group] = jnp.where(even, north, pltpu.roll(south, 2, 1))
 
     thermal = THERMAL / HALINE
     push = 0.5 * GRAVITY * HALINE
@@ -154,8 +176,8 @@
             here.append(value)
             east.append(jnp.where(sub == SUB - 1, row_at(from_east, row), pltpu.roll(value, SUB - 1, 0)))
             west.append(jnp.where(sub == 0, row_at(from_west, row), pltpu.roll(value, 1, 0)))
-            north.append(pltpu.roll(jnp.where(lane == 0, side, value), LANE - 1, 1))
-            south.append(pltpu.roll(jnp.where(lane == LANE - 1, side, value), 1, 1))
+            north.append(jnp.where(lane == LANE - 1, side, pltpu.roll(value, LANE - 1, 1)))
+            south.append(jnp.where(lane == 0, side, pltpu.roll(value, 1, 1)))
         wet_e, wet_w, wet_n, wet_s = level < depth_e, level < depth_w, level < depth_n, level < depth_s
         keep = 1.0 - (
             (jnp.where(wet_e, DIFFUSE, 0.0) + jnp.where(wet_w, DIFFUSE, 0.0))
@@ -220,13 +242,28 @@
                 now.append(value)
                 if not final:
                     j = inner * FIELDS + field
-                    packed = jnp.where(pair == j, pltpu.roll(value, 2 * j + 1, 1), packed)
+                    packed = jnp.where(pair == j, pltpu.roll(value, 2 * j, 1) if j else value, packed)
             following = tuple(now)
         if not final:
             put_tile(edge_ref, group, packed)
+        else:
+            for copy in copies_of(group):
+                copy.start()
         return following
 
+    def copies_of(group):
+        size = GROUP * SUB
+        for field in range(FIELDS):
+            start = pl.multiple_of(field * levels * SUB + group * size, size)
+            yield pltpu.make_async_copy(
+                out_ref.at[pl.ds(start, size), :], result_ref.at[pl.ds(start, size), :], sem_ref.at[group, field]
+            )
+
     lax.fori_loop(0, groups, backward_group, (zero,) * FIELDS)
+    if final:
+        for group in range(groups):
+            for copy in copies_of(group):
+                copy.wait()
     if not final:
         rows = FIELDS * levels
         for out_col, column in ((east_ref, SUB - 1), (west_ref, 0)):
@@ -235,7 +272,7 @@
 
 
 def first_kernel(levels, lon_total, x_ref, count_ref, gain_ref, down_ref, up_ref, west_in, east_in,
-                 south_in, north_in, parts_ref, *rest):
+                 swap_a, swap_b, parts_ref, *rest):
     others = rest[:lon_total - 3]
     out_ref, east_ref, west_ref, edge_ref, depth_ref, merged_ref = rest[lon_total - 3:]
     sub = sublane_ids()
@@ -246,12 +283,11 @@
     extra_w = west_in[pl.ds(rows, EXTRA), :]
     extra_e = east_in[pl.ds(rows, EXTRA), :]
     groups = levels // GROUP
-    side_s = tile_at(south_in, groups)
-    side_n = tile_at(north_in, groups)
+    side_s, side_n = lat_sides(swap_a, swap_b, groups)
     depth_e = jnp.where(sub == SUB - 1, spread(extra_e[COUNT_ROW:COUNT_ROW + 1]), pltpu.roll(count_f, SUB - 1, 0))
     depth_w = jnp.where(sub == 0, spread(extra_w[COUNT_ROW:COUNT_ROW + 1]), pltpu.roll(count_f, 1, 0))
-    depth_n = pltpu.roll(jnp.where(lane == 0, pltpu.roll(side_n, LANE - 1, 1), count_f), LANE - 1, 1)
-    depth_s = pltpu.roll(jnp.where(lane == LANE - 1, pltpu.roll(side_s, LANE - 1, 1), count_f), 1, 1)
+    depth_n = jnp.where(lane == LANE - 1, pltpu.roll(side_n, LANE - 1, 1), pltpu.roll(count_f, LANE - 1, 1))
+    depth_s = jnp.where(lane == 0, pltpu.roll(side_s, 1, 1), pltpu.roll(count_f, 1, 1))
     depths = []
     for at, value in enumerate((depth_e, depth_w, depth_n, depth_s)):
         value = value.astype(jnp.int32)
@@ -263,14 +299,14 @@
         for field in range(FIELDS):
             forcing[field] = forcing[field] + jnp.where(mine, spread(tile[field:field + 1]), 0.0)
     step_body(levels, True, False, x_ref, depth, depths, gain_ref, down_ref, up_ref, west_in, east_in,
-              south_in, north_in, forcing, out_ref, east_ref, west_ref, edge_ref, merged_ref)
+              swap_a, swap_b, forcing, out_ref, east_ref, west_ref, edge_ref, merged_ref)
     put_tile(edge_ref, groups, jnp.zeros((SUB, LANE), jnp.float32))
 
 
-def second_kernel(levels, lon_total, x_ref, gain_ref, down_ref, up_ref, west_in, east_in, south_in, north_in,
+def second_kernel(levels, lon_total, x_ref, gain_ref, down_ref, up_ref, west_in, east_in, swap_a, swap_b,
                   depth_ref, extra_w_ref, extra_e_ref, parts_ref, *rest):
     others = rest[:lon_total - 3]
-    out_ref, merged_ref = rest[lon_total - 3:]
+    result_ref, merged_ref, out_ref, sem_ref = rest[lon_total - 3:]
     sub = sublane_ids()
     rows = FIELDS * levels
     extra_w = extra_w_ref[pl.ds(rows, EXTRA), :]
@@ -282,31 +318,47 @@
         for field in range(FIELDS):
             forcing[field] = forcing[field] + jnp.where(mine, spread(tile[field:field + 1]), 0.0)
     step_body(levels, False, True, x_ref, None, depths, gain_ref, down_ref, up_ref, west_in, east_in,
-              south_in, north_in, forcing, out_ref, None, None, None, merged_ref)
-
-
-def call(kernel, outs, args, specs=None, scratch=()):
+              swap_a, swap_b, forcing, out_ref, None, None, None, merged_ref, result_ref, sem_ref)
+
+
+VMEM_BYTES = 16 << 20
+
+
+def call(kernel, outs, args, specs=None, scratch=(), to_hbm=False):
+    specs = specs or [VMEM_SPEC] * len(args)
+    held = [
+        pltpu.with_memory_space_constraint(arg, pltpu.VMEM) if spec is VMEM_SPEC else arg
+        for arg, spec in zip(args, specs)
+    ]
+    kind = jax.ShapeDtypeStruct if to_hbm else pltpu.VMEM
     return pl.pallas_call(
         kernel,
-        out_shape=[jax.ShapeDtypeStruct(shape, dtype) for shape, dtype in outs],
-        in_specs=specs or [VMEM_SPEC] * len(args),
-        out_specs=[VMEM_SPEC] * len(outs),
+        out_shape=[kind(shape, dtype) for shape, dtype in outs],
+        in_specs=specs,
+        out_specs=[ANY_SPEC if to_hbm else VMEM_SPEC] * len(outs),
         scratch_shapes=list(scratch),
-    )(*args)
-
-
-def shift_by(value, axis, amount, periodic):
+        compiler_params=pltpu.CompilerParams(vmem_limit_bytes=VMEM_BYTES),
+    )(*held)
+
+
+def ring_shift(value, axis, amount):
     count = lax.axis_size(axis)
-    if periodic:
-        pairs = [(i, (i + amount) % count) for i in range(count)]
-    else:
-        pairs = [(i, i + amount) for i in range(count) if 0 <= i + amount < count]
+    return lax.ppermute(value, axis, [(i, (i + amount) % count) for i in range(count)])
+
+
+def pair_swap(value, axis, first):
+    count = lax.axis_size(axis)
+    pairs = []
+    for low in range(first, count, 2):
+        high = (low + 1) % count
+        pairs += [(low, high), (high, low)]
     return lax.ppermute(value, axis, pairs)
 
 
 def bind(kernel, *head):
     def bound(*refs):
         return kernel(*head, *refs)
+
     bound.__name__ = kernel.__name__
     return bound
 
@@ -322,36 +374,38 @@
     edges = (((groups + 1) * SUB, lat_dev), f32)
     table = ((levels, lon_dev, lat_dev), f32)
 
-    east, west, edge, parts = call(
+    east, west, parts = call(
         bind(pack_kernel, levels, lon_total),
-        [message, message, edges, ((lon_total, SUB, lat_dev), f32)],
+        [message, message, ((lon_total, SUB, lat_dev), f32)],
         (x, level_count, atmos_flux[0], remap_weight[0], remap_target, remap_slot),
         [VMEM_SPEC] * 4 + [SMEM_SPEC] * 2,
     )
-    from_west = shift_by(east, "lon", 1, True)
-    from_east = shift_by(west, "lon", -1, True)
-    from_south = shift_by(edge, LAT_AXES, 1, False)
-    from_north = shift_by(edge, LAT_AXES, -1, False)
-    others = [shift_by(parts[s], "lon", s, True) for s in range(2, lon_total - 1)]
+    from_west = ring_shift(east, "lon", 1)
+    from_east = ring_shift(west, "lon", -1)
+    others = [ring_shift(parts[s], "lon", s) for s in range(2, lon_total - 1)]
+    (edge,) = call(bind(edge_kernel, levels), [edges], (x, level_count, parts))
+    swap_a = pair_swap(edge, LAT_AXES, 0)
+    swap_b = pair_swap(edge, LAT_AXES, 1)
     gain, down, up = call(bind(factor_kernel, levels), [table] * 3, (mix_rate, level_count))
     scratch = [pltpu.VMEM((groups, SUB, LANE), f32)]
     next_message = ((rows, lat_dev), f32)
     state, east, west, edge, depths = call(
         bind(first_kernel, levels, lon_total),
         [((rows * lon_dev, lat_dev), f32), next_message, next_message, edges, ((4 * SUB, LANE), jnp.int32)],
-        (x, level_count, gain, down, up, from_west, from_east, from_south, from_north, parts, *others),
+        (x, level_count, gain, down, up, from_west, from_east, swap_a, swap_b, parts, *others),
         scratch=scratch,
     )
-    second_west = shift_by(east, "lon", 1, True)
-    second_east = shift_by(west, "lon", -1, True)
-    second_south = shift_by(edge, LAT_AXES, 1, False)
-    second_north = shift_by(edge, LAT_AXES, -1, False)
+    second_west = ring_shift(east, "lon", 1)
+    second_east = ring_shift(west, "lon", -1)
+    second_a = pair_swap(edge, LAT_AXES, 0)
+    second_b = pair_swap(edge, LAT_AXES, 1)
     (state,) = call(
         bind(second_kernel, levels, lon_total),
         [((rows * lon_dev, lat_dev), f32)],
-        (state, gain, down, up, second_west, second_east, second_south, second_north, depths,
+        (state, gain, down, up, second_west, second_east, second_a, second_b, depths,
          from_west, from_east, parts, *others),
-        scratch=scratch,
+        scratch=scratch + [pltpu.VMEM((rows * lon_dev, lat_dev), f32), pltpu.SemaphoreType.DMA((groups, FIELDS))],
+        to_hbm=True,
     )
     return state.reshape(ocean_state.shape)
 
@@ -366,6 +420,7 @@
         P(LAT_AXES, "lon"),
         P(LAT_AXES, "lon"),
     )
+
     return jax.shard_map(
         local,
         mesh=mesh,

time: 49.8 us -> 36.8 us (0.74)
  Pallas kernels: 23.6 us -> 7.22 us
  waiting for transfers between devices: 6.21 us -> 12.3 us
  starting transfers between devices: 17.5 us -> 12 us
  local copies, waits for them, and re-layouts: 2.01 us -> 4.97 us
    pallas_call x4 -> x5, Pallas kernels: 23.6 us -> 7.22 us  [call(): pl.pallas_call(kernel, out_shape=[kind(shape, dtype) for shape, dtype in...]
    ppermute x9, waiting for transfers between devices: 6.21 us -> 12.3 us  [the longest x5 7.26 us: ring_shift(): lax.ppermute(value, axis, [(i, (i + amount) % count) for i in range(count)])]
    ppermute x9, starting transfers between devices: 17.5 us -> 12 us  [the longest x5 7.42 us: ring_shift(): lax.ppermute(value, axis, [(i, (i + amount) % count) for i in range(count)])]
    unnamed x18 -> x16, local copies, waits for them, and re-layouts: 1.33 us -> 4.96 us
    squeeze x1, local copies, waits for them, and re-layouts: 0.68 us -> 0.01 us  [local(): others = [ring_shift(parts[s], 'lon', s) for s in range(2, lon_total - 1)]]
  transfers between devices with their start and end apart: 9 -> 9, of which waited for: 3 -> 5; matrix products, arithmetic and copies ran while one was open for 1% -> 0% of each run, Pallas kernels for 5% -> 2%
where the time goes in v2:
time: 36.8 us; the launch traced here: 36.6 us
  waiting for transfers between devices  12.3 us (33%)
  starting transfers between devices  12 us (33%)
  Pallas kernels  7.22 us (20%)
  local copies, waits for them, and re-layouts  4.97 us (14%)
    ppermute x5, starting transfers between devices, ring_shift(): lax.ppermute(value, axis, [(i, (i + amount) % count) for i in range(count)])  7.42 us
    ppermute x5, waiting for transfers between devices, ring_shift(): lax.ppermute(value, axis, [(i, (i + amount) % count) for i in range(count)])  7.26 us
    pallas_call x5, Pallas kernels, call(): pl.pallas_call(kernel, out_shape=[kind(shape, dtype) for shape, dtype in...  7.22 us
    ppermute x4, waiting for transfers between devices, pair_swap(): return lax.ppermute(value, axis, pairs)  5.05 us
    unnamed x16, local copies, waits for them, and re-layouts  4.96 us
    ppermute x4, starting transfers between devices, pair_swap(): return lax.ppermute(value, axis, pairs)  4.59 us
  transfers between devices with their start and end apart: 9, of which 5 were waited for; matrix products, arithmetic and copies ran while one was open for 0% of the time, Pallas kernels for 2%

profile of v2, /device:TPU:0, one launch (start us, length us, event | category | flops | bytes accessed | tf_op | source)
XLA Modules:
  0.0 36.6 jit_solution(1931075984117016777)
XLA Ops:
  0.0 0.0 copy-start
  0.0 1.3 %copy-done = f32[4,80,8,128]{3,2,1,0:T(8,128)S(1)} copy-done((f32[4,80,8,128]{3,2,1,0:T(8,128)S(1)}, f32[4,80,8,128]{3,2,1,0:T(8,128)}, u32[]{:S(2)}) %copy-start) | copy-done | bytes 1310744
  1.3 0.0 copy-start.3
  1.3 0.9 %copy-done.3 = bf16[1,4,256,128]{3,2,1,0:T(8,128)(2,1)S(1)} copy-done((bf16[1,4,256,128]{3,2,1,0:T(8,128)(2,1)S(1)}, bf16[1,4,256,128]{3,2,1,0:T(8,128)(2,1)}, u32[]{:S(2)}) %copy-start.3) | copy-done | bytes 262168
  2.3 0.0 copy-start.4
  2.3 0.7 %copy-done.4 = s32[8,128]{1,0:T(8,128)S(1)} copy-done((s32[8,128]{1,0:T(8,128)S(1)}, s32[8,128]{1,0:T(8,128)}, u32[]{:S(2)}) %copy-start.4) | copy-done | bytes 4120
  3.0 0.0 copy-start.5
  3.0 0.7 %copy-done.5 = bf16[1,4,4,256]{3,2,1,0:T(4,128)(2,1)S(1)} copy-done((bf16[1,4,4,256]{3,2,1,0:T(4,128)(2,1)S(1)}, bf16[1,4,4,256]{3,2,1,0:T(4,128)(2,1)}, u32[]{:S(2)}) %copy-start.5) | copy-done | bytes 8216
  3.7 0.0 copy-start.6
  3.7 0.7 %copy-done.6 = s32[1,4]{1,0:T(1,128)S(1)} copy-done((s32[1,4]{1,0:T(1,128)S(1)}, s32[1,4]{1,0:T(1,128)}, u32[]{:S(2)}) %copy-start.6) | copy-done | bytes 40
  4.3 0.0 copy-start.7
  4.3 0.7 %copy-done.7 = s32[1,4]{1,0:T(1,128)S(1)} copy-done((s32[1,4]{1,0:T(1,128)S(1)}, s32[1,4]{1,0:T(1,128)}, u32[]{:S(2)}) %copy-start.7) | copy-done | bytes 40
  5.0 0.0 copy-start.2
  5.0 0.0 copy-start.1
  5.0 0.7 %shard_map.74 = (f32[328,128]{1,0:T(8,128)S(1)}, f32[328,128]{1,0:T(8,128)S(1)}, f32[4,8,128]{2,1,0:T(8,128)S(1)}) custom-call(f32[2560,128]{1,0:T(8,128)S(1)} %bitcast.6, s32[8,128]{1,0:T(8,128)S(1)} %copy-done.4, bf16[4,4,256]{2,1,0:T(4,128)(2,1)S(1)} %bitcast.10, bf16[4,256,128]{2,1,0:T(8,128)(2,1)S(1)} %bitcast.9, s32[1,4]{1,0:T(1,128)S(1)} %copy-done.6, ...), custom_call_target="tpu_custom_call" | custom-call | tf_op jit(solution)/shard_map/pallas_call | solution.py:334
  5.7 0.7 %shard_map.75 = f32[48,128]{1,0:T(8,128)S(1)} custom-call(f32[2560,128]{1,0:T(8,128)S(1)} %bitcast.7, s32[8,128]{1,0:T(8,128)S(1)} %copy-done.4, f32[4,8,128]{2,1,0:T(8,128)S(1)} %get-tuple-element.21.refs_2_.refs_9_.refs_11_), custom_call_target="tpu_custom_call" | custom-call | tf_op jit(solution)/shard_map/pallas_call | solution.py:334
  6.4 4.6 %collective-permute-start.3 = (f32[48,128]{1,0:T(8,128)S(1)}, f32[48,128]{1,0:T(8,128)S(1)}, u32[]{:S(2)}, u32[]{:S(2)}) collective-permute-start(f32[48,128]{1,0:T(8,128)S(1)} %shard_map.75), channel_id=1, source_target_pairs={{1,2},{2,1},{3,4},{4,3},{5,6},{6,5},{7,0},{0,7},{9,10},{10,9},{11,... | collective-permute-start | bytes 73736 | tf_op jit(solution)/shard_map/ppermute | solution.py:355
  10.9 0.0 collective-permute-start.2
  10.9 1.5 %collective-permute-start = (f32[328,128]{1,0:T(8,128)S(1)}, f32[328,128]{1,0:T(8,128)S(1)}, u32[]{:S(2)}, u32[]{:S(2)}) collective-permute-start(f32[328,128]{1,0:T(8,128)S(1)} %get-tuple-element.19), channel_id=1, source_target_pairs={{0,8},{8,16},{16,24},{24,0},{1,9},{9,17},{17,25},{25,1},{2,10},{10... | collective-permute-start | bytes 503816 | tf_op jit(solution)/shard_map/ppermute | solution.py:346
  12.4 1.4 %collective-permute-start.1 = (f32[328,128]{1,0:T(8,128)S(1)}, f32[328,128]{1,0:T(8,128)S(1)}, u32[]{:S(2)}, u32[]{:S(2)}) collective-permute-start(f32[328,128]{1,0:T(8,128)S(1)} %get-tuple-element.20), channel_id=1, source_target_pairs={{0,24},{8,0},{16,8},{24,16},{1,25},{9,1},{17,9},{25,17},{2,26},{10... | collective-permute-start | bytes 503816 | tf_op jit(solution)/shard_map/ppermute | solution.py:346
  13.9 1.5 %collective-permute-start.4 = (f32[8,128]{1,0:T(8,128)S(1)}, f32[8,128]{1,0:T(8,128)S(1)}, u32[]{:S(2)}, u32[]{:S(2)}) collective-permute-start(f32[8,128]{1,0:T(8,128)S(1)} %slice_bitcast_fusion), channel_id=1, source_target_pairs={{0,16},{8,24},{16,0},{24,8},{1,17},{9,25},{17,1},{25,9},{2,18},{10... | collective-permute-start | bytes 12296 | tf_op jit(solution)/shard_map/ppermute | solution.py:346
  15.4 0.0 copy-done.2
  15.4 0.8 %shard_map.73 = (f32[80,8,128]{2,1,0:T(8,128)S(1)}, f32[80,8,128]{2,1,0:T(8,128)S(1)}, f32[80,8,128]{2,1,0:T(8,128)S(1)}) custom-call(f32[80,8,128]{2,1,0:T(8,128)S(1)} %copy-done.2, s32[8,128]{1,0:T(8,128)S(1)} %copy-done.4), custom_call_target="tpu_custom_call" | custom-call | tf_op jit(solution)/shard_map/pallas_call | solution.py:334
  16.2 1.7 %collective-permute-done.4.refs_10_.refs_12_ = f32[8,128]{1,0:T(8,128)S(1)} collective-permute-done((f32[8,128]{1,0:T(8,128)S(1)}, f32[8,128]{1,0:T(8,128)S(1)}, u32[]{:S(2)}, u32[]{:S(2)}) %collective-permute-start.4) | collective-permute-done | bytes 4128 | tf_op jit(solution)/shard_map/ppermute | solution.py:346
  17.8 0.0 collective-permute-done.3.refs_8_
  17.8 0.0 collective-permute-done.2.refs_7_
  17.8 1.2 %collective-permute-done.refs_5_.refs_9_ = f32[328,128]{1,0:T(8,128)S(1)} collective-permute-done((f32[328,128]{1,0:T(8,128)S(1)}, f32[328,128]{1,0:T(8,128)S(1)}, u32[]{:S(2)}, u32[]{:S(2)}) %collective-permute-start) | collective-permute-done | bytes 167968 | tf_op jit(solution)/shard_map/ppermute | solution.py:346
  19.0 3.2 %collective-permute-done.1.refs_6_.refs_10_ = f32[328,128]{1,0:T(8,128)S(1)} collective-permute-done((f32[328,128]{1,0:T(8,128)S(1)}, f32[328,128]{1,0:T(8,128)S(1)}, u32[]{:S(2)}, u32[]{:S(2)}) %collective-permute-start.1) | collective-permute-done | bytes 167968 | tf_op jit(solution)/shard_map/ppermute | solution.py:346
  22.2 0.0 copy-done.1
  22.2 2.3 %shard_map.76 = (f32[2560,128]{1,0:T(8,128)S(1)}, f32[320,128]{1,0:T(8,128)S(1)}, f32[320,128]{1,0:T(8,128)S(1)}, f32[48,128]{1,0:T(8,128)S(1)}, s32[32,128]{1,0:T(8,128)S(1)}) custom-call(f32[2560,128]{1,0:T(8,128)S(1)} %bitcast.8, s32[8,128]{1,0:T(8,128)S(1)} %copy-done.4, f32[80,8,128]{2,1,0:T(8,128)S(1)} %get-tuple-element.16.refs_2_.refs_1_, ...), custom_call_target="tpu_custom_call" | custom-call | tf_op jit(solution)/shard_map/pallas_call | solution.py:334
  24.5 1.5 %collective-permute-start.5 = (f32[320,128]{1,0:T(8,128)S(1)}, f32[320,128]{1,0:T(8,128)S(1)}, u32[]{:S(2)}, u32[]{:S(2)}) collective-permute-start(f32[320,128]{1,0:T(8,128)S(1)} %get-tuple-element.23), channel_id=1, source_target_pairs={{0,8},{8,16},{16,24},{24,0},{1,9},{9,17},{17,25},{25,1},{2,10},{10... | collective-permute-start | bytes 491528 | tf_op jit(solution)/shard_map/ppermute | solution.py:346
  26.0 1.4 %collective-permute-start.6 = (f32[320,128]{1,0:T(8,128)S(1)}, f32[320,128]{1,0:T(8,128)S(1)}, u32[]{:S(2)}, u32[]{:S(2)}) collective-permute-start(f32[320,128]{1,0:T(8,128)S(1)} %get-tuple-element.24), channel_id=1, source_target_pairs={{0,24},{8,0},{16,8},{24,16},{1,25},{9,1},{17,9},{25,17},{2,26},{10... | collective-permute-start | bytes 491528 | tf_op jit(solution)/shard_map/ppermute | solution.py:346
  27.5 0.0 collective-permute-start.8
  27.5 0.0 collective-permute-start.7
  27.5 5.0 %collective-permute-done.8.refs_7_ = f32[48,128]{1,0:T(8,128)S(1)} collective-permute-done((f32[48,128]{1,0:T(8,128)S(1)}, f32[48,128]{1,0:T(8,128)S(1)}, u32[]{:S(2)}, u32[]{:S(2)}) %collective-permute-start.8) | collective-permute-done | bytes 24608 | tf_op jit(solution)/shard_map/ppermute | solution.py:355
  32.5 0.0 collective-permute-done.7.refs_6_
  32.5 0.0 collective-permute-done.5.refs_4_
  32.5 1.2 %collective-permute-done.6.refs_5_ = f32[320,128]{1,0:T(8,128)S(1)} collective-permute-done((f32[320,128]{1,0:T(8,128)S(1)}, f32[320,128]{1,0:T(8,128)S(1)}, u32[]{:S(2)}, u32[]{:S(2)}) %collective-permute-start.6) | collective-permute-done | bytes 163872 | tf_op jit(solution)/shard_map/ppermute | solution.py:346
  33.7 2.8 %shard_map.77 = f32[2560,128]{1,0:T(8,128)} custom-call(f32[2560,128]{1,0:T(8,128)S(1)} %get-tuple-element.22.refs_0_, f32[80,8,128]{2,1,0:T(8,128)S(1)} %get-tuple-element.16.refs_2_.refs_1_, f32[80,8,128]{2,1,0:T(8,128)S(1)} %get-tuple-element.17.refs_3_.refs_2_, f32[80,8,128]{2,1,0:T(8,128)S(1)} %get-tuple-element.18.refs_4_.refs_3_, ...), custom_call_target="tpu_custom_call" | custom-call | tf_op jit(solution)/shard_map/pallas_call | solution.py:334
  (1 shorter events, 0.0 us)
Async XLA Ops:
  0.0 1.3 %copy-start = (f32[4,80,8,128]{3,2,1,0:T(8,128)S(1)}, f32[4,80,8,128]{3,2,1,0:T(8,128)}, u32[]{:S(2)}) copy-start(f32[4,80,8,128]{3,2,1,0:T(8,128)} %param.7) | copy-start | bytes 3932164
  1.3 0.9 %copy-start.3 = (bf16[1,4,256,128]{3,2,1,0:T(8,128)(2,1)S(1)}, bf16[1,4,256,128]{3,2,1,0:T(8,128)(2,1)}, u32[]{:S(2)}) copy-start(bf16[1,4,256,128]{3,2,1,0:T(8,128)(2,1)} %param.11) | copy-start | bytes 786436
  2.3 0.7 %copy-start.4 = (s32[8,128]{1,0:T(8,128)S(1)}, s32[8,128]{1,0:T(8,128)}, u32[]{:S(2)}) copy-start(s32[8,128]{1,0:T(8,128)} %refs_1_.7) | copy-start | bytes 12292
  3.0 0.7 %copy-start.5 = (bf16[1,4,4,256]{3,2,1,0:T(4,128)(2,1)S(1)}, bf16[1,4,4,256]{3,2,1,0:T(4,128)(2,1)}, u32[]{:S(2)}) copy-start(bf16[1,4,4,256]{3,2,1,0:T(4,128)(2,1)} %param.10) | copy-start | bytes 24580
  3.7 0.7 %copy-start.6 = (s32[1,4]{1,0:T(1,128)S(1)}, s32[1,4]{1,0:T(1,128)}, u32[]{:S(2)}) copy-start(s32[1,4]{1,0:T(1,128)} %refs_4_.1) | copy-start | bytes 52
  4.3 0.7 %copy-start.7 = (s32[1,4]{1,0:T(1,128)S(1)}, s32[1,4]{1,0:T(1,128)}, u32[]{:S(2)}) copy-start(s32[1,4]{1,0:T(1,128)} %refs_5_.1) | copy-start | bytes 52
  5.0 10.4 %copy-start.2 = (f32[80,8,128]{2,1,0:T(8,128)S(1)}, f32[80,8,128]{2,1,0:T(8,128)}, u32[]{:S(2)}) copy-start(f32[80,8,128]{2,1,0:T(8,128)} %refs_0_.1) | copy-start | bytes 983044
  5.0 17.2 %copy-start.1 = (f32[4,80,8,128]{3,2,1,0:T(8,128)S(1)}, f32[4,80,8,128]{3,2,1,0:T(8,128)}, u32[]{:S(2)}) copy-start(f32[4,80,8,128]{3,2,1,0:T(8,128)} %param.7) | copy-start | bytes 3932164
  6.4 11.5 %collective-permute-start.3 = (f32[48,128]{1,0:T(8,128)S(1)}, f32[48,128]{1,0:T(8,128)S(1)}, u32[]{:S(2)}, u32[]{:S(2)}) collective-permute-start(f32[48,128]{1,0:T(8,128)S(1)} %shard_map.75), channel_id=1, source_target_pairs={{1,2},{2,1},{3,4},{4,3},{5,6},{6,5},{7,0},{0,7},{9,10},{10,9},{11,... | collective-permute-start | bytes 73736 | tf_op jit(solution)/shard_map/ppermute | solution.py:355
  10.9 6.9 %collective-permute-start.2 = (f32[48,128]{1,0:T(8,128)S(1)}, f32[48,128]{1,0:T(8,128)S(1)}, u32[]{:S(2)}, u32[]{:S(2)}) collective-permute-start(f32[48,128]{1,0:T(8,128)S(1)} %shard_map.75), channel_id=1, source_target_pairs={{0,1},{1,0},{2,3},{3,2},{4,5},{5,4},{6,7},{7,6},{8,9},{9,8},{10,11... | collective-permute-start | bytes 73736 | tf_op jit(solution)/shard_map/ppermute | solution.py:355
  10.9 8.1 %collective-permute-start = (f32[328,128]{1,0:T(8,128)S(1)}, f32[328,128]{1,0:T(8,128)S(1)}, u32[]{:S(2)}, u32[]{:S(2)}) collective-permute-start(f32[328,128]{1,0:T(8,128)S(1)} %get-tuple-element.19), channel_id=1, source_target_pairs={{0,8},{8,16},{16,24},{24,0},{1,9},{9,17},{17,25},{25,1},{2,10},{10... | collective-permute-start | bytes 503816 | tf_op jit(solution)/shard_map/ppermute | solution.py:346
  12.4 9.8 %collective-permute-start.1 = (f32[328,128]{1,0:T(8,128)S(1)}, f32[328,128]{1,0:T(8,128)S(1)}, u32[]{:S(2)}, u32[]{:S(2)}) collective-permute-start(f32[328,128]{1,0:T(8,128)S(1)} %get-tuple-element.20), channel_id=1, source_target_pairs={{0,24},{8,0},{16,8},{24,16},{1,25},{9,1},{17,9},{25,17},{2,26},{10... | collective-permute-start | bytes 503816 | tf_op jit(solution)/shard_map/ppermute | solution.py:346
  13.9 4.0 %collective-permute-start.4 = (f32[8,128]{1,0:T(8,128)S(1)}, f32[8,128]{1,0:T(8,128)S(1)}, u32[]{:S(2)}, u32[]{:S(2)}) collective-permute-start(f32[8,128]{1,0:T(8,128)S(1)} %slice_bitcast_fusion), channel_id=1, source_target_pairs={{0,16},{8,24},{16,0},{24,8},{1,17},{9,25},{17,1},{25,9},{2,18},{10... | collective-permute-start | bytes 12296 | tf_op jit(solution)/shard_map/ppermute | solution.py:346
  24.5 8.0 %collective-permute-start.5 = (f32[320,128]{1,0:T(8,128)S(1)}, f32[320,128]{1,0:T(8,128)S(1)}, u32[]{:S(2)}, u32[]{:S(2)}) collective-permute-start(f32[320,128]{1,0:T(8,128)S(1)} %get-tuple-element.23), channel_id=1, source_target_pairs={{0,8},{8,16},{16,24},{24,0},{1,9},{9,17},{17,25},{25,1},{2,10},{10... | collective-permute-start | bytes 491528 | tf_op jit(solution)/shard_map/ppermute | solution.py:346
  26.0 7.7 %collective-permute-start.6 = (f32[320,128]{1,0:T(8,128)S(1)}, f32[320,128]{1,0:T(8,128)S(1)}, u32[]{:S(2)}, u32[]{:S(2)}) collective-permute-start(f32[320,128]{1,0:T(8,128)S(1)} %get-tuple-element.24), channel_id=1, source_target_pairs={{0,24},{8,0},{16,8},{24,16},{1,25},{9,1},{17,9},{25,17},{2,26},{10... | collective-permute-start | bytes 491528 | tf_op jit(solution)/shard_map/ppermute | solution.py:346
  27.5 5.0 %collective-permute-start.8 = (f32[48,128]{1,0:T(8,128)S(1)}, f32[48,128]{1,0:T(8,128)S(1)}, u32[]{:S(2)}, u32[]{:S(2)}) collective-permute-start(f32[48,128]{1,0:T(8,128)S(1)} %get-tuple-element.25), channel_id=1, source_target_pairs={{1,2},{2,1},{3,4},{4,3},{5,6},{6,5},{7,0},{0,7},{9,10},{10,9},{11,... | collective-permute-start | bytes 73736 | tf_op jit(solution)/shard_map/ppermute | solution.py:355
  27.5 5.0 %collective-permute-start.7 = (f32[48,128]{1,0:T(8,128)S(1)}, f32[48,128]{1,0:T(8,128)S(1)}, u32[]{:S(2)}, u32[]{:S(2)}) collective-permute-start(f32[48,128]{1,0:T(8,128)S(1)} %get-tuple-element.25), channel_id=1, source_target_pairs={{0,1},{1,0},{2,3},{3,2},{4,5},{5,4},{6,7},{7,6},{8,9},{9,8},{10,11... | collective-permute-start | bytes 73736 | tf_op jit(solution)/shard_map/ppermute | solution.py:355

commit v3 on v2

v3 whole, which is shorter than its diff:
```python
import jax
import jax.numpy as jnp
from jax import lax
from jax.experimental import pallas as pl
from jax.experimental.pallas import tpu as pltpu
from jax.sharding import PartitionSpec as P


DIFFUSE = 0.2
ADVECTION = 0.5
THERMAL = 0.2
HALINE = 0.15
GRAVITY = 0.05
CORIOLIS = 0.3
SURFACE_GAIN = (0.5, 0.4, 0.6, 0.6)

FIELDS = 4
SUB = 8
LANE = 128
PAIRS = LANE // 2
GROUP = PAIRS // FIELDS
EXTRA = 8
SLOT_ROW = 4
COUNT_ROW = 5
LAT_AXES = ("lat", "comp")
QUARTER = 0.5 * ADVECTION
WARMTH = THERMAL / HALINE
PUSH = 0.5 * GRAVITY * HALINE

VMEM_SPEC = pl.BlockSpec(memory_space=pltpu.VMEM)
HBM_SPEC = pl.BlockSpec(memory_space=pltpu.HBM)
VMEM_BYTES = 16 << 20


def sublane_ids():
    return lax.broadcasted_iota(jnp.int32, (SUB, LANE), 0)


def lane_ids():
    return lax.broadcasted_iota(jnp.int32, (SUB, LANE), 1)


def zeros():
    return jnp.zeros((SUB, LANE), jnp.float32)


def spread(row):
    return jnp.broadcast_to(row, (SUB, LANE))


def tile_at(ref, index):
    return ref[pl.ds(pl.multiple_of(index * SUB, SUB), SUB), :]


def put_tile(ref, index, value):
    ref[pl.ds(pl.multiple_of(index * SUB, SUB), SUB), :] = value


def lat_place():
    return lax.axis_index("lat") * lax.axis_size("comp") + lax.axis_index("comp")


def lat_sides(swap_a, swap_b, index):
    place = lat_place()
    total = lax.axis_size("lat") * lax.axis_size("comp")
    tile_a, tile_b = tile_at(swap_a, index), tile_at(swap_b, index)
    evenly = place % 2 == 0
    north = jnp.where(jnp.logical_and(place < total - 1, evenly), tile_a, 0.0)
    north = jnp.where(jnp.logical_and(place < total - 1, jnp.logical_not(evenly)), tile_b, north)
    south = jnp.where(jnp.logical_and(place > 0, evenly), tile_b, 0.0)
    south = jnp.where(jnp.logical_and(place > 0, jnp.logical_not(evenly)), tile_a, south)
    return south, north


def column_tiles(levels, level, east_ref, west_ref, even):
    half = levels // 2
    if level < half:
        return jnp.where(even, tile_at(east_ref, level), pltpu.roll(tile_at(west_ref, level), 1, 0))
    at = level - half
    return jnp.where(even, pltpu.roll(tile_at(east_ref, at), SUB - 1, 0), tile_at(west_ref, at))


def column_kernel(levels, lon_total, x_ref, count_hbm, flux_hbm, weight_hbm, target_hbm, slot_hbm,
                  east_ref, west_ref, parts_ref, count_ref,
                  columns, flux_ref, weight_ref, target_ref, slot_ref, sems):
    me = lax.axis_index("lon")
    half = levels // 2
    sub = sublane_ids()
    copies = [
        pltpu.make_async_copy(count_hbm, count_ref, sems.at[2]),
        pltpu.make_async_copy(flux_hbm, flux_ref, sems.at[3]),
        pltpu.make_async_copy(weight_hbm, weight_ref, sems.at[4]),
        pltpu.make_async_copy(target_hbm, target_ref, sems.at[5]),
        pltpu.make_async_copy(slot_hbm, slot_ref, sems.at[6]),
    ]
    sides = [
        pltpu.make_async_copy(x_ref.at[:, SUB - 1, :], columns.at[0], sems.at[0]),
        pltpu.make_async_copy(x_ref.at[:, 0, :], columns.at[1], sems.at[1]),
    ]
    for copy in sides + copies:
        copy.start()
    for copy in copies:
        copy.wait()

    blocks = flux_ref.shape[0]
    for block in range(blocks):
        partial = jnp.dot(flux_ref[block], weight_ref[block], preferred_element_type=jnp.float32)
        slot = slot_ref[0, block].astype(jnp.float32)
        tile = jnp.concatenate([partial, jnp.full((SUB - FIELDS, LANE), slot, jnp.float32)], axis=0)
        shift = lax.rem(target_ref[0, block] - me + lon_total, lon_total)
        parts_ref[shift] = tile

    count = count_ref[...]
    count_f = count.astype(jnp.float32)
    for side, (out_ref, column, shift) in enumerate(
        ((east_ref, SUB - 1, 1), (west_ref, 0, lon_total - 1))
    ):
        sides[side].wait()
        depth = spread(count[column:column + 1, :])
        for field in range(FIELDS):
            for start in range(0, levels, SUB):
                value = columns[side, pl.ds(field * levels + start, SUB), :]
                value = jnp.where(start + sub < depth, value, 0.0)
                upper = start // half
                row = (start - upper * half) * SUB + 2 * field + upper
                out_ref[pl.ds(row, SUB, stride=SUB), :] = value
        out_ref[pl.ds(half * SUB, EXTRA), :] = jnp.where(
            sub == COUNT_ROW, spread(count_f[column:column + 1, :]), parts_ref[shift]
        )


def edge_kernel(levels, x_ref, count_ref, edge_ref):
    pair = ((lane_ids() + 1) % LANE) // 2
    count = count_ref[...]

    def group_body(group, carry):
        packed = zeros()
        for inner in range(GROUP):
            level = group * GROUP + inner
            wet = level < count
            for field in range(FIELDS):
                j = inner * FIELDS + field
                value = jnp.where(wet, tile_at(x_ref, field * levels + level), 0.0)
                packed = jnp.where(pair == j, pltpu.roll(value, 2 * j, 1) if j else value, packed)
        put_tile(edge_ref, group, packed)
        return carry

    lax.fori_loop(0, levels // GROUP, group_body, 0)
    put_tile(edge_ref, levels // GROUP, count.astype(jnp.float32))


def factor_kernel(levels, rate_ref, count_ref, gain_ref, down_ref, up_ref, reply_ref,
                  edge_gain_ref, edge_down_ref, edge_up_ref):
    count = count_ref[...]

    def level_body(level, carry):
        lower, prev, reply = carry
        upper = jnp.where(level + 1 < count, tile_at(rate_ref, level), 0.0)
        upper = jnp.where(level < levels - 1, upper, 0.0)
        pivot = 1.0 + upper + lower - lower * prev
        inverse = 1.0 / pivot
        ratio = upper * inverse
        gain = jnp.where(level < count, inverse, 0.0)
        down = lower * inverse
        put_tile(gain_ref, level, gain)
        put_tile(down_ref, level, down)
        put_tile(up_ref, level, ratio)
        reply = jnp.where(level == 0, gain, down * reply)
        put_tile(reply_ref, level, reply)
        return upper, ratio, reply

    lax.fori_loop(0, levels, level_body, (zeros(), zeros(), zeros()), unroll=8)

    def back_body(step, following):
        level = levels - 1 - step
        value = tile_at(reply_ref, level) + tile_at(up_ref, level) * following
        put_tile(reply_ref, level, value)
        return value

    lax.fori_loop(0, levels, back_body, zeros(), unroll=8)
    for source_ref, out_ref in ((gain_ref, edge_gain_ref), (down_ref, edge_down_ref), (up_ref, edge_up_ref)):
        pack_edges(levels, 1, source_ref, out_ref)


def pack_edges(levels, fields, source_ref, out_ref):
    for side, column in ((0, SUB - 1), (1, 0)):
        for start in range(0, levels, SUB):
            for field in range(FIELDS):
                if field < fields:
                    row = (field * levels + start) * SUB + column
                    value = source_ref[pl.ds(row, SUB, stride=SUB), :]
                out_ref[pl.ds(start * SUB + 2 * field + side, SUB, stride=SUB), :] = value


def inner_step(levels, first, x_ref, depth, depths, gain_ref, down_ref, up_ref, swap_a, swap_b,
               out_ref, merged_ref, group_done, force_ref=None):
    sub = sublane_ids()
    lane = lane_ids()
    even = lane % 2 == 0
    groups = levels // GROUP
    lat_total = LANE * lax.axis_size("lat") * lax.axis_size("comp")
    row_ids = (lat_place() * LANE + lane).astype(jnp.float32)
    rotation = CORIOLIS * (2.0 * (row_ids + 0.5) / lat_total - 1.0)
    depth_e, depth_w, depth_n, depth_s = depths
    for group in range(groups):
        south, north = lat_sides(swap_a, swap_b, group)
        merged_ref[group] = jnp.where(even, north, pltpu.roll(south, 2, 1))

    def forward_level(level, inner, halo, carry):
        sum_e, sum_w, sum_n, sum_s, *prev = carry
        here, east, west, north, south = [], [], [], [], []
        for field in range(FIELDS):
            value = tile_at(x_ref, field * levels + level)
            if first:
                value = jnp.where(level < depth, value, 0.0)
            j = inner * FIELDS + field
            side = pltpu.roll(halo, (LANE - 1 - 2 * j) % LANE, 1)
            here.append(value)
            east.append(jnp.where(sub == SUB - 1, 0.0, pltpu.roll(value, SUB - 1, 0)))
            west.append(jnp.where(sub == 0, 0.0, pltpu.roll(value, 1, 0)))
            north.append(jnp.where(lane == LANE - 1, side, pltpu.roll(value, LANE - 1, 1)))
            south.append(jnp.where(lane == 0, side, pltpu.roll(value, 1, 1)))
        wet_e, wet_w, wet_n, wet_s = level < depth_e, level < depth_w, level < depth_n, level < depth_s
        keep = 1.0 - (
            (jnp.where(wet_e, DIFFUSE, 0.0) + jnp.where(wet_w, DIFFUSE, 0.0))
            + (jnp.where(wet_n, DIFFUSE, 0.0) + jnp.where(wet_s, DIFFUSE, 0.0))
        )
        sum_e = sum_e + (east[1] - WARMTH * east[0])
        sum_w = sum_w + (west[1] - WARMTH * west[0])
        sum_n = sum_n + (north[1] - WARMTH * north[0])
        sum_s = sum_s + (south[1] - WARMTH * south[0])
        force_x = PUSH * (jnp.where(wet_e, sum_e, 0.0) - jnp.where(wet_w, sum_w, 0.0))
        force_y = PUSH * (jnp.where(wet_n, sum_n, 0.0) - jnp.where(wet_s, sum_s, 0.0))
        u, v = here[2], here[3]
        u_part = QUARTER * u
        v_part = QUARTER * v
        gain = tile_at(gain_ref, level)
        down = tile_at(down_ref, level)
        done = []
        for field in range(FIELDS):
            around = (east[field] + west[field]) + (north[field] + south[field])
            value = keep * here[field] + DIFFUSE * around
            if field < 2:
                value = value - (
                    u_part * (east[field] - west[field]) + v_part * (north[field] - south[field])
                )
            elif field == 2:
                value = value + (rotation * v - force_x)
            else:
                value = value - (rotation * u + force_y)
            if inner == 0 and force_ref is not None:
                value = value + jnp.where(level == 0, tile_at(force_ref, FIELDS + field), 0.0)
            value = value * gain + down * prev[field]
            put_tile(out_ref, field * levels + level, value)
            done.append(value)
        return (sum_e, sum_w, sum_n, sum_s, *done)

    def forward_group(group, carry):
        halo = merged_ref[group]
        for inner in range(GROUP):
            carry = forward_level(group * GROUP + inner, inner, halo, carry)
        return carry

    lax.fori_loop(0, groups, forward_group, (zeros(),) * 8)

    def backward_group(step, following):
        group = groups - 1 - step
        for inner in range(GROUP - 1, -1, -1):
            level = group * GROUP + inner
            ratio = tile_at(up_ref, level)
            now = []
            for field in range(FIELDS):
                value = tile_at(out_ref, field * levels + level) + ratio * following[field]
                put_tile(out_ref, field * levels + level, value)
                now.append(value)
            following = tuple(now)
        group_done(group)
        return following

    lax.fori_loop(0, groups, backward_group, (zeros(),) * FIELDS)


def first_kernel(levels, x_ref, count_ref, gain_ref, down_ref, up_ref, swap_a, swap_b,
                 out_ref, packed_ref, depth_ref, merged_ref):
    sub = sublane_ids()
    lane = lane_ids()
    depth = count_ref[...]
    count_f = depth.astype(jnp.float32)
    side_s, side_n = lat_sides(swap_a, swap_b, levels // GROUP)
    depths = []
    for at, value in enumerate((
        jnp.where(sub == SUB - 1, 0.0, pltpu.roll(count_f, SUB - 1, 0)),
        jnp.where(sub == 0, 0.0, pltpu.roll(count_f, 1, 0)),
        jnp.where(lane == LANE - 1, pltpu.roll(side_n, LANE - 1, 1), pltpu.roll(count_f, LANE - 1, 1)),
        jnp.where(lane == 0, pltpu.roll(side_s, 1, 1), pltpu.roll(count_f, 1, 1)),
    )):
        value = value.astype(jnp.int32)
        put_tile(depth_ref, at, value)
        depths.append(value)
    inner_step(levels, True, x_ref, depth, depths, gain_ref, down_ref, up_ref, swap_a, swap_b,
               out_ref, merged_ref, lambda group: None)
    pack_edges(levels, FIELDS, out_ref, packed_ref)


def second_kernel(levels, x_ref, depth_ref, gain_ref, down_ref, up_ref, swap_a, swap_b, force_ref,
                  result_ref, packed_ref, merged_ref, out_ref, sem_ref):
    groups = levels // GROUP
    size = GROUP * SUB
    depths = [tile_at(depth_ref, at) for at in range(4)]

    def copies_of(group):
        for field in range(FIELDS):
            start = pl.multiple_of(field * levels * SUB + group * size, size)
            yield pltpu.make_async_copy(
                out_ref.at[pl.ds(start, size), :], result_ref.at[pl.ds(start, size), :], sem_ref.at[group, field]
            )

    def group_done(group):
        for copy in copies_of(group):
            copy.start()

    inner_step(levels, False, x_ref, None, depths, gain_ref, down_ref, up_ref, swap_a, swap_b,
               out_ref, merged_ref, group_done, force_ref)
    pack_edges(levels, FIELDS, out_ref, packed_ref)
    for group in range(groups):
        for copy in copies_of(group):
            copy.wait()


def edge_change(levels, halo_at, own_at, halo_depth, gain_ref, down_ref, up_ref, surface, change_ref, finish):
    sub = sublane_ids()
    even = sub % 2 == 0
    field = sub // 2
    sign = jnp.where(even, 1.0, -1.0)
    carry_by = jnp.where(field < 2, -QUARTER * sign, 0.0)
    push_by = jnp.where(field == 2, -PUSH * sign, 0.0)
    total = zeros()
    value = zeros()
    for level in range(levels):
        halo = halo_at(level)
        own = own_at(level)
        wet = level < halo_depth
        speed = jnp.where(field == 0, pltpu.roll(own, 4, 0), pltpu.roll(own, 6, 0))
        total = total + (pltpu.roll(halo, 2, 0) - WARMTH * pltpu.roll(halo, 4, 0))
        change = DIFFUSE * (halo - jnp.where(wet, own, 0.0)) + (carry_by * speed) * halo
        change = change + push_by * jnp.where(wet, total, 0.0)
        if level == 0 and surface is not None:
            change = change + surface
        value = change * tile_at(gain_ref, level) + tile_at(down_ref, level) * value
        put_tile(change_ref, level, value)
    following = zeros()
    for level in range(levels - 1, -1, -1):
        following = tile_at(change_ref, level) + tile_at(up_ref, level) * following
        put_tile(change_ref, level, following)
        finish(level, following)


def first_edge_kernel(levels, lon_total, west_in, east_in, east_own, west_own, packed_ref,
                      gain_ref, down_ref, up_ref, parts_ref, *rest):
    others = rest[:lon_total - 3]
    east_ref, west_ref, full_ref, change_ref, force_ref, depth_ref = rest[lon_total - 3:]
    sub = sublane_ids()
    even = sub % 2 == 0
    half = levels // 2
    extra_w = west_in[pl.ds(half * SUB, EXTRA), :]
    extra_e = east_in[pl.ds(half * SUB, EXTRA), :]
    depth_f = jnp.where(even, spread(extra_e[COUNT_ROW:COUNT_ROW + 1]), spread(extra_w[COUNT_ROW:COUNT_ROW + 1]))
    halo_depth = depth_f.astype(jnp.int32)
    depth_ref[...] = halo_depth
    forcing = [zeros()] * FIELDS
    for tile in [parts_ref[0], extra_w, extra_e] + [other[...] for other in others]:
        mine = sub == spread(tile[SLOT_ROW:SLOT_ROW + 1]).astype(jnp.int32)
        for field in range(FIELDS):
            forcing[field] = forcing[field] + jnp.where(mine, spread(tile[field:field + 1]), 0.0)
    surface = zeros()
    rim = jnp.logical_or(sub == 0, sub == SUB - 1)
    for field in range(FIELDS):
        value = SURFACE_GAIN[field] * forcing[field]
        surface = jnp.where(sub == 2 * field, spread(value[SUB - 1:SUB]), surface)
        surface = jnp.where(sub == 2 * field + 1, spread(value[0:1]), surface)
        put_tile(force_ref, field, jnp.where(rim, 0.0, value))
        put_tile(force_ref, FIELDS + field, value)

    def finish(level, change):
        full = tile_at(packed_ref, level) + change
        put_tile(full_ref, level, full)
        if level < half:
            later = tile_at(full_ref, level + half)
            put_tile(east_ref, level, jnp.where(even, full, pltpu.roll(later, 1, 0)))
            put_tile(west_ref, level, jnp.where(even, pltpu.roll(full, SUB - 1, 0), later))

    edge_change(
        levels,
        lambda level: column_tiles(levels, level, east_in, west_in, even),
        lambda level: column_tiles(levels, level, east_own, west_own, even),
        halo_depth, gain_ref, down_ref, up_ref, surface, change_ref, finish,
    )


def merge_kernel(levels, inner_ref, reply_ref, change_ref, force_ref, out_ref, edge_ref):
    sub = sublane_ids()
    pair = ((lane_ids() + 1) % LANE) // 2
    forces = [tile_at(force_ref, field) for field in range(FIELDS)]

    def group_body(group, carry):
        packed = zeros()
        for inner in range(GROUP):
            level = group * GROUP + inner
            reply = tile_at(reply_ref, level)
            change = tile_at(change_ref, level)
            for field in range(FIELDS):
                j = inner * FIELDS + field
                side = pltpu.roll(change, SUB - 1 - 2 * field, 0)
                rim = jnp.logical_or(sub == 0, sub == SUB - 1)
                value = tile_at(inner_ref, field * levels + level) + jnp.where(rim, side, forces[field] * reply)
                put_tile(out_ref, field * levels + level, value)
                packed = jnp.where(pair == j, pltpu.roll(value, 2 * j, 1) if j else value, packed)
        put_tile(edge_ref, group, packed)
        return carry

    lax.fori_loop(0, levels // GROUP, group_body, 0)


def second_edge_kernel(levels, west_in, east_in, full_ref, packed_ref, gain_ref, down_ref, up_ref, depth_ref,
                       inner_ref, result_ref, change_ref, columns, sems):
    del inner_ref
    even = sublane_ids() % 2 == 0

    def finish(level, change):
        columns[level] = tile_at(packed_ref, level) + change

    edge_change(
        levels,
        lambda level: column_tiles(levels, level, east_in, west_in, even),
        lambda level: tile_at(full_ref, level),
        depth_ref[...], gain_ref, down_ref, up_ref, None, change_ref, finish,
    )
    copies = []
    for field in range(FIELDS):
        for side, column in ((0, SUB - 1), (1, 0)):
            copies.append(pltpu.make_async_copy(
                columns.at[:, 2 * field + side, :],
                result_ref.at[pl.ds(field * levels, levels), column, :],
                sems.at[field, side],
            ))
    for copy in copies:
        copy.start()
    for copy in copies:
        copy.wait()


def in_vmem(value):
    return pltpu.with_memory_space_constraint(value, pltpu.VMEM)


def in_hbm(value):
    return pltpu.with_memory_space_constraint(value, pltpu.HBM)


def call(kernel, outs, args, scratch=(), hbm_in=(), hbm_out=(), aliases=None):
    return pl.pallas_call(
        kernel,
        out_shape=[
            (pltpu.HBM if at in hbm_out else pltpu.VMEM)(shape, dtype)
            for at, (shape, dtype) in enumerate(outs)
        ],
        in_specs=[HBM_SPEC if at in hbm_in else VMEM_SPEC for at in range(len(args))],
        out_specs=[HBM_SPEC if at in hbm_out else VMEM_SPEC for at in range(len(outs))],
        scratch_shapes=list(scratch),
        input_output_aliases=aliases or {},
        compiler_params=pltpu.CompilerParams(vmem_limit_bytes=VMEM_BYTES),
    )(*[in_hbm(arg) if at in hbm_in else in_vmem(arg) for at, arg in enumerate(args)])


def ring_shift(value, axis, amount):
    count = lax.axis_size(axis)
    return lax.ppermute(value, axis, [(i, (i + amount) % count) for i in range(count)])


def pair_swap(value, axis, first):
    count = lax.axis_size(axis)
    pairs = []
    for low in range(first, count, 2):
        high = (low + 1) % count
        pairs += [(low, high), (high, low)]
    return lax.ppermute(value, axis, pairs)


def bind(kernel, *head):
    def bound(*refs):
        return kernel(*head, *refs)

    bound.__name__ = kernel.__name__
    return bound


def local(ocean_state, level_count, mix_rate, atmos_flux, remap_weight, remap_target, remap_slot):
    field_total, levels, lon_dev, lat_dev = ocean_state.shape
    lon_total = lax.axis_size("lon")
    rows = field_total * levels
    groups = levels // GROUP
    f32, i32 = jnp.float32, jnp.int32
    state_shape = ((rows * lon_dev, lat_dev), f32)
    message = ((rows, lat_dev), f32)
    long_message = ((rows + EXTRA, lat_dev), f32)
    table = ((levels * lon_dev, lat_dev), f32)
    dma = pltpu.SemaphoreType.DMA
    merged = pltpu.VMEM((groups, SUB, LANE), f32)
    x = in_vmem(ocean_state.reshape(rows * lon_dev, lat_dev))

    east, west, parts, count = call(
        bind(column_kernel, levels, lon_total),
        [long_message, long_message, ((lon_total, SUB, lat_dev), f32), ((lon_dev, lat_dev), i32)],
        (ocean_state.reshape(rows, lon_dev, lat_dev), level_count, atmos_flux[0], remap_weight[0],
         remap_target, remap_slot),
        scratch=[
            pltpu.VMEM((2, rows, lat_dev), f32),
            pltpu.VMEM(atmos_flux.shape[1:], atmos_flux.dtype),
            pltpu.VMEM(remap_weight.shape[1:], remap_weight.dtype),
            pltpu.SMEM(remap_target.shape, i32),
            pltpu.SMEM(remap_slot.shape, i32),
            dma((7,)),
        ],
        hbm_in=range(6),
    )
    from_west = ring_shift(east, "lon", 1)
    from_east = ring_shift(west, "lon", -1)
    (edge,) = call(bind(edge_kernel, levels), [(((groups + 1) * SUB, lat_dev), f32)], (x, count))
    swap_a = pair_swap(edge, LAT_AXES, 0)
    swap_b = pair_swap(edge, LAT_AXES, 1)
    others = [ring_shift(parts[s], "lon", s) for s in range(2, lon_total - 1)]
    gain, down, up, reply, edge_gain, edge_down, edge_up = call(
        bind(factor_kernel, levels), [table] * 7, (mix_rate.reshape(levels * lon_dev, lat_dev), count)
    )
    inner, packed, depths = call(
        bind(first_kernel, levels),
        [state_shape, table, ((4 * SUB, LANE), i32)],
        (x, count, gain, down, up, swap_a, swap_b),
        scratch=[merged],
    )
    east_next, west_next, full, change, force, halo_depth = call(
        bind(first_edge_kernel, levels, lon_total),
        [message, message, table, table, ((2 * FIELDS * SUB, LANE), f32), ((SUB, LANE), i32)],
        (from_west, from_east, east, west, packed, edge_gain, edge_down, edge_up, parts, *others),
    )
    from_west = ring_shift(east_next, "lon", 1)
    from_east = ring_shift(west_next, "lon", -1)
    state, edge = call(
        bind(merge_kernel, levels),
        [state_shape, ((groups * SUB, lat_dev), f32)],
        (inner, reply, change, force),
    )
    swap_a = pair_swap(edge, LAT_AXES, 0)
    swap_b = pair_swap(edge, LAT_AXES, 1)
    result, packed = call(
        bind(second_kernel, levels),
        [state_shape, table],
        (state, depths, gain, down, up, swap_a, swap_b, force),
        scratch=[merged, pltpu.VMEM(*state_shape), dma((groups, FIELDS))],
        hbm_out=(0,),
    )
    (result,) = call(
        bind(second_edge_kernel, levels),
        [((rows, lon_dev, lat_dev), f32)],
        (from_west, from_east, full, packed, edge_gain, edge_down, edge_up, halo_depth,
         result.reshape(rows, lon_dev, lat_dev)),
        scratch=[pltpu.VMEM(*table), pltpu.VMEM((levels, SUB, LANE), f32), dma((FIELDS, 2))],
        hbm_in=(8,), hbm_out=(0,), aliases={8: 0},
    )
    return result.reshape(ocean_state.shape)


def solution(mesh):
    placed = (
        P(None, None, "lon", LAT_AXES),
        P("lon", LAT_AXES),
        P(None, "lon", LAT_AXES),
        P(LAT_AXES, "lon", None, None),
        P(LAT_AXES, "lon", None, None),
        P(LAT_AXES, "lon"),
        P(LAT_AXES, "lon"),
    )

    return jax.shard_map(
        local,
        mesh=mesh,
        in_specs=placed,
        out_specs=P(None, None, "lon", LAT_AXES),
        check_vma=False,
    )
```

time: 36.8 us -> 31.5 us (0.86)
  local copies, waits for them, and re-layouts: 4.97 us -> 0.02 us
  waiting for transfers between devices: 12.3 us -> 8.58 us
  Pallas kernels: 7.22 us -> 10.5 us
    unnamed x16 -> x4, local copies, waits for them, and re-layouts: 4.96 us -> 0.01 us
    ppermute x5, waiting for transfers between devices: 7.26 us -> 3.66 us  [ring_shift(): lax.ppermute(value, axis, [(i, (i + amount) % count) for i in range(count)])]
    pallas_call x5 -> x8, Pallas kernels: 7.22 us -> 10.5 us  [call(): pl.pallas_call(kernel, out_shape=[(pltpu.HBM if at in hbm_out else pltpu....]
  transfers between devices with their start and end apart: 9 -> 9, of which waited for: 5 -> 3; matrix products, arithmetic and copies ran while one was open for 0% -> 0% of each run, Pallas kernels for 2% -> 21%
where the time goes in v3:
time: 31.5 us; the launch traced here: 31.4 us
  starting transfers between devices  12.1 us (38%)
  Pallas kernels  10.5 us (33%)
  waiting for transfers between devices  8.58 us (27%)
    pallas_call x8, Pallas kernels, call(): pl.pallas_call(kernel, out_shape=[(pltpu.HBM if at in hbm_out else pltpu....  10.5 us
    ppermute x5, starting transfers between devices, ring_shift(): lax.ppermute(value, axis, [(i, (i + amount) % count) for i in range(count)])  7.42 us
    ppermute x4, waiting for transfers between devices, pair_swap(): return lax.ppermute(value, axis, pairs)  4.92 us
    ppermute x4, starting transfers between devices, pair_swap(): return lax.ppermute(value, axis, pairs)  4.73 us
    ppermute x5, waiting for transfers between devices, ring_shift(): lax.ppermute(value, axis, [(i, (i + amount) % count) for i in range(count)])  3.66 us
  transfers between devices with their start and end apart: 9, of which 3 were waited for; matrix products, arithmetic and copies ran while one was open for 0% of the time, Pallas kernels for 21%

profile of v3, /device:TPU:0, one launch (start us, length us, event | category | flops | bytes accessed | tf_op | source)
XLA Modules:
  0.0 31.4 jit_solution(3476550628681945994)
XLA Ops:
  0.0 0.0 copy-start
  0.0 0.0 copy-start.1
  0.0 1.6 %shard_map.73 = (f32[328,128]{1,0:T(8,128)S(1)}, f32[328,128]{1,0:T(8,128)S(1)}, f32[4,8,128]{2,1,0:T(8,128)S(1)}, s32[8,128]{1,0:T(8,128)S(1)}) custom-call(f32[320,8,128]{2,1,0:T(8,128)} %bitcast.9, s32[8,128]{1,0:T(8,128)} %refs_1_.1, bf16[4,4,256]{2,1,0:T(4,128)(2,1)} %bitcast.15, bf16[4,256,128]{2,1,0:T(8,128)(2,1)} %bitcast.14, s32[1,4]{1,0:T(1,128)} %refs_4_.1, ...), custom_call_target="tpu_custom_call" | custom-call | tf_op jit(solution)/shard_map/pallas_call | solution.py:461
  1.6 0.0 copy-done
  1.6 0.7 %shard_map.75 = f32[48,128]{1,0:T(8,128)S(1)} custom-call(f32[2560,128]{1,0:T(8,128)S(1)} %bitcast.10, s32[8,128]{1,0:T(8,128)S(1)} %get-tuple-element.31.refs_1_), custom_call_target="tpu_custom_call" | custom-call | tf_op jit(solution)/shard_map/pallas_call | solution.py:461
  2.3 4.6 %collective-permute-start.3 = (f32[48,128]{1,0:T(8,128)S(1)}, f32[48,128]{1,0:T(8,128)S(1)}, u32[]{:S(2)}, u32[]{:S(2)}) collective-permute-start(f32[48,128]{1,0:T(8,128)S(1)} %shard_map.75), channel_id=1, source_target_pairs={{1,2},{2,1},{3,4},{4,3},{5,6},{6,5},{7,0},{0,7},{9,10},{10,9},{11,... | collective-permute-start | bytes 73736 | tf_op jit(solution)/shard_map/ppermute | solution.py:486
  6.9 0.0 collective-permute-start.2
  6.9 1.5 %collective-permute-start = (f32[328,128]{1,0:T(8,128)S(1)}, f32[328,128]{1,0:T(8,128)S(1)}, u32[]{:S(2)}, u32[]{:S(2)}) collective-permute-start(f32[328,128]{1,0:T(8,128)S(1)} %get-tuple-element.29.refs_2_), channel_id=1, source_target_pairs={{0,8},{8,16},{16,24},{24,0},{1,9},{9,17},{17,25},{25,1},{2,10},{10... | collective-permute-start | bytes 503816 | tf_op jit(solution)/shard_map/ppermute | solution.py:477
  8.3 1.4 %collective-permute-start.1 = (f32[328,128]{1,0:T(8,128)S(1)}, f32[328,128]{1,0:T(8,128)S(1)}, u32[]{:S(2)}, u32[]{:S(2)}) collective-permute-start(f32[328,128]{1,0:T(8,128)S(1)} %get-tuple-element.30.refs_3_), channel_id=1, source_target_pairs={{0,24},{8,0},{16,8},{24,16},{1,25},{9,1},{17,9},{25,17},{2,26},{10... | collective-permute-start | bytes 503816 | tf_op jit(solution)/shard_map/ppermute | solution.py:477
  9.8 1.5 %collective-permute-start.4 = (f32[8,128]{1,0:T(8,128)S(1)}, f32[8,128]{1,0:T(8,128)S(1)}, u32[]{:S(2)}, u32[]{:S(2)}) collective-permute-start(f32[8,128]{1,0:T(8,128)S(1)} %slice_bitcast_fusion), channel_id=1, source_target_pairs={{0,16},{8,24},{16,0},{24,8},{1,17},{9,25},{17,1},{25,9},{2,18},{10... | collective-permute-start | bytes 12296 | tf_op jit(solution)/shard_map/ppermute | solution.py:477
  11.3 0.0 copy-done.1
  11.3 1.3 %shard_map.74 = (f32[640,128]{1,0:T(8,128)S(1)}, f32[640,128]{1,0:T(8,128)S(1)}, f32[640,128]{1,0:T(8,128)S(1)}, f32[640,128]{1,0:T(8,128)S(1)}, f32[640,128]{1,...) custom-call(f32[640,128]{1,0:T(8,128)S(1)} %bitcast.12, s32[8,128]{1,0:T(8,128)S(1)} %get-tuple-element.31.refs_1_), custom_call_target="tpu_custom_call" | custom-call | tf_op jit(solution)/shard_map/pallas_call | solution.py:461
  12.6 0.0 collective-permute-done.3.refs_6_
  12.6 0.0 collective-permute-done.2.refs_5_
  12.6 1.8 %shard_map.76 = (f32[2560,128]{1,0:T(8,128)S(1)}, f32[640,128]{1,0:T(8,128)S(1)}, s32[32,128]{1,0:T(8,128)S(1)}) custom-call(f32[2560,128]{1,0:T(8,128)S(1)} %bitcast.11, s32[8,128]{1,0:T(8,128)S(1)} %get-tuple-element.31.refs_1_, f32[640,128]{1,0:T(8,128)S(1)} %get-tuple-element.32.refs_2_, f32[640,128]{1,0:T(8,128)S(1)} %get-tuple-element.33.refs_3_, ...), custom_call_target="tpu_custom_call" | custom-call | tf_op jit(solution)/shard_map/pallas_call | solution.py:461
  14.4 0.0 collective-permute-done.4.refs_9_
  14.5 0.5 %collective-permute-done.refs_0_ = f32[328,128]{1,0:T(8,128)S(1)} collective-permute-done((f32[328,128]{1,0:T(8,128)S(1)}, f32[328,128]{1,0:T(8,128)S(1)}, u32[]{:S(2)}, u32[]{:S(2)}) %collective-permute-start) | collective-permute-done | bytes 167968 | tf_op jit(solution)/shard_map/ppermute | solution.py:477
  14.9 3.2 %collective-permute-done.1.refs_1_ = f32[328,128]{1,0:T(8,128)S(1)} collective-permute-done((f32[328,128]{1,0:T(8,128)S(1)}, f32[328,128]{1,0:T(8,128)S(1)}, u32[]{:S(2)}, u32[]{:S(2)}) %collective-permute-start.1) | collective-permute-done | bytes 167968 | tf_op jit(solution)/shard_map/ppermute | solution.py:477
  18.1 0.5 %shard_map.77 = (f32[320,128]{1,0:T(8,128)S(1)}, f32[320,128]{1,0:T(8,128)S(1)}, f32[640,128]{1,0:T(8,128)S(1)}, f32[640,128]{1,0:T(8,128)S(1)}, f32[64,128]{1,0:T(8,128)S(1)}, /*index=5*/s32[8,128]{1,0:T(8,128)S(1)}) custom-call(f32[328,128]{1,0:T(8,128)S(1)} %collective-permute-done.refs_0_, f32[328,128]{1,0:T(8,128)S(1)} %collective-permute-done.1.refs_1_, ...), custom_call_target="tpu_custom_call" | custom-call | tf_op jit(solution)/shard_map/pallas_call | solution.py:461
  18.6 1.5 %collective-permute-start.5 = (f32[320,128]{1,0:T(8,128)S(1)}, f32[320,128]{1,0:T(8,128)S(1)}, u32[]{:S(2)}, u32[]{:S(2)}) collective-permute-start(f32[320,128]{1,0:T(8,128)S(1)} %get-tuple-element.40), channel_id=1, source_target_pairs={{0,8},{8,16},{16,24},{24,0},{1,9},{9,17},{17,25},{25,1},{2,10},{10... | collective-permute-start | bytes 491528 | tf_op jit(solution)/shard_map/ppermute | solution.py:477
  20.1 1.4 %collective-permute-start.6 = (f32[320,128]{1,0:T(8,128)S(1)}, f32[320,128]{1,0:T(8,128)S(1)}, u32[]{:S(2)}, u32[]{:S(2)}) collective-permute-start(f32[320,128]{1,0:T(8,128)S(1)} %get-tuple-element.41), channel_id=1, source_target_pairs={{0,24},{8,0},{16,8},{24,16},{1,25},{9,1},{17,9},{25,17},{2,26},{10... | collective-permute-start | bytes 491528 | tf_op jit(solution)/shard_map/ppermute | solution.py:477
  21.6 0.7 %shard_map.78 = (f32[2560,128]{1,0:T(8,128)S(1)}, f32[40,128]{1,0:T(8,128)S(1)}) custom-call(f32[2560,128]{1,0:T(8,128)S(1)} %get-tuple-element.43.refs_0_, f32[640,128]{1,0:T(8,128)S(1)} %get-tuple-element.44.refs_1_, f32[640,128]{1,0:T(8,128)S(1)} %get-tuple-element.45.refs_2_, f32[64,128]{1,0:T(8,128)S(1)} %get-tuple-element.46.refs_3_.refs_7_), custom_call_target="tpu_custom_call" | custom-call | tf_op jit(solution)/shard_map/pallas_call | solution.py:461
  22.3 0.1 collective-permute-start.8
  22.3 0.1 collective-permute-start.7
  22.4 4.9 %collective-permute-done.8.refs_6_ = f32[40,128]{1,0:T(8,128)S(1)} collective-permute-done((f32[40,128]{1,0:T(8,128)S(1)}, f32[40,128]{1,0:T(8,128)S(1)}, u32[]{:S(2)}, u32[]{:S(2)}) %collective-permute-start.8) | collective-permute-done | bytes 20512 | tf_op jit(solution)/shard_map/ppermute | solution.py:486
  27.3 0.0 collective-permute-done.7.refs_5_
  27.3 2.8 %shard_map.79 = (f32[2560,128]{1,0:T(8,128)}, f32[640,128]{1,0:T(8,128)S(1)}) custom-call(f32[2560,128]{1,0:T(8,128)S(1)} %get-tuple-element.47.refs_0_, s32[32,128]{1,0:T(8,128)S(1)} %get-tuple-element.48.refs_1_, f32[640,128]{1,0:T(8,128)S(1)} %get-tuple-element.32.refs_2_, f32[640,128]{1,0:T(8,128)S(1)} %get-tuple-element.33.refs_3_, ...), custom_call_target="tpu_custom_call" | custom-call | tf_op jit(solution)/shard_map/pallas_call | solution.py:461
  30.2 0.0 collective-permute-done.5.refs_0_
  30.2 0.0 collective-permute-done.6.refs_1_
  30.2 1.2 %shard_map.80 = f32[320,8,128]{2,1,0:T(8,128)} custom-call(f32[320,128]{1,0:T(8,128)S(1)} %collective-permute-done.5.refs_0_, f32[320,128]{1,0:T(8,128)S(1)} %collective-permute-done.6.refs_1_, f32[640,128]{1,0:T(8,128)S(1)} %get-tuple-element.42.refs_2_, f32[640,128]{1,0:T(8,128)S(1)} %get-tuple-element.50.refs_3_, ...), custom_call_target="tpu_custom_call", output_to_operand_aliasing={{}: (8, {})} | custom-call | tf_op jit(solution)/shard_map/pallas_call | solution.py:461
  (1 shorter events, 0.0 us)
Async XLA Ops:
  0.0 1.6 %copy-start = (f32[4,80,8,128]{3,2,1,0:T(8,128)S(1)}, f32[4,80,8,128]{3,2,1,0:T(8,128)}, u32[]{:S(2)}) copy-start(f32[4,80,8,128]{3,2,1,0:T(8,128)} %param.7) | copy-start | bytes 3932164
  0.0 11.3 %copy-start.1 = (f32[80,8,128]{2,1,0:T(8,128)S(1)}, f32[80,8,128]{2,1,0:T(8,128)}, u32[]{:S(2)}) copy-start(f32[80,8,128]{2,1,0:T(8,128)} %param.9) | copy-start | bytes 983044
  2.3 10.3 %collective-permute-start.3 = (f32[48,128]{1,0:T(8,128)S(1)}, f32[48,128]{1,0:T(8,128)S(1)}, u32[]{:S(2)}, u32[]{:S(2)}) collective-permute-start(f32[48,128]{1,0:T(8,128)S(1)} %shard_map.75), channel_id=1, source_target_pairs={{1,2},{2,1},{3,4},{4,3},{5,6},{6,5},{7,0},{0,7},{9,10},{10,9},{11,... | collective-permute-start | bytes 73736 | tf_op jit(solution)/shard_map/ppermute | solution.py:486
  6.9 5.8 %collective-permute-start.2 = (f32[48,128]{1,0:T(8,128)S(1)}, f32[48,128]{1,0:T(8,128)S(1)}, u32[]{:S(2)}, u32[]{:S(2)}) collective-permute-start(f32[48,128]{1,0:T(8,128)S(1)} %shard_map.75), channel_id=1, source_target_pairs={{0,1},{1,0},{2,3},{3,2},{4,5},{5,4},{6,7},{7,6},{8,9},{9,8},{10,11... | collective-permute-start | bytes 73736 | tf_op jit(solution)/shard_map/ppermute | solution.py:486
  6.9 8.1 %collective-permute-start = (f32[328,128]{1,0:T(8,128)S(1)}, f32[328,128]{1,0:T(8,128)S(1)}, u32[]{:S(2)}, u32[]{:S(2)}) collective-permute-start(f32[328,128]{1,0:T(8,128)S(1)} %get-tuple-element.29.refs_2_), channel_id=1, source_target_pairs={{0,8},{8,16},{16,24},{24,0},{1,9},{9,17},{17,25},{25,1},{2,10},{10... | collective-permute-start | bytes 503816 | tf_op jit(solution)/shard_map/ppermute | solution.py:477
  8.3 9.8 %collective-permute-start.1 = (f32[328,128]{1,0:T(8,128)S(1)}, f32[328,128]{1,0:T(8,128)S(1)}, u32[]{:S(2)}, u32[]{:S(2)}) collective-permute-start(f32[328,128]{1,0:T(8,128)S(1)} %get-tuple-element.30.refs_3_), channel_id=1, source_target_pairs={{0,24},{8,0},{16,8},{24,16},{1,25},{9,1},{17,9},{25,17},{2,26},{10... | collective-permute-start | bytes 503816 | tf_op jit(solution)/shard_map/ppermute | solution.py:477
  9.8 4.7 %collective-permute-start.4 = (f32[8,128]{1,0:T(8,128)S(1)}, f32[8,128]{1,0:T(8,128)S(1)}, u32[]{:S(2)}, u32[]{:S(2)}) collective-permute-start(f32[8,128]{1,0:T(8,128)S(1)} %slice_bitcast_fusion), channel_id=1, source_target_pairs={{0,16},{8,24},{16,0},{24,8},{1,17},{9,25},{17,1},{25,9},{2,18},{10... | collective-permute-start | bytes 12296 | tf_op jit(solution)/shard_map/ppermute | solution.py:477
  18.6 11.6 %collective-permute-start.5 = (f32[320,128]{1,0:T(8,128)S(1)}, f32[320,128]{1,0:T(8,128)S(1)}, u32[]{:S(2)}, u32[]{:S(2)}) collective-permute-start(f32[320,128]{1,0:T(8,128)S(1)} %get-tuple-element.40), channel_id=1, source_target_pairs={{0,8},{8,16},{16,24},{24,0},{1,9},{9,17},{17,25},{25,1},{2,10},{10... | collective-permute-start | bytes 491528 | tf_op jit(solution)/shard_map/ppermute | solution.py:477
  20.1 10.1 %collective-permute-start.6 = (f32[320,128]{1,0:T(8,128)S(1)}, f32[320,128]{1,0:T(8,128)S(1)}, u32[]{:S(2)}, u32[]{:S(2)}) collective-permute-start(f32[320,128]{1,0:T(8,128)S(1)} %get-tuple-element.41), channel_id=1, source_target_pairs={{0,24},{8,0},{16,8},{24,16},{1,25},{9,1},{17,9},{25,17},{2,26},{10... | collective-permute-start | bytes 491528 | tf_op jit(solution)/shard_map/ppermute | solution.py:477
  22.3 5.1 %collective-permute-start.8 = (f32[40,128]{1,0:T(8,128)S(1)}, f32[40,128]{1,0:T(8,128)S(1)}, u32[]{:S(2)}, u32[]{:S(2)}) collective-permute-start(f32[40,128]{1,0:T(8,128)S(1)} %get-tuple-element.49), channel_id=1, source_target_pairs={{1,2},{2,1},{3,4},{4,3},{5,6},{6,5},{7,0},{0,7},{9,10},{10,9},{11,... | collective-permute-start | bytes 61448 | tf_op jit(solution)/shard_map/ppermute | solution.py:486
  22.3 5.0 %collective-permute-start.7 = (f32[40,128]{1,0:T(8,128)S(1)}, f32[40,128]{1,0:T(8,128)S(1)}, u32[]{:S(2)}, u32[]{:S(2)}) collective-permute-start(f32[40,128]{1,0:T(8,128)S(1)} %get-tuple-element.49), channel_id=1, source_target_pairs={{0,1},{1,0},{2,3},{3,2},{4,5},{5,4},{6,7},{7,6},{8,9},{9,8},{10,11... | collective-permute-start | bytes 61448 | tf_op jit(solution)/shard_map/ppermute | solution.py:486

commit v4 on v3

--- a/solution.py
+++ b/solution.py
@@ -81,7 +81,7 @@
 
 
 def column_kernel(levels, lon_total, x_ref, count_hbm, flux_hbm, weight_hbm, target_hbm, slot_hbm,
-                  east_ref, west_ref, parts_ref, count_ref,
+                  rate_hbm, east_ref, west_ref, parts_ref, count_ref, rate_ref,
                   columns, flux_ref, weight_ref, target_ref, slot_ref, sems):
     me = lax.axis_index("lon")
     half = levels // 2
@@ -97,7 +97,8 @@
         pltpu.make_async_copy(x_ref.at[:, SUB - 1, :], columns.at[0], sems.at[0]),
         pltpu.make_async_copy(x_ref.at[:, 0, :], columns.at[1], sems.at[1]),
     ]
-    for copy in sides + copies:
+    later = pltpu.make_async_copy(rate_hbm, rate_ref, sems.at[7])
+    for copy in sides + copies + [later]:
         copy.start()
     for copy in copies:
         copy.wait()
@@ -127,14 +128,17 @@
         out_ref[pl.ds(half * SUB, EXTRA), :] = jnp.where(
             sub == COUNT_ROW, spread(count_f[column:column + 1, :]), parts_ref[shift]
         )
-
-
-def edge_kernel(levels, x_ref, count_ref, edge_ref):
+    later.wait()
+
+
+def prepare_kernel(levels, x_ref, count_ref, rate_ref, edge_ref, gain_ref, down_ref, up_ref, reply_ref,
+                   edge_gain_ref, edge_down_ref, edge_up_ref):
     pair = ((lane_ids() + 1) % LANE) // 2
     count = count_ref[...]
 
     def group_body(group, carry):
         packed = zeros()
+        lower, prev, reply = carry
         for inner in range(GROUP):
             level = group * GROUP + inner
             wet = level < count
@@ -142,34 +146,23 @@
                 j = inner * FIELDS + field
                 value = jnp.where(wet, tile_at(x_ref, field * levels + level), 0.0)
                 packed = jnp.where(pair == j, pltpu.roll(value, 2 * j, 1) if j else value, packed)
+            upper = jnp.where(level + 1 < count, tile_at(rate_ref, level), 0.0)
+            upper = jnp.where(level < levels - 1, upper, 0.0)
+            inverse = 1.0 / (1.0 + upper + lower - lower * prev)
+            prev = upper * inverse
+            gain = jnp.where(wet, inverse, 0.0)
+            down = lower * inverse
+            reply = jnp.where(level == 0, gain, down * reply)
+            put_tile(gain_ref, level, gain)
+            put_tile(down_ref, level, down)
+            put_tile(up_ref, level, prev)
+            put_tile(reply_ref, level, reply)
+            lower = upper
         put_tile(edge_ref, group, packed)
-        return carry
-
-    lax.fori_loop(0, levels // GROUP, group_body, 0)
+        return lower, prev, reply
+
+    lax.fori_loop(0, levels // GROUP, group_body, (zeros(), zeros(), zeros()))
     put_tile(edge_ref, levels // GROUP, count.astype(jnp.float32))
-
-
-def factor_kernel(levels, rate_ref, count_ref, gain_ref, down_ref, up_ref, reply_ref,
-                  edge_gain_ref, edge_down_ref, edge_up_ref):
-    count = count_ref[...]
-
-    def level_body(level, carry):
-        lower, prev, reply = carry
-        upper = jnp.where(level + 1 < count, tile_at(rate_ref, level), 0.0)
-        upper = jnp.where(level < levels - 1, upper, 0.0)
-        pivot = 1.0 + upper + lower - lower * prev
-        inverse = 1.0 / pivot
-        ratio = upper * inverse
-        gain = jnp.where(level < count, inverse, 0.0)
-        down = lower * inverse
-        put_tile(gain_ref, level, gain)
-        put_tile(down_ref, level, down)
-        put_tile(up_ref, level, ratio)
-        reply = jnp.where(level == 0, gain, down * reply)
-        put_tile(reply_ref, level, reply)
-        return upper, ratio, reply
-
-    lax.fori_loop(0, levels, level_body, (zeros(), zeros(), zeros()), unroll=8)
 
     def back_body(step, following):
         level = levels - 1 - step
@@ -177,7 +170,7 @@
         put_tile(reply_ref, level, value)
         return value
 
-    lax.fori_loop(0, levels, back_body, zeros(), unroll=8)
+    lax.fori_loop(0, levels, back_body, zeros(), unroll=16)
     for source_ref, out_ref in ((gain_ref, edge_gain_ref), (down_ref, edge_down_ref), (up_ref, edge_up_ref)):
         pack_edges(levels, 1, source_ref, out_ref)
 
@@ -193,7 +186,7 @@
 
 
 def inner_step(levels, first, x_ref, depth, depths, gain_ref, down_ref, up_ref, swap_a, swap_b,
-               out_ref, merged_ref, group_done, force_ref=None):
+               out_ref, merged_ref, force_ref=None):
     sub = sublane_ids()
     lane = lane_ids()
     even = lane % 2 == 0
@@ -274,7 +267,6 @@
                 put_tile(out_ref, field * levels + level, value)
                 now.append(value)
             following = tuple(now)
-        group_done(group)
         return following
 
     lax.fori_loop(0, groups, backward_group, (zeros(),) * FIELDS)
@@ -298,33 +290,16 @@
         put_tile(depth_ref, at, value)
         depths.append(value)
     inner_step(levels, True, x_ref, depth, depths, gain_ref, down_ref, up_ref, swap_a, swap_b,
-               out_ref, merged_ref, lambda group: None)
+               out_ref, merged_ref)
     pack_edges(levels, FIELDS, out_ref, packed_ref)
 
 
 def second_kernel(levels, x_ref, depth_ref, gain_ref, down_ref, up_ref, swap_a, swap_b, force_ref,
-                  result_ref, packed_ref, merged_ref, out_ref, sem_ref):
-    groups = levels // GROUP
-    size = GROUP * SUB
+                  out_ref, packed_ref, merged_ref):
     depths = [tile_at(depth_ref, at) for at in range(4)]
-
-    def copies_of(group):
-        for field in range(FIELDS):
-            start = pl.multiple_of(field * levels * SUB + group * size, size)
-            yield pltpu.make_async_copy(
-                out_ref.at[pl.ds(start, size), :], result_ref.at[pl.ds(start, size), :], sem_ref.at[group, field]
-            )
-
-    def group_done(group):
-        for copy in copies_of(group):
-            copy.start()
-
     inner_step(levels, False, x_ref, None, depths, gain_ref, down_ref, up_ref, swap_a, swap_b,
-               out_ref, merged_ref, group_done, force_ref)
+               out_ref, merged_ref, force_ref)
     pack_edges(levels, FIELDS, out_ref, packed_ref)
-    for group in range(groups):
-        for copy in copies_of(group):
-            copy.wait()
 
 
 def edge_change(levels, halo_at, own_at, halo_depth, gain_ref, down_ref, up_ref, surface, change_ref, finish):
@@ -422,12 +397,26 @@
 
 
 def second_edge_kernel(levels, west_in, east_in, full_ref, packed_ref, gain_ref, down_ref, up_ref, depth_ref,
-                       inner_ref, result_ref, change_ref, columns, sems):
-    del inner_ref
+                       inner_ref, result_ref, state_ref, change_ref, sems):
     even = sublane_ids() % 2 == 0
+    sub = sublane_ids()
+    copies = []
 
     def finish(level, change):
-        columns[level] = tile_at(packed_ref, level) + change
+        edge = tile_at(packed_ref, level) + change
+        for field in range(FIELDS):
+            side = pltpu.roll(edge, SUB - 1 - 2 * field, 0)
+            rim = jnp.logical_or(sub == 0, sub == SUB - 1)
+            row = field * levels + level
+            put_tile(state_ref, row, jnp.where(rim, side, tile_at(inner_ref, row)))
+        if level % GROUP == 0:
+            for field in range(FIELDS):
+                piece = pl.ds((field * levels + level) * SUB, GROUP * SUB)
+                copy = pltpu.make_async_copy(
+                    state_ref.at[piece, :], result_ref.at[piece, :], sems.at[level // GROUP, field]
+                )
+                copy.start()
+                copies.append(copy)
 
     edge_change(
         levels,
@@ -435,16 +424,6 @@
         lambda level: tile_at(full_ref, level),
         depth_ref[...], gain_ref, down_ref, up_ref, None, change_ref, finish,
     )
-    copies = []
-    for field in range(FIELDS):
-        for side, column in ((0, SUB - 1), (1, 0)):
-            copies.append(pltpu.make_async_copy(
-                columns.at[:, 2 * field + side, :],
-                result_ref.at[pl.ds(field * levels, levels), column, :],
-                sems.at[field, side],
-            ))
-    for copy in copies:
-        copy.start()
     for copy in copies:
         copy.wait()
 
@@ -479,11 +458,17 @@
 
 def pair_swap(value, axis, first):
     count = lax.axis_size(axis)
-    pairs = []
-    for low in range(first, count, 2):
-        high = (low + 1) % count
-        pairs += [(low, high), (high, low)]
+    pairs = [(at, at) for at in range(first)]
+    for low in range(first, count - 1, 2):
+        pairs += [(low, low + 1), (low + 1, low)]
+    pairs += [(at, at) for at in range(len(pairs), count)]
     return lax.ppermute(value, axis, pairs)
+
+
+def lat_exchange(edge):
+    swap_a = pair_swap(edge, LAT_AXES, 0)
+    swap_b = pair_swap(edge, LAT_AXES, 1)
+    return swap_a, swap_b
 
 
 def bind(kernel, *head):
@@ -508,30 +493,30 @@
     merged = pltpu.VMEM((groups, SUB, LANE), f32)
     x = in_vmem(ocean_state.reshape(rows * lon_dev, lat_dev))
 
-    east, west, parts, count = call(
+    east, west, parts, count, rate = call(
         bind(column_kernel, levels, lon_total),
-        [long_message, long_message, ((lon_total, SUB, lat_dev), f32), ((lon_dev, lat_dev), i32)],
+        [long_message, long_message, ((lon_total, SUB, lat_dev), f32), ((lon_dev, lat_dev), i32), table],
         (ocean_state.reshape(rows, lon_dev, lat_dev), level_count, atmos_flux[0], remap_weight[0],
-         remap_target, remap_slot),
+         remap_target, remap_slot, mix_rate.reshape(levels * lon_dev, lat_dev)),
         scratch=[
             pltpu.VMEM((2, rows, lat_dev), f32),
             pltpu.VMEM(atmos_flux.shape[1:], atmos_flux.dtype),
             pltpu.VMEM(remap_weight.shape[1:], remap_weight.dtype),
             pltpu.SMEM(remap_target.shape, i32),
             pltpu.SMEM(remap_slot.shape, i32),
-            dma((7,)),
+            dma((8,)),
         ],
-        hbm_in=range(6),
+        hbm_in=range(7),
     )
     from_west = ring_shift(east, "lon", 1)
     from_east = ring_shift(west, "lon", -1)
-    (edge,) = call(bind(edge_kernel, levels), [(((groups + 1) * SUB, lat_dev), f32)], (x, count))
-    swap_a = pair_swap(edge, LAT_AXES, 0)
-    swap_b = pair_swap(edge, LAT_AXES, 1)
+    edge, gain, down, up, reply, edge_gain, edge_down, edge_up = call(
+        bind(prepare_kernel, levels),
+        [(((groups + 1) * SUB, lat_dev), f32)] + [table] * 7,
+        (x, count, rate),
+    )
+    swap_a, swap_b = lat_exchange(edge)
     others = [ring_shift(parts[s], "lon", s) for s in range(2, lon_total - 1)]
-    gain, down, up, reply, edge_gain, edge_down, edge_up = call(
-        bind(factor_kernel, levels), [table] * 7, (mix_rate.reshape(levels * lon_dev, lat_dev), count)
-    )
     inner, packed, depths = call(
         bind(first_kernel, levels),
         [state_shape, table, ((4 * SUB, LANE), i32)],
@@ -550,22 +535,19 @@
         [state_shape, ((groups * SUB, lat_dev), f32)],
         (inner, reply, change, force),
     )
-    swap_a = pair_swap(edge, LAT_AXES, 0)
-    swap_b = pair_swap(edge, LAT_AXES, 1)
-    result, packed = call(
+    swap_a, swap_b = lat_exchange(edge)
+    inner, packed = call(
         bind(second_kernel, levels),
         [state_shape, table],
         (state, depths, gain, down, up, swap_a, swap_b, force),
-        scratch=[merged, pltpu.VMEM(*state_shape), dma((groups, FIELDS))],
-        hbm_out=(0,),
+        scratch=[merged],
     )
     (result,) = call(
         bind(second_edge_kernel, levels),
-        [((rows, lon_dev, lat_dev), f32)],
-        (from_west, from_east, full, packed, edge_gain, edge_down, edge_up, halo_depth,
-         result.reshape(rows, lon_dev, lat_dev)),
-        scratch=[pltpu.VMEM(*table), pltpu.VMEM((levels, SUB, LANE), f32), dma((FIELDS, 2))],
-        hbm_in=(8,), hbm_out=(0,), aliases={8: 0},
+        [state_shape],
+        (from_west, from_east, full, packed, edge_gain, edge_down, edge_up, halo_depth, inner),
+        scratch=[pltpu.VMEM(*state_shape), pltpu.VMEM(*table), dma((groups, FIELDS))],
+        hbm_out=(0,),
     )
     return result.reshape(ocean_state.shape)
 

time: 31.5 us -> 31.3 us (level)
  starting transfers between devices: 12.1 us -> 16.2 us
  waiting for transfers between devices: 8.58 us -> 5.4 us
  Pallas kernels: 10.5 us -> 9.09 us
    ppermute x4, starting transfers between devices: 4.73 us -> 8.81 us  [pair_swap(): return lax.ppermute(value, axis, pairs)]
    ppermute x4, waiting for transfers between devices: 4.92 us -> 0.85 us  [pair_swap(): return lax.ppermute(value, axis, pairs)]
    pallas_call x8 -> x7, Pallas kernels: 10.5 us -> 9.09 us  [call(): pl.pallas_call(kernel, out_shape=[(pltpu.HBM if at in hbm_out else pltpu....]
    ppermute x5, waiting for transfers between devices: 3.66 us -> 4.55 us  [ring_shift(): lax.ppermute(value, axis, [(i, (i + amount) % count) for i in range(count)])]
  transfers between devices with their start and end apart: 9 -> 9, of which waited for: 3 -> 4; matrix products, arithmetic and copies ran while one was open for 0% -> 0% of each run, Pallas kernels for 21% -> 14%
where the time goes in v4:
time: 31.3 us; the launch traced here: 30.9 us
  starting transfers between devices  16.2 us (52%)
  Pallas kernels  9.09 us (29%)
  waiting for transfers between devices  5.4 us (17%)
    pallas_call x7, Pallas kernels, call(): pl.pallas_call(kernel, out_shape=[(pltpu.HBM if at in hbm_out else pltpu....  9.09 us
    ppermute x4, starting transfers between devices, pair_swap(): return lax.ppermute(value, axis, pairs)  8.81 us
    ppermute x5, starting transfers between devices, ring_shift(): lax.ppermute(value, axis, [(i, (i + amount) % count) for i in range(count)])  7.42 us
    ppermute x5, waiting for transfers between devices, ring_shift(): lax.ppermute(value, axis, [(i, (i + amount) % count) for i in range(count)])  4.55 us
    ppermute x4, waiting for transfers between devices, pair_swap(): return lax.ppermute(value, axis, pairs)  0.85 us
  transfers between devices with their start and end apart: 9, of which 4 were waited for; matrix products, arithmetic and copies ran while one was open for 0% of the time, Pallas kernels for 14%

profile of v4, /device:TPU:0, one launch (start us, length us, event | category | flops | bytes accessed | tf_op | source)
XLA Modules:
  0.0 30.9 jit_solution(812508541955030661)
XLA Ops:
  0.0 0.0 copy-start
  0.0 1.6 %shard_map.73 = (f32[328,128]{1,0:T(8,128)S(1)}, f32[328,128]{1,0:T(8,128)S(1)}, f32[4,8,128]{2,1,0:T(8,128)S(1)}, s32[8,128]{1,0:T(8,128)S(1)}, f32[640,128]{1,0:T(8,128)S(1)}) custom-call(f32[320,8,128]{2,1,0:T(8,128)} %bitcast.8, s32[8,128]{1,0:T(8,128)} %refs_1_.1, bf16[4,4,256]{2,1,0:T(4,128)(2,1)} %bitcast.13, bf16[4,256,128]{2,1,0:T(8,128)(2,1)} %bitcast.12, ...), custom_call_target="tpu_custom_call" | custom-call | tf_op jit(solution)/shard_map/pallas_call | solution.py:440
  1.6 0.1 copy-done
  1.7 1.2 %shard_map.74 = (f32[48,128]{1,0:T(8,128)S(1)}, f32[640,128]{1,0:T(8,128)S(1)}, f32[640,128]{1,0:T(8,128)S(1)}, f32[640,128]{1,0:T(8,128)S(1)}, f32[640,128]{1,0...) custom-call(f32[2560,128]{1,0:T(8,128)S(1)} %bitcast.9, ...), custom_call_target="tpu_custom_call" | custom-call | tf_op jit(solution)/shard_map/pallas_call | solution.py:440
  2.9 0.7 %collective-permute-start.3 = (f32[48,128]{1,0:T(8,128)S(1)}, f32[48,128]{1,0:T(8,128)S(1)}, u32[]{:S(2)}, u32[]{:S(2)}) collective-permute-start(f32[48,128]{1,0:T(8,128)S(1)} %get-tuple-element.38), channel_id=1, source_target_pairs={{0,0},{1,2},{2,1},{3,4},{4,3},{5,6},{6,5},{7,7},{8,8},{9,10},{10,9... | collective-permute-start | bytes 73736 | tf_op jit(solution)/shard_map/ppermute | solution.py:465
  3.6 4.5 %collective-permute-start.2 = (f32[48,128]{1,0:T(8,128)S(1)}, f32[48,128]{1,0:T(8,128)S(1)}, u32[]{:S(2)}, u32[]{:S(2)}) collective-permute-start(f32[48,128]{1,0:T(8,128)S(1)} %get-tuple-element.38), channel_id=1, source_target_pairs={{0,1},{1,0},{2,3},{3,2},{4,5},{5,4},{6,7},{7,6},{8,9},{9,8},{10,11... | collective-permute-start | bytes 73736 | tf_op jit(solution)/shard_map/ppermute | solution.py:465
  8.1 1.5 %collective-permute-start = (f32[328,128]{1,0:T(8,128)S(1)}, f32[328,128]{1,0:T(8,128)S(1)}, u32[]{:S(2)}, u32[]{:S(2)}) collective-permute-start(f32[328,128]{1,0:T(8,128)S(1)} %get-tuple-element.31.refs_2_), channel_id=1, source_target_pairs={{0,8},{8,16},{16,24},{24,0},{1,9},{9,17},{17,25},{25,1},{2,10},{10... | collective-permute-start | bytes 503816 | tf_op jit(solution)/shard_map/ppermute | solution.py:456
  9.6 1.4 %collective-permute-start.1 = (f32[328,128]{1,0:T(8,128)S(1)}, f32[328,128]{1,0:T(8,128)S(1)}, u32[]{:S(2)}, u32[]{:S(2)}) collective-permute-start(f32[328,128]{1,0:T(8,128)S(1)} %get-tuple-element.32.refs_3_), channel_id=1, source_target_pairs={{0,24},{8,0},{16,8},{24,16},{1,25},{9,1},{17,9},{25,17},{2,26},{10... | collective-permute-start | bytes 503816 | tf_op jit(solution)/shard_map/ppermute | solution.py:456
  11.0 1.5 %collective-permute-start.4 = (f32[8,128]{1,0:T(8,128)S(1)}, f32[8,128]{1,0:T(8,128)S(1)}, u32[]{:S(2)}, u32[]{:S(2)}) collective-permute-start(f32[8,128]{1,0:T(8,128)S(1)} %slice_bitcast_fusion), channel_id=1, source_target_pairs={{0,16},{8,24},{16,0},{24,8},{1,17},{9,25},{17,1},{25,9},{2,18},{10... | collective-permute-start | bytes 12296 | tf_op jit(solution)/shard_map/ppermute | solution.py:456
  12.5 0.0 collective-permute-done.3.refs_6_
  12.5 0.0 collective-permute-done.2.refs_5_
  12.5 1.8 %shard_map.75 = (f32[2560,128]{1,0:T(8,128)S(1)}, f32[640,128]{1,0:T(8,128)S(1)}, s32[32,128]{1,0:T(8,128)S(1)}) custom-call(f32[2560,128]{1,0:T(8,128)S(1)} %bitcast.10, s32[8,128]{1,0:T(8,128)S(1)} %get-tuple-element.33.refs_1_, f32[640,128]{1,0:T(8,128)S(1)} %get-tuple-element.35.refs_2_, f32[640,128]{1,0:T(8,128)S(1)} %get-tuple-element.36.refs_3_, ...), custom_call_target="tpu_custom_call" | custom-call | tf_op jit(solution)/shard_map/pallas_call | solution.py:440
  14.3 0.3 collective-permute-done.4.refs_9_
  14.6 1.5 %collective-permute-done.refs_0_ = f32[328,128]{1,0:T(8,128)S(1)} collective-permute-done((f32[328,128]{1,0:T(8,128)S(1)}, f32[328,128]{1,0:T(8,128)S(1)}, u32[]{:S(2)}, u32[]{:S(2)}) %collective-permute-start) | collective-permute-done | bytes 167968 | tf_op jit(solution)/shard_map/ppermute | solution.py:456
  16.1 2.8 %collective-permute-done.1.refs_1_ = f32[328,128]{1,0:T(8,128)S(1)} collective-permute-done((f32[328,128]{1,0:T(8,128)S(1)}, f32[328,128]{1,0:T(8,128)S(1)}, u32[]{:S(2)}, u32[]{:S(2)}) %collective-permute-start.1) | collective-permute-done | bytes 167968 | tf_op jit(solution)/shard_map/ppermute | solution.py:456
  18.9 0.5 %shard_map.76 = (f32[320,128]{1,0:T(8,128)S(1)}, f32[320,128]{1,0:T(8,128)S(1)}, f32[640,128]{1,0:T(8,128)S(1)}, f32[640,128]{1,0:T(8,128)S(1)}, f32[64,128]{1,0:T(8,128)S(1)}, /*index=5*/s32[8,128]{1,0:T(8,128)S(1)}) custom-call(f32[328,128]{1,0:T(8,128)S(1)} %collective-permute-done.refs_0_, f32[328,128]{1,0:T(8,128)S(1)} %collective-permute-done.1.refs_1_, ...), custom_call_target="tpu_custom_call" | custom-call | tf_op jit(solution)/shard_map/pallas_call | solution.py:440
  19.4 1.5 %collective-permute-start.5 = (f32[320,128]{1,0:T(8,128)S(1)}, f32[320,128]{1,0:T(8,128)S(1)}, u32[]{:S(2)}, u32[]{:S(2)}) collective-permute-start(f32[320,128]{1,0:T(8,128)S(1)} %get-tuple-element.44), channel_id=1, source_target_pairs={{0,8},{8,16},{16,24},{24,0},{1,9},{9,17},{17,25},{25,1},{2,10},{10... | collective-permute-start | bytes 491528 | tf_op jit(solution)/shard_map/ppermute | solution.py:456
  20.9 1.4 %collective-permute-start.6 = (f32[320,128]{1,0:T(8,128)S(1)}, f32[320,128]{1,0:T(8,128)S(1)}, u32[]{:S(2)}, u32[]{:S(2)}) collective-permute-start(f32[320,128]{1,0:T(8,128)S(1)} %get-tuple-element.45), channel_id=1, source_target_pairs={{0,24},{8,0},{16,8},{24,16},{1,25},{9,1},{17,9},{25,17},{2,26},{10... | collective-permute-start | bytes 491528 | tf_op jit(solution)/shard_map/ppermute | solution.py:456
  22.3 0.7 %shard_map.77 = (f32[2560,128]{1,0:T(8,128)S(1)}, f32[40,128]{1,0:T(8,128)S(1)}) custom-call(f32[2560,128]{1,0:T(8,128)S(1)} %get-tuple-element.47.refs_0_, f32[640,128]{1,0:T(8,128)S(1)} %get-tuple-element.48.refs_1_, f32[640,128]{1,0:T(8,128)S(1)} %get-tuple-element.49.refs_2_, f32[64,128]{1,0:T(8,128)S(1)} %get-tuple-element.50.refs_3_.refs_7_), custom_call_target="tpu_custom_call" | custom-call | tf_op jit(solution)/shard_map/pallas_call | solution.py:440
  23.0 0.7 %collective-permute-start.8 = (f32[40,128]{1,0:T(8,128)S(1)}, f32[40,128]{1,0:T(8,128)S(1)}, u32[]{:S(2)}, u32[]{:S(2)}) collective-permute-start(f32[40,128]{1,0:T(8,128)S(1)} %get-tuple-element.53), channel_id=1, source_target_pairs={{0,0},{1,2},{2,1},{3,4},{4,3},{5,6},{6,5},{7,7},{8,8},{9,10},{10,9... | collective-permute-start | bytes 61448 | tf_op jit(solution)/shard_map/ppermute | solution.py:465
  23.7 3.0 %collective-permute-start.7 = (f32[40,128]{1,0:T(8,128)S(1)}, f32[40,128]{1,0:T(8,128)S(1)}, u32[]{:S(2)}, u32[]{:S(2)}) collective-permute-start(f32[40,128]{1,0:T(8,128)S(1)} %get-tuple-element.53), channel_id=1, source_target_pairs={{0,1},{1,0},{2,3},{3,2},{4,5},{5,4},{6,7},{7,6},{8,9},{9,8},{10,11... | collective-permute-start | bytes 61448 | tf_op jit(solution)/shard_map/ppermute | solution.py:465
  26.7 0.0 collective-permute-done.8.refs_6_
  26.7 0.8 %collective-permute-done.7.refs_5_ = f32[40,128]{1,0:T(8,128)S(1)} collective-permute-done((f32[40,128]{1,0:T(8,128)S(1)}, f32[40,128]{1,0:T(8,128)S(1)}, u32[]{:S(2)}, u32[]{:S(2)}) %collective-permute-start.7) | collective-permute-done | bytes 20512 | tf_op jit(solution)/shard_map/ppermute | solution.py:465
  27.6 1.8 %shard_map.78 = (f32[2560,128]{1,0:T(8,128)S(1)}, f32[640,128]{1,0:T(8,128)S(1)}) custom-call(f32[2560,128]{1,0:T(8,128)S(1)} %get-tuple-element.51.refs_0_, s32[32,128]{1,0:T(8,128)S(1)} %get-tuple-element.52.refs_1_, f32[640,128]{1,0:T(8,128)S(1)} %get-tuple-element.35.refs_2_, f32[640,128]{1,0:T(8,128)S(1)} %get-tuple-element.36.refs_3_, ...), custom_call_target="tpu_custom_call" | custom-call | tf_op jit(solution)/shard_map/pallas_call | solution.py:440
  29.4 0.0 collective-permute-done.5.refs_0_
  29.4 0.0 collective-permute-done.6.refs_1_
  29.4 1.5 %shard_map.79 = f32[2560,128]{1,0:T(8,128)} custom-call(f32[320,128]{1,0:T(8,128)S(1)} %collective-permute-done.5.refs_0_, f32[320,128]{1,0:T(8,128)S(1)} %collective-permute-done.6.refs_1_, f32[640,128]{1,0:T(8,128)S(1)} %get-tuple-element.46.refs_2_, f32[640,128]{1,0:T(8,128)S(1)} %get-tuple-element.54.refs_3_, ...), custom_call_target="tpu_custom_call" | custom-call | tf_op jit(solution)/shard_map/pallas_call | solution.py:440
  (1 shorter events, 0.0 us)
Async XLA Ops:
  0.0 1.7 %copy-start = (f32[4,80,8,128]{3,2,1,0:T(8,128)S(1)}, f32[4,80,8,128]{3,2,1,0:T(8,128)}, u32[]{:S(2)}) copy-start(f32[4,80,8,128]{3,2,1,0:T(8,128)} %param.7) | copy-start | bytes 3932164
  2.9 9.6 %collective-permute-start.3 = (f32[48,128]{1,0:T(8,128)S(1)}, f32[48,128]{1,0:T(8,128)S(1)}, u32[]{:S(2)}, u32[]{:S(2)}) collective-permute-start(f32[48,128]{1,0:T(8,128)S(1)} %get-tuple-element.38), channel_id=1, source_target_pairs={{0,0},{1,2},{2,1},{3,4},{4,3},{5,6},{6,5},{7,7},{8,8},{9,10},{10,9... | collective-permute-start | bytes 73736 | tf_op jit(solution)/shard_map/ppermute | solution.py:465
  3.6 8.9 %collective-permute-start.2 = (f32[48,128]{1,0:T(8,128)S(1)}, f32[48,128]{1,0:T(8,128)S(1)}, u32[]{:S(2)}, u32[]{:S(2)}) collective-permute-start(f32[48,128]{1,0:T(8,128)S(1)} %get-tuple-element.38), channel_id=1, source_target_pairs={{0,1},{1,0},{2,3},{3,2},{4,5},{5,4},{6,7},{7,6},{8,9},{9,8},{10,11... | collective-permute-start | bytes 73736 | tf_op jit(solution)/shard_map/ppermute | solution.py:465
  8.1 8.1 %collective-permute-start = (f32[328,128]{1,0:T(8,128)S(1)}, f32[328,128]{1,0:T(8,128)S(1)}, u32[]{:S(2)}, u32[]{:S(2)}) collective-permute-start(f32[328,128]{1,0:T(8,128)S(1)} %get-tuple-element.31.refs_2_), channel_id=1, source_target_pairs={{0,8},{8,16},{16,24},{24,0},{1,9},{9,17},{17,25},{25,1},{2,10},{10... | collective-permute-start | bytes 503816 | tf_op jit(solution)/shard_map/ppermute | solution.py:456
  9.6 9.3 %collective-permute-start.1 = (f32[328,128]{1,0:T(8,128)S(1)}, f32[328,128]{1,0:T(8,128)S(1)}, u32[]{:S(2)}, u32[]{:S(2)}) collective-permute-start(f32[328,128]{1,0:T(8,128)S(1)} %get-tuple-element.32.refs_3_), channel_id=1, source_target_pairs={{0,24},{8,0},{16,8},{24,16},{1,25},{9,1},{17,9},{25,17},{2,26},{10... | collective-permute-start | bytes 503816 | tf_op jit(solution)/shard_map/ppermute | solution.py:456
  11.0 3.6 %collective-permute-start.4 = (f32[8,128]{1,0:T(8,128)S(1)}, f32[8,128]{1,0:T(8,128)S(1)}, u32[]{:S(2)}, u32[]{:S(2)}) collective-permute-start(f32[8,128]{1,0:T(8,128)S(1)} %slice_bitcast_fusion), channel_id=1, source_target_pairs={{0,16},{8,24},{16,0},{24,8},{1,17},{9,25},{17,1},{25,9},{2,18},{10... | collective-permute-start | bytes 12296 | tf_op jit(solution)/shard_map/ppermute | solution.py:456
  19.4 10.0 %collective-permute-start.5 = (f32[320,128]{1,0:T(8,128)S(1)}, f32[320,128]{1,0:T(8,128)S(1)}, u32[]{:S(2)}, u32[]{:S(2)}) collective-permute-start(f32[320,128]{1,0:T(8,128)S(1)} %get-tuple-element.44), channel_id=1, source_target_pairs={{0,8},{8,16},{16,24},{24,0},{1,9},{9,17},{17,25},{25,1},{2,10},{10... | collective-permute-start | bytes 491528 | tf_op jit(solution)/shard_map/ppermute | solution.py:456
  20.9 8.5 %collective-permute-start.6 = (f32[320,128]{1,0:T(8,128)S(1)}, f32[320,128]{1,0:T(8,128)S(1)}, u32[]{:S(2)}, u32[]{:S(2)}) collective-permute-start(f32[320,128]{1,0:T(8,128)S(1)} %get-tuple-element.45), channel_id=1, source_target_pairs={{0,24},{8,0},{16,8},{24,16},{1,25},{9,1},{17,9},{25,17},{2,26},{10... | collective-permute-start | bytes 491528 | tf_op jit(solution)/shard_map/ppermute | solution.py:456
  23.0 3.7 %collective-permute-start.8 = (f32[40,128]{1,0:T(8,128)S(1)}, f32[40,128]{1,0:T(8,128)S(1)}, u32[]{:S(2)}, u32[]{:S(2)}) collective-permute-start(f32[40,128]{1,0:T(8,128)S(1)} %get-tuple-element.53), channel_id=1, source_target_pairs={{0,0},{1,2},{2,1},{3,4},{4,3},{5,6},{6,5},{7,7},{8,8},{9,10},{10,9... | collective-permute-start | bytes 61448 | tf_op jit(solution)/shard_map/ppermute | solution.py:465
  23.7 3.8 %collective-permute-start.7 = (f32[40,128]{1,0:T(8,128)S(1)}, f32[40,128]{1,0:T(8,128)S(1)}, u32[]{:S(2)}, u32[]{:S(2)}) collective-permute-start(f32[40,128]{1,0:T(8,128)S(1)} %get-tuple-element.53), channel_id=1, source_target_pairs={{0,1},{1,0},{2,3},{3,2},{4,5},{5,4},{6,7},{7,6},{8,9},{9,8},{10,11... | collective-permute-start | bytes 61448 | tf_op jit(solution)/shard_map/ppermute | solution.py:465

commit v5 on v4

--- a/solution.py
+++ b/solution.py
@@ -458,10 +458,10 @@
 
 def pair_swap(value, axis, first):
     count = lax.axis_size(axis)
-    pairs = [(at, at) for at in range(first)]
-    for low in range(first, count - 1, 2):
-        pairs += [(low, low + 1), (low + 1, low)]
-    pairs += [(at, at) for at in range(len(pairs), count)]
+    pairs = []
+    for low in range(first, count, 2):
+        high = (low + 1) % count
+        pairs += [(low, high), (high, low)]
     return lax.ppermute(value, axis, pairs)
 
 

time: 31.3 us -> 31.5 us (level)
  waiting for transfers between devices: 5.4 us -> 9.91 us
  starting transfers between devices: 16.2 us -> 12.1 us
    ppermute x4, starting transfers between devices: 8.81 us -> 4.73 us  [pair_swap(): return lax.ppermute(value, axis, pairs)]
    ppermute x4, waiting for transfers between devices: 0.85 us -> 4.92 us  [pair_swap(): return lax.ppermute(value, axis, pairs)]
    ppermute x5, waiting for transfers between devices: 4.55 us -> 4.99 us  [ring_shift(): lax.ppermute(value, axis, [(i, (i + amount) % count) for i in range(count)])]
where the time goes in v5:
time: 31.5 us; the launch traced here: 31.3 us
  starting transfers between devices  12.1 us (38%)
  waiting for transfers between devices  9.91 us (31%)
  Pallas kernels  9.09 us (29%)
    pallas_call x7, Pallas kernels, call(): pl.pallas_call(kernel, out_shape=[(pltpu.HBM if at in hbm_out else pltpu....  9.09 us
    ppermute x5, starting transfers between devices, ring_shift(): lax.ppermute(value, axis, [(i, (i + amount) % count) for i in range(count)])  7.42 us
    ppermute x5, waiting for transfers between devices, ring_shift(): lax.ppermute(value, axis, [(i, (i + amount) % count) for i in range(count)])  4.99 us
    ppermute x4, waiting for transfers between devices, pair_swap(): return lax.ppermute(value, axis, pairs)  4.92 us
    ppermute x4, starting transfers between devices, pair_swap(): return lax.ppermute(value, axis, pairs)  4.73 us
  transfers between devices with their start and end apart: 9, of which 4 were waited for; matrix products, arithmetic and copies ran while one was open for 0% of the time, Pallas kernels for 14%

profile of v5, /device:TPU:0, one launch (start us, length us, event | category | flops | bytes accessed | tf_op | source)
XLA Modules:
  0.0 31.3 jit_solution(5341019370297642235)
XLA Ops:
  0.0 0.0 copy-start
  0.0 1.6 %shard_map.73 = (f32[328,128]{1,0:T(8,128)S(1)}, f32[328,128]{1,0:T(8,128)S(1)}, f32[4,8,128]{2,1,0:T(8,128)S(1)}, s32[8,128]{1,0:T(8,128)S(1)}, f32[640,128]{1,0:T(8,128)S(1)}) custom-call(f32[320,8,128]{2,1,0:T(8,128)} %bitcast.8, s32[8,128]{1,0:T(8,128)} %refs_1_.1, bf16[4,4,256]{2,1,0:T(4,128)(2,1)} %bitcast.13, bf16[4,256,128]{2,1,0:T(8,128)(2,1)} %bitcast.12, ...), custom_call_target="tpu_custom_call" | custom-call | tf_op jit(solution)/shard_map/pallas_call | solution.py:440
  1.6 0.1 copy-done
  1.7 1.2 %shard_map.74 = (f32[48,128]{1,0:T(8,128)S(1)}, f32[640,128]{1,0:T(8,128)S(1)}, f32[640,128]{1,0:T(8,128)S(1)}, f32[640,128]{1,0:T(8,128)S(1)}, f32[640,128]{1,0...) custom-call(f32[2560,128]{1,0:T(8,128)S(1)} %bitcast.9, ...), custom_call_target="tpu_custom_call" | custom-call | tf_op jit(solution)/shard_map/pallas_call | solution.py:440
  2.9 4.6 %collective-permute-start.3 = (f32[48,128]{1,0:T(8,128)S(1)}, f32[48,128]{1,0:T(8,128)S(1)}, u32[]{:S(2)}, u32[]{:S(2)}) collective-permute-start(f32[48,128]{1,0:T(8,128)S(1)} %get-tuple-element.38), channel_id=1, source_target_pairs={{1,2},{2,1},{3,4},{4,3},{5,6},{6,5},{7,0},{0,7},{9,10},{10,9},{11,... | collective-permute-start | bytes 73736 | tf_op jit(solution)/shard_map/ppermute | solution.py:465
  7.5 0.0 collective-permute-start.2
  7.5 1.5 %collective-permute-start = (f32[328,128]{1,0:T(8,128)S(1)}, f32[328,128]{1,0:T(8,128)S(1)}, u32[]{:S(2)}, u32[]{:S(2)}) collective-permute-start(f32[328,128]{1,0:T(8,128)S(1)} %get-tuple-element.31.refs_2_), channel_id=1, source_target_pairs={{0,8},{8,16},{16,24},{24,0},{1,9},{9,17},{17,25},{25,1},{2,10},{10... | collective-permute-start | bytes 503816 | tf_op jit(solution)/shard_map/ppermute | solution.py:456
  9.0 1.4 %collective-permute-start.1 = (f32[328,128]{1,0:T(8,128)S(1)}, f32[328,128]{1,0:T(8,128)S(1)}, u32[]{:S(2)}, u32[]{:S(2)}) collective-permute-start(f32[328,128]{1,0:T(8,128)S(1)} %get-tuple-element.32.refs_3_), channel_id=1, source_target_pairs={{0,24},{8,0},{16,8},{24,16},{1,25},{9,1},{17,9},{25,17},{2,26},{10... | collective-permute-start | bytes 503816 | tf_op jit(solution)/shard_map/ppermute | solution.py:456
  10.4 1.5 %collective-permute-start.4 = (f32[8,128]{1,0:T(8,128)S(1)}, f32[8,128]{1,0:T(8,128)S(1)}, u32[]{:S(2)}, u32[]{:S(2)}) collective-permute-start(f32[8,128]{1,0:T(8,128)S(1)} %slice_bitcast_fusion), channel_id=1, source_target_pairs={{0,16},{8,24},{16,0},{24,8},{1,17},{9,25},{17,1},{25,9},{2,18},{10... | collective-permute-start | bytes 12296 | tf_op jit(solution)/shard_map/ppermute | solution.py:456
  12.0 0.0 collective-permute-done.3.refs_6_
  12.0 0.0 collective-permute-done.2.refs_5_
  12.0 1.8 %shard_map.75 = (f32[2560,128]{1,0:T(8,128)S(1)}, f32[640,128]{1,0:T(8,128)S(1)}, s32[32,128]{1,0:T(8,128)S(1)}) custom-call(f32[2560,128]{1,0:T(8,128)S(1)} %bitcast.10, s32[8,128]{1,0:T(8,128)S(1)} %get-tuple-element.33.refs_1_, f32[640,128]{1,0:T(8,128)S(1)} %get-tuple-element.35.refs_2_, f32[640,128]{1,0:T(8,128)S(1)} %get-tuple-element.36.refs_3_, ...), custom_call_target="tpu_custom_call" | custom-call | tf_op jit(solution)/shard_map/pallas_call | solution.py:440
  13.8 0.6 %collective-permute-done.4.refs_9_ = f32[8,128]{1,0:T(8,128)S(1)} collective-permute-done((f32[8,128]{1,0:T(8,128)S(1)}, f32[8,128]{1,0:T(8,128)S(1)}, u32[]{:S(2)}, u32[]{:S(2)}) %collective-permute-start.4) | collective-permute-done | bytes 4128 | tf_op jit(solution)/shard_map/ppermute | solution.py:456
  14.4 1.2 %collective-permute-done.refs_0_ = f32[328,128]{1,0:T(8,128)S(1)} collective-permute-done((f32[328,128]{1,0:T(8,128)S(1)}, f32[328,128]{1,0:T(8,128)S(1)}, u32[]{:S(2)}, u32[]{:S(2)}) %collective-permute-start) | collective-permute-done | bytes 167968 | tf_op jit(solution)/shard_map/ppermute | solution.py:456
  15.6 3.2 %collective-permute-done.1.refs_1_ = f32[328,128]{1,0:T(8,128)S(1)} collective-permute-done((f32[328,128]{1,0:T(8,128)S(1)}, f32[328,128]{1,0:T(8,128)S(1)}, u32[]{:S(2)}, u32[]{:S(2)}) %collective-permute-start.1) | collective-permute-done | bytes 167968 | tf_op jit(solution)/shard_map/ppermute | solution.py:456
  18.8 0.5 %shard_map.76 = (f32[320,128]{1,0:T(8,128)S(1)}, f32[320,128]{1,0:T(8,128)S(1)}, f32[640,128]{1,0:T(8,128)S(1)}, f32[640,128]{1,0:T(8,128)S(1)}, f32[64,128]{1,0:T(8,128)S(1)}, /*index=5*/s32[8,128]{1,0:T(8,128)S(1)}) custom-call(f32[328,128]{1,0:T(8,128)S(1)} %collective-permute-done.refs_0_, f32[328,128]{1,0:T(8,128)S(1)} %collective-permute-done.1.refs_1_, ...), custom_call_target="tpu_custom_call" | custom-call | tf_op jit(solution)/shard_map/pallas_call | solution.py:440
  19.2 1.5 %collective-permute-start.5 = (f32[320,128]{1,0:T(8,128)S(1)}, f32[320,128]{1,0:T(8,128)S(1)}, u32[]{:S(2)}, u32[]{:S(2)}) collective-permute-start(f32[320,128]{1,0:T(8,128)S(1)} %get-tuple-element.44), channel_id=1, source_target_pairs={{0,8},{8,16},{16,24},{24,0},{1,9},{9,17},{17,25},{25,1},{2,10},{10... | collective-permute-start | bytes 491528 | tf_op jit(solution)/shard_map/ppermute | solution.py:456
  20.8 1.4 %collective-permute-start.6 = (f32[320,128]{1,0:T(8,128)S(1)}, f32[320,128]{1,0:T(8,128)S(1)}, u32[]{:S(2)}, u32[]{:S(2)}) collective-permute-start(f32[320,128]{1,0:T(8,128)S(1)} %get-tuple-element.45), channel_id=1, source_target_pairs={{0,24},{8,0},{16,8},{24,16},{1,25},{9,1},{17,9},{25,17},{2,26},{10... | collective-permute-start | bytes 491528 | tf_op jit(solution)/shard_map/ppermute | solution.py:456
  22.2 0.7 %shard_map.77 = (f32[2560,128]{1,0:T(8,128)S(1)}, f32[40,128]{1,0:T(8,128)S(1)}) custom-call(f32[2560,128]{1,0:T(8,128)S(1)} %get-tuple-element.47.refs_0_, f32[640,128]{1,0:T(8,128)S(1)} %get-tuple-element.48.refs_1_, f32[640,128]{1,0:T(8,128)S(1)} %get-tuple-element.49.refs_2_, f32[64,128]{1,0:T(8,128)S(1)} %get-tuple-element.50.refs_3_.refs_7_), custom_call_target="tpu_custom_call" | custom-call | tf_op jit(solution)/shard_map/pallas_call | solution.py:440
  22.9 0.1 collective-permute-start.8
  23.0 0.1 collective-permute-start.7
  23.1 4.9 %collective-permute-done.8.refs_6_ = f32[40,128]{1,0:T(8,128)S(1)} collective-permute-done((f32[40,128]{1,0:T(8,128)S(1)}, f32[40,128]{1,0:T(8,128)S(1)}, u32[]{:S(2)}, u32[]{:S(2)}) %collective-permute-start.8) | collective-permute-done | bytes 20512 | tf_op jit(solution)/shard_map/ppermute | solution.py:465
  28.0 0.0 collective-permute-done.7.refs_5_
  28.0 1.8 %shard_map.78 = (f32[2560,128]{1,0:T(8,128)S(1)}, f32[640,128]{1,0:T(8,128)S(1)}) custom-call(f32[2560,128]{1,0:T(8,128)S(1)} %get-tuple-element.51.refs_0_, s32[32,128]{1,0:T(8,128)S(1)} %get-tuple-element.52.refs_1_, f32[640,128]{1,0:T(8,128)S(1)} %get-tuple-element.35.refs_2_, f32[640,128]{1,0:T(8,128)S(1)} %get-tuple-element.36.refs_3_, ...), custom_call_target="tpu_custom_call" | custom-call | tf_op jit(solution)/shard_map/pallas_call | solution.py:440
  29.8 0.0 collective-permute-done.5.refs_0_
  29.8 0.0 collective-permute-done.6.refs_1_
  29.8 1.5 %shard_map.79 = f32[2560,128]{1,0:T(8,128)} custom-call(f32[320,128]{1,0:T(8,128)S(1)} %collective-permute-done.5.refs_0_, f32[320,128]{1,0:T(8,128)S(1)} %collective-permute-done.6.refs_1_, f32[640,128]{1,0:T(8,128)S(1)} %get-tuple-element.46.refs_2_, f32[640,128]{1,0:T(8,128)S(1)} %get-tuple-element.54.refs_3_, ...), custom_call_target="tpu_custom_call" | custom-call | tf_op jit(solution)/shard_map/pallas_call | solution.py:440
  (1 shorter events, 0.0 us)
Async XLA Ops:
  0.0 1.7 %copy-start = (f32[4,80,8,128]{3,2,1,0:T(8,128)S(1)}, f32[4,80,8,128]{3,2,1,0:T(8,128)}, u32[]{:S(2)}) copy-start(f32[4,80,8,128]{3,2,1,0:T(8,128)} %param.7) | copy-start | bytes 3932164
  2.9 9.0 %collective-permute-start.3 = (f32[48,128]{1,0:T(8,128)S(1)}, f32[48,128]{1,0:T(8,128)S(1)}, u32[]{:S(2)}, u32[]{:S(2)}) collective-permute-start(f32[48,128]{1,0:T(8,128)S(1)} %get-tuple-element.38), channel_id=1, source_target_pairs={{1,2},{2,1},{3,4},{4,3},{5,6},{6,5},{7,0},{0,7},{9,10},{10,9},{11,... | collective-permute-start | bytes 73736 | tf_op jit(solution)/shard_map/ppermute | solution.py:465
  7.5 4.5 %collective-permute-start.2 = (f32[48,128]{1,0:T(8,128)S(1)}, f32[48,128]{1,0:T(8,128)S(1)}, u32[]{:S(2)}, u32[]{:S(2)}) collective-permute-start(f32[48,128]{1,0:T(8,128)S(1)} %get-tuple-element.38), channel_id=1, source_target_pairs={{0,1},{1,0},{2,3},{3,2},{4,5},{5,4},{6,7},{7,6},{8,9},{9,8},{10,11... | collective-permute-start | bytes 73736 | tf_op jit(solution)/shard_map/ppermute | solution.py:465
  7.5 8.1 %collective-permute-start = (f32[328,128]{1,0:T(8,128)S(1)}, f32[328,128]{1,0:T(8,128)S(1)}, u32[]{:S(2)}, u32[]{:S(2)}) collective-permute-start(f32[328,128]{1,0:T(8,128)S(1)} %get-tuple-element.31.refs_2_), channel_id=1, source_target_pairs={{0,8},{8,16},{16,24},{24,0},{1,9},{9,17},{17,25},{25,1},{2,10},{10... | collective-permute-start | bytes 503816 | tf_op jit(solution)/shard_map/ppermute | solution.py:456
  9.0 9.8 %collective-permute-start.1 = (f32[328,128]{1,0:T(8,128)S(1)}, f32[328,128]{1,0:T(8,128)S(1)}, u32[]{:S(2)}, u32[]{:S(2)}) collective-permute-start(f32[328,128]{1,0:T(8,128)S(1)} %get-tuple-element.32.refs_3_), channel_id=1, source_target_pairs={{0,24},{8,0},{16,8},{24,16},{1,25},{9,1},{17,9},{25,17},{2,26},{10... | collective-permute-start | bytes 503816 | tf_op jit(solution)/shard_map/ppermute | solution.py:456
  10.4 4.0 %collective-permute-start.4 = (f32[8,128]{1,0:T(8,128)S(1)}, f32[8,128]{1,0:T(8,128)S(1)}, u32[]{:S(2)}, u32[]{:S(2)}) collective-permute-start(f32[8,128]{1,0:T(8,128)S(1)} %slice_bitcast_fusion), channel_id=1, source_target_pairs={{0,16},{8,24},{16,0},{24,8},{1,17},{9,25},{17,1},{25,9},{2,18},{10... | collective-permute-start | bytes 12296 | tf_op jit(solution)/shard_map/ppermute | solution.py:456
  19.2 10.6 %collective-permute-start.5 = (f32[320,128]{1,0:T(8,128)S(1)}, f32[320,128]{1,0:T(8,128)S(1)}, u32[]{:S(2)}, u32[]{:S(2)}) collective-permute-start(f32[320,128]{1,0:T(8,128)S(1)} %get-tuple-element.44), channel_id=1, source_target_pairs={{0,8},{8,16},{16,24},{24,0},{1,9},{9,17},{17,25},{25,1},{2,10},{10... | collective-permute-start | bytes 491528 | tf_op jit(solution)/shard_map/ppermute | solution.py:456
  20.8 9.1 %collective-permute-start.6 = (f32[320,128]{1,0:T(8,128)S(1)}, f32[320,128]{1,0:T(8,128)S(1)}, u32[]{:S(2)}, u32[]{:S(2)}) collective-permute-start(f32[320,128]{1,0:T(8,128)S(1)} %get-tuple-element.45), channel_id=1, source_target_pairs={{0,24},{8,0},{16,8},{24,16},{1,25},{9,1},{17,9},{25,17},{2,26},{10... | collective-permute-start | bytes 491528 | tf_op jit(solution)/shard_map/ppermute | solution.py:456
  22.9 5.1 %collective-permute-start.8 = (f32[40,128]{1,0:T(8,128)S(1)}, f32[40,128]{1,0:T(8,128)S(1)}, u32[]{:S(2)}, u32[]{:S(2)}) collective-permute-start(f32[40,128]{1,0:T(8,128)S(1)} %get-tuple-element.53), channel_id=1, source_target_pairs={{1,2},{2,1},{3,4},{4,3},{5,6},{6,5},{7,0},{0,7},{9,10},{10,9},{11,... | collective-permute-start | bytes 61448 | tf_op jit(solution)/shard_map/ppermute | solution.py:465
  23.0 5.0 %collective-permute-start.7 = (f32[40,128]{1,0:T(8,128)S(1)}, f32[40,128]{1,0:T(8,128)S(1)}, u32[]{:S(2)}, u32[]{:S(2)}) collective-permute-start(f32[40,128]{1,0:T(8,128)S(1)} %get-tuple-element.53), channel_id=1, source_target_pairs={{0,1},{1,0},{2,3},{3,2},{4,5},{5,4},{6,7},{7,6},{8,9},{9,8},{10,11... | collective-permute-start | bytes 61448 | tf_op jit(solution)/shard_map/ppermute | solution.py:465

commit v6 on v5

--- a/solution.py
+++ b/solution.py
@@ -456,18 +456,21 @@
     return lax.ppermute(value, axis, [(i, (i + amount) % count) for i in range(count)])
 
 
-def pair_swap(value, axis, first):
-    count = lax.axis_size(axis)
-    pairs = []
-    for low in range(first, count, 2):
-        high = (low + 1) % count
-        pairs += [(low, high), (high, low)]
-    return lax.ppermute(value, axis, pairs)
-
-
 def lat_exchange(edge):
-    swap_a = pair_swap(edge, LAT_AXES, 0)
-    swap_b = pair_swap(edge, LAT_AXES, 1)
+    lon_total = lax.axis_size("lon")
+    lat_total = lax.axis_size("lat") * lax.axis_size("comp")
+    inside, between = [], []
+    for lon in range(lon_total):
+        first = lon * lat_total
+        for low in range(0, lat_total, 2):
+            inside += [(first + low, first + low + 1), (first + low + 1, first + low)]
+        for low in range(1, lat_total - 1, 2):
+            between += [(first + low, first + low + 1), (first + low + 1, first + low)]
+        across = (lon + lon_total // 2) % lon_total * lat_total
+        for end in (0, lat_total - 1):
+            between.append((first + end, across + end))
+    swap_a = lax.ppermute(edge, ("lon",) + LAT_AXES, inside)
+    swap_b = lax.ppermute(edge, ("lon",) + LAT_AXES, between)
     return swap_a, swap_b
 
 

time: 31.5 us -> 28.6 us (0.908)
  waiting for transfers between devices: 9.91 us -> 6.8 us
    ppermute x4, waiting for transfers between devices: 4.92 us -> 2.31 us  [the longest x2 2.31 us: lat_exchange(): swap_b = lax.ppermute(edge, ('lon',) + LAT_AXES, between)]
    ppermute x5, waiting for transfers between devices: 4.99 us -> 4.49 us  [ring_shift(): lax.ppermute(value, axis, [(i, (i + amount) % count) for i in range(count)])]
  transfers between devices with their start and end apart: 9 -> 9, of which waited for: 4 -> 4; matrix products, arithmetic and copies ran while one was open for 0% -> 0% of each run, Pallas kernels for 14% -> 15%
where the time goes in v6:
time: 28.6 us; the launch traced here: 28.5 us
  starting transfers between devices  12.4 us (43%)
  Pallas kernels  9.09 us (32%)
  waiting for transfers between devices  6.8 us (24%)
    pallas_call x7, Pallas kernels, call(): pl.pallas_call(kernel, out_shape=[(pltpu.HBM if at in hbm_out else pltpu....  9.09 us
    ppermute x5, starting transfers between devices, ring_shift(): lax.ppermute(value, axis, [(i, (i + amount) % count) for i in range(count)])  7.42 us
    ppermute x5, waiting for transfers between devices, ring_shift(): lax.ppermute(value, axis, [(i, (i + amount) % count) for i in range(count)])  4.49 us
    ppermute x2, starting transfers between devices, lat_exchange(): swap_b = lax.ppermute(edge, ('lon',) + LAT_AXES, between)  3.97 us
    ppermute x2, waiting for transfers between devices, lat_exchange(): swap_b = lax.ppermute(edge, ('lon',) + LAT_AXES, between)  2.31 us
    ppermute x2, starting transfers between devices, lat_exchange(): swap_a = lax.ppermute(edge, ('lon',) + LAT_AXES, inside)  1.02 us
  transfers between devices with their start and end apart: 9, of which 4 were waited for; matrix products, arithmetic and copies ran while one was open for 0% of the time, Pallas kernels for 15%

profile of v6, /device:TPU:0, one launch (start us, length us, event | category | flops | bytes accessed | tf_op | source)
XLA Modules:
  0.0 28.5 jit_solution(14099777199149367668)
XLA Ops:
  0.0 0.0 copy-start
  0.0 1.6 %shard_map.73 = (f32[328,128]{1,0:T(8,128)S(1)}, f32[328,128]{1,0:T(8,128)S(1)}, f32[4,8,128]{2,1,0:T(8,128)S(1)}, s32[8,128]{1,0:T(8,128)S(1)}, f32[640,128]{1,0:T(8,128)S(1)}) custom-call(f32[320,8,128]{2,1,0:T(8,128)} %bitcast.8, s32[8,128]{1,0:T(8,128)} %refs_1_.1, bf16[4,4,256]{2,1,0:T(4,128)(2,1)} %bitcast.13, bf16[4,256,128]{2,1,0:T(8,128)(2,1)} %bitcast.12, ...), custom_call_target="tpu_custom_call" | custom-call | tf_op jit(solution)/shard_map/pallas_call | solution.py:440
  1.6 0.1 copy-done
  1.7 1.2 %shard_map.74 = (f32[48,128]{1,0:T(8,128)S(1)}, f32[640,128]{1,0:T(8,128)S(1)}, f32[640,128]{1,0:T(8,128)S(1)}, f32[640,128]{1,0:T(8,128)S(1)}, f32[640,128]{1,0...) custom-call(f32[2560,128]{1,0:T(8,128)S(1)} %bitcast.9, ...), custom_call_target="tpu_custom_call" | custom-call | tf_op jit(solution)/shard_map/pallas_call | solution.py:440
  2.9 3.1 %collective-permute-start.3 = (f32[48,128]{1,0:T(8,128)S(1)}, f32[48,128]{1,0:T(8,128)S(1)}, u32[]{:S(2)}, u32[]{:S(2)}) collective-permute-start(f32[48,128]{1,0:T(8,128)S(1)} %get-tuple-element.38), channel_id=1, source_target_pairs={{1,2},{2,1},{3,4},{4,3},{5,6},{6,5},{0,16},{7,23},{9,10},{10,9},{1... | collective-permute-start | bytes 73736 | tf_op jit(solution)/shard_map/ppermute | solution.py:473
  6.0 0.2 collective-permute-start.2
  6.2 1.5 %collective-permute-start = (f32[328,128]{1,0:T(8,128)S(1)}, f32[328,128]{1,0:T(8,128)S(1)}, u32[]{:S(2)}, u32[]{:S(2)}) collective-permute-start(f32[328,128]{1,0:T(8,128)S(1)} %get-tuple-element.31.refs_2_), channel_id=1, source_target_pairs={{0,8},{8,16},{16,24},{24,0},{1,9},{9,17},{17,25},{25,1},{2,10},{10... | collective-permute-start | bytes 503816 | tf_op jit(solution)/shard_map/ppermute | solution.py:456
  7.6 1.4 %collective-permute-start.1 = (f32[328,128]{1,0:T(8,128)S(1)}, f32[328,128]{1,0:T(8,128)S(1)}, u32[]{:S(2)}, u32[]{:S(2)}) collective-permute-start(f32[328,128]{1,0:T(8,128)S(1)} %get-tuple-element.32.refs_3_), channel_id=1, source_target_pairs={{0,24},{8,0},{16,8},{24,16},{1,25},{9,1},{17,9},{25,17},{2,26},{10... | collective-permute-start | bytes 503816 | tf_op jit(solution)/shard_map/ppermute | solution.py:456
  9.1 1.5 %collective-permute-start.4 = (f32[8,128]{1,0:T(8,128)S(1)}, f32[8,128]{1,0:T(8,128)S(1)}, u32[]{:S(2)}, u32[]{:S(2)}) collective-permute-start(f32[8,128]{1,0:T(8,128)S(1)} %slice_bitcast_fusion), channel_id=1, source_target_pairs={{0,16},{8,24},{16,0},{24,8},{1,17},{9,25},{17,1},{25,9},{2,18},{10... | collective-permute-start | bytes 12296 | tf_op jit(solution)/shard_map/ppermute | solution.py:456
  10.6 0.0 collective-permute-done.3.refs_6_
  10.6 0.0 collective-permute-done.2.refs_5_
  10.6 1.8 %shard_map.75 = (f32[2560,128]{1,0:T(8,128)S(1)}, f32[640,128]{1,0:T(8,128)S(1)}, s32[32,128]{1,0:T(8,128)S(1)}) custom-call(f32[2560,128]{1,0:T(8,128)S(1)} %bitcast.10, s32[8,128]{1,0:T(8,128)S(1)} %get-tuple-element.33.refs_1_, f32[640,128]{1,0:T(8,128)S(1)} %get-tuple-element.35.refs_2_, f32[640,128]{1,0:T(8,128)S(1)} %get-tuple-element.36.refs_3_, ...), custom_call_target="tpu_custom_call" | custom-call | tf_op jit(solution)/shard_map/pallas_call | solution.py:440
  12.4 0.6 %collective-permute-done.4.refs_9_ = f32[8,128]{1,0:T(8,128)S(1)} collective-permute-done((f32[8,128]{1,0:T(8,128)S(1)}, f32[8,128]{1,0:T(8,128)S(1)}, u32[]{:S(2)}, u32[]{:S(2)}) %collective-permute-start.4) | collective-permute-done | bytes 4128 | tf_op jit(solution)/shard_map/ppermute | solution.py:456
  13.0 1.2 %collective-permute-done.refs_0_ = f32[328,128]{1,0:T(8,128)S(1)} collective-permute-done((f32[328,128]{1,0:T(8,128)S(1)}, f32[328,128]{1,0:T(8,128)S(1)}, u32[]{:S(2)}, u32[]{:S(2)}) %collective-permute-start) | collective-permute-done | bytes 167968 | tf_op jit(solution)/shard_map/ppermute | solution.py:456
  14.2 2.7 %collective-permute-done.1.refs_1_ = f32[328,128]{1,0:T(8,128)S(1)} collective-permute-done((f32[328,128]{1,0:T(8,128)S(1)}, f32[328,128]{1,0:T(8,128)S(1)}, u32[]{:S(2)}, u32[]{:S(2)}) %collective-permute-start.1) | collective-permute-done | bytes 167968 | tf_op jit(solution)/shard_map/ppermute | solution.py:456
  16.9 0.5 %shard_map.76 = (f32[320,128]{1,0:T(8,128)S(1)}, f32[320,128]{1,0:T(8,128)S(1)}, f32[640,128]{1,0:T(8,128)S(1)}, f32[640,128]{1,0:T(8,128)S(1)}, f32[64,128]{1,0:T(8,128)S(1)}, /*index=5*/s32[8,128]{1,0:T(8,128)S(1)}) custom-call(f32[328,128]{1,0:T(8,128)S(1)} %collective-permute-done.refs_0_, f32[328,128]{1,0:T(8,128)S(1)} %collective-permute-done.1.refs_1_, ...), custom_call_target="tpu_custom_call" | custom-call | tf_op jit(solution)/shard_map/pallas_call | solution.py:440
  17.4 1.5 %collective-permute-start.5 = (f32[320,128]{1,0:T(8,128)S(1)}, f32[320,128]{1,0:T(8,128)S(1)}, u32[]{:S(2)}, u32[]{:S(2)}) collective-permute-start(f32[320,128]{1,0:T(8,128)S(1)} %get-tuple-element.44), channel_id=1, source_target_pairs={{0,8},{8,16},{16,24},{24,0},{1,9},{9,17},{17,25},{25,1},{2,10},{10... | collective-permute-start | bytes 491528 | tf_op jit(solution)/shard_map/ppermute | solution.py:456
  18.9 1.4 %collective-permute-start.6 = (f32[320,128]{1,0:T(8,128)S(1)}, f32[320,128]{1,0:T(8,128)S(1)}, u32[]{:S(2)}, u32[]{:S(2)}) collective-permute-start(f32[320,128]{1,0:T(8,128)S(1)} %get-tuple-element.45), channel_id=1, source_target_pairs={{0,24},{8,0},{16,8},{24,16},{1,25},{9,1},{17,9},{25,17},{2,26},{10... | collective-permute-start | bytes 491528 | tf_op jit(solution)/shard_map/ppermute | solution.py:456
  20.4 0.7 %shard_map.77 = (f32[2560,128]{1,0:T(8,128)S(1)}, f32[40,128]{1,0:T(8,128)S(1)}) custom-call(f32[2560,128]{1,0:T(8,128)S(1)} %get-tuple-element.47.refs_0_, f32[640,128]{1,0:T(8,128)S(1)} %get-tuple-element.48.refs_1_, f32[640,128]{1,0:T(8,128)S(1)} %get-tuple-element.49.refs_2_, f32[64,128]{1,0:T(8,128)S(1)} %get-tuple-element.50.refs_3_.refs_7_), custom_call_target="tpu_custom_call" | custom-call | tf_op jit(solution)/shard_map/pallas_call | solution.py:440
  21.1 0.9 %collective-permute-start.8 = (f32[40,128]{1,0:T(8,128)S(1)}, f32[40,128]{1,0:T(8,128)S(1)}, u32[]{:S(2)}, u32[]{:S(2)}) collective-permute-start(f32[40,128]{1,0:T(8,128)S(1)} %get-tuple-element.53), channel_id=1, source_target_pairs={{1,2},{2,1},{3,4},{4,3},{5,6},{6,5},{0,16},{7,23},{9,10},{10,9},{1... | collective-permute-start | bytes 61448 | tf_op jit(solution)/shard_map/ppermute | solution.py:473
  22.0 0.8 %collective-permute-start.7 = (f32[40,128]{1,0:T(8,128)S(1)}, f32[40,128]{1,0:T(8,128)S(1)}, u32[]{:S(2)}, u32[]{:S(2)}) collective-permute-start(f32[40,128]{1,0:T(8,128)S(1)} %get-tuple-element.53), channel_id=1, source_target_pairs={{0,1},{1,0},{2,3},{3,2},{4,5},{5,4},{6,7},{7,6},{8,9},{9,8},{10,11... | collective-permute-start | bytes 61448 | tf_op jit(solution)/shard_map/ppermute | solution.py:472
  22.8 2.3 %collective-permute-done.8.refs_6_ = f32[40,128]{1,0:T(8,128)S(1)} collective-permute-done((f32[40,128]{1,0:T(8,128)S(1)}, f32[40,128]{1,0:T(8,128)S(1)}, u32[]{:S(2)}, u32[]{:S(2)}) %collective-permute-start.8) | collective-permute-done | bytes 20512 | tf_op jit(solution)/shard_map/ppermute | solution.py:473
  25.1 0.0 collective-permute-done.7.refs_5_
  25.1 1.8 %shard_map.78 = (f32[2560,128]{1,0:T(8,128)S(1)}, f32[640,128]{1,0:T(8,128)S(1)}) custom-call(f32[2560,128]{1,0:T(8,128)S(1)} %get-tuple-element.51.refs_0_, s32[32,128]{1,0:T(8,128)S(1)} %get-tuple-element.52.refs_1_, f32[640,128]{1,0:T(8,128)S(1)} %get-tuple-element.35.refs_2_, f32[640,128]{1,0:T(8,128)S(1)} %get-tuple-element.36.refs_3_, ...), custom_call_target="tpu_custom_call" | custom-call | tf_op jit(solution)/shard_map/pallas_call | solution.py:440
  26.9 0.0 collective-permute-done.5.refs_0_
  27.0 0.0 collective-permute-done.6.refs_1_
  27.0 1.5 %shard_map.79 = f32[2560,128]{1,0:T(8,128)} custom-call(f32[320,128]{1,0:T(8,128)S(1)} %collective-permute-done.5.refs_0_, f32[320,128]{1,0:T(8,128)S(1)} %collective-permute-done.6.refs_1_, f32[640,128]{1,0:T(8,128)S(1)} %get-tuple-element.46.refs_2_, f32[640,128]{1,0:T(8,128)S(1)} %get-tuple-element.54.refs_3_, ...), custom_call_target="tpu_custom_call" | custom-call | tf_op jit(solution)/shard_map/pallas_call | solution.py:440
  (1 shorter events, 0.0 us)
Async XLA Ops:
  0.0 1.7 %copy-start = (f32[4,80,8,128]{3,2,1,0:T(8,128)S(1)}, f32[4,80,8,128]{3,2,1,0:T(8,128)}, u32[]{:S(2)}) copy-start(f32[4,80,8,128]{3,2,1,0:T(8,128)} %param.7) | copy-start | bytes 3932164
  2.9 7.7 %collective-permute-start.3 = (f32[48,128]{1,0:T(8,128)S(1)}, f32[48,128]{1,0:T(8,128)S(1)}, u32[]{:S(2)}, u32[]{:S(2)}) collective-permute-start(f32[48,128]{1,0:T(8,128)S(1)} %get-tuple-element.38), channel_id=1, source_target_pairs={{1,2},{2,1},{3,4},{4,3},{5,6},{6,5},{0,16},{7,23},{9,10},{10,9},{1... | collective-permute-start | bytes 73736 | tf_op jit(solution)/shard_map/ppermute | solution.py:473
  6.0 4.6 %collective-permute-start.2 = (f32[48,128]{1,0:T(8,128)S(1)}, f32[48,128]{1,0:T(8,128)S(1)}, u32[]{:S(2)}, u32[]{:S(2)}) collective-permute-start(f32[48,128]{1,0:T(8,128)S(1)} %get-tuple-element.38), channel_id=1, source_target_pairs={{0,1},{1,0},{2,3},{3,2},{4,5},{5,4},{6,7},{7,6},{8,9},{9,8},{10,11... | collective-permute-start | bytes 73736 | tf_op jit(solution)/shard_map/ppermute | solution.py:472
  6.2 8.1 %collective-permute-start = (f32[328,128]{1,0:T(8,128)S(1)}, f32[328,128]{1,0:T(8,128)S(1)}, u32[]{:S(2)}, u32[]{:S(2)}) collective-permute-start(f32[328,128]{1,0:T(8,128)S(1)} %get-tuple-element.31.refs_2_), channel_id=1, source_target_pairs={{0,8},{8,16},{16,24},{24,0},{1,9},{9,17},{17,25},{25,1},{2,10},{10... | collective-permute-start | bytes 503816 | tf_op jit(solution)/shard_map/ppermute | solution.py:456
  7.6 9.3 %collective-permute-start.1 = (f32[328,128]{1,0:T(8,128)S(1)}, f32[328,128]{1,0:T(8,128)S(1)}, u32[]{:S(2)}, u32[]{:S(2)}) collective-permute-start(f32[328,128]{1,0:T(8,128)S(1)} %get-tuple-element.32.refs_3_), channel_id=1, source_target_pairs={{0,24},{8,0},{16,8},{24,16},{1,25},{9,1},{17,9},{25,17},{2,26},{10... | collective-permute-start | bytes 503816 | tf_op jit(solution)/shard_map/ppermute | solution.py:456
  9.1 4.0 %collective-permute-start.4 = (f32[8,128]{1,0:T(8,128)S(1)}, f32[8,128]{1,0:T(8,128)S(1)}, u32[]{:S(2)}, u32[]{:S(2)}) collective-permute-start(f32[8,128]{1,0:T(8,128)S(1)} %slice_bitcast_fusion), channel_id=1, source_target_pairs={{0,16},{8,24},{16,0},{24,8},{1,17},{9,25},{17,1},{25,9},{2,18},{10... | collective-permute-start | bytes 12296 | tf_op jit(solution)/shard_map/ppermute | solution.py:456
  17.4 9.6 %collective-permute-start.5 = (f32[320,128]{1,0:T(8,128)S(1)}, f32[320,128]{1,0:T(8,128)S(1)}, u32[]{:S(2)}, u32[]{:S(2)}) collective-permute-start(f32[320,128]{1,0:T(8,128)S(1)} %get-tuple-element.44), channel_id=1, source_target_pairs={{0,8},{8,16},{16,24},{24,0},{1,9},{9,17},{17,25},{25,1},{2,10},{10... | collective-permute-start | bytes 491528 | tf_op jit(solution)/shard_map/ppermute | solution.py:456
  18.9 8.0 %collective-permute-start.6 = (f32[320,128]{1,0:T(8,128)S(1)}, f32[320,128]{1,0:T(8,128)S(1)}, u32[]{:S(2)}, u32[]{:S(2)}) collective-permute-start(f32[320,128]{1,0:T(8,128)S(1)} %get-tuple-element.45), channel_id=1, source_target_pairs={{0,24},{8,0},{16,8},{24,16},{1,25},{9,1},{17,9},{25,17},{2,26},{10... | collective-permute-start | bytes 491528 | tf_op jit(solution)/shard_map/ppermute | solution.py:456
  21.1 4.1 %collective-permute-start.8 = (f32[40,128]{1,0:T(8,128)S(1)}, f32[40,128]{1,0:T(8,128)S(1)}, u32[]{:S(2)}, u32[]{:S(2)}) collective-permute-start(f32[40,128]{1,0:T(8,128)S(1)} %get-tuple-element.53), channel_id=1, source_target_pairs={{1,2},{2,1},{3,4},{4,3},{5,6},{6,5},{0,16},{7,23},{9,10},{10,9},{1... | collective-permute-start | bytes 61448 | tf_op jit(solution)/shard_map/ppermute | solution.py:473
  22.0 3.2 %collective-permute-start.7 = (f32[40,128]{1,0:T(8,128)S(1)}, f32[40,128]{1,0:T(8,128)S(1)}, u32[]{:S(2)}, u32[]{:S(2)}) collective-permute-start(f32[40,128]{1,0:T(8,128)S(1)} %get-tuple-element.53), channel_id=1, source_target_pairs={{0,1},{1,0},{2,3},{3,2},{4,5},{5,4},{6,7},{7,6},{8,9},{9,8},{10,11... | collective-permute-start | bytes 61448 | tf_op jit(solution)/shard_map/ppermute | solution.py:472

commit v7 on v6

--- a/solution.py
+++ b/solution.py
@@ -185,34 +185,35 @@
                 out_ref[pl.ds(start * SUB + 2 * field + side, SUB, stride=SUB), :] = value
 
 
-def inner_step(levels, first, x_ref, depth, depths, gain_ref, down_ref, up_ref, swap_a, swap_b,
-               out_ref, merged_ref, force_ref=None):
+def explicit_kernel(levels, later, x_ref, count_ref, *rest):
+    force_ref, out_ref = rest if later else (None, rest[0])
     sub = sublane_ids()
     lane = lane_ids()
-    even = lane % 2 == 0
-    groups = levels // GROUP
     lat_total = LANE * lax.axis_size("lat") * lax.axis_size("comp")
     row_ids = (lat_place() * LANE + lane).astype(jnp.float32)
     rotation = CORIOLIS * (2.0 * (row_ids + 0.5) / lat_total - 1.0)
-    depth_e, depth_w, depth_n, depth_s = depths
-    for group in range(groups):
-        south, north = lat_sides(swap_a, swap_b, group)
-        merged_ref[group] = jnp.where(even, north, pltpu.roll(south, 2, 1))
-
-    def forward_level(level, inner, halo, carry):
-        sum_e, sum_w, sum_n, sum_s, *prev = carry
+    depth = count_ref[...]
+
+    def neighbours(value):
+        return (
+            jnp.where(sub == SUB - 1, 0, pltpu.roll(value, SUB - 1, 0)),
+            jnp.where(sub == 0, 0, pltpu.roll(value, 1, 0)),
+            jnp.where(lane == LANE - 1, 0, pltpu.roll(value, LANE - 1, 1)),
+            jnp.where(lane == 0, 0, pltpu.roll(value, 1, 1)),
+        )
+
+    depth_e, depth_w, depth_n, depth_s = neighbours(depth)
+
+    def level_body(level, inner, carry):
+        sum_e, sum_w, sum_n, sum_s = carry
         here, east, west, north, south = [], [], [], [], []
         for field in range(FIELDS):
             value = tile_at(x_ref, field * levels + level)
-            if first:
+            if not later:
                 value = jnp.where(level < depth, value, 0.0)
-            j = inner * FIELDS + field
-            side = pltpu.roll(halo, (LANE - 1 - 2 * j) % LANE, 1)
             here.append(value)
-            east.append(jnp.where(sub == SUB - 1, 0.0, pltpu.roll(value, SUB - 1, 0)))
-            west.append(jnp.where(sub == 0, 0.0, pltpu.roll(value, 1, 0)))
-            north.append(jnp.where(lane == LANE - 1, side, pltpu.roll(value, LANE - 1, 1)))
-            south.append(jnp.where(lane == 0, side, pltpu.roll(value, 1, 1)))
+            for into, side in zip((east, west, north, south), neighbours(value)):
+                into.append(side)
         wet_e, wet_w, wet_n, wet_s = level < depth_e, level < depth_w, level < depth_n, level < depth_s
         keep = 1.0 - (
             (jnp.where(wet_e, DIFFUSE, 0.0) + jnp.where(wet_w, DIFFUSE, 0.0))
@@ -227,9 +228,6 @@
         u, v = here[2], here[3]
         u_part = QUARTER * u
         v_part = QUARTER * v
-        gain = tile_at(gain_ref, level)
-        down = tile_at(down_ref, level)
-        done = []
         for field in range(FIELDS):
             around = (east[field] + west[field]) + (north[field] + south[field])
             value = keep * here[field] + DIFFUSE * around
@@ -241,20 +239,74 @@
                 value = value + (rotation * v - force_x)
             else:
                 value = value - (rotation * u + force_y)
-            if inner == 0 and force_ref is not None:
+            if inner == 0 and later:
                 value = value + jnp.where(level == 0, tile_at(force_ref, FIELDS + field), 0.0)
+            put_tile(out_ref, field * levels + level, value)
+        return sum_e, sum_w, sum_n, sum_s
+
+    def group_body(group, carry):
+        for inner in range(GROUP):
+            carry = level_body(group * GROUP + inner, inner, carry)
+        return carry
+
+    lax.fori_loop(0, levels // GROUP, group_body, (zeros(),) * 4)
+
+
+def solve_kernel(levels, later, x_ref, explicit_ref, gain_ref, down_ref, up_ref, swap_a, swap_b, *rest):
+    if later:
+        depth_ref, out_ref, packed_ref, merged_ref = rest
+    else:
+        out_ref, packed_ref, depth_ref, merged_ref = rest
+    lane = lane_ids()
+    even = lane % 2 == 0
+    groups = levels // GROUP
+    north_lane, south_lane = lane == LANE - 1, lane == 0
+    rim = jnp.logical_or(north_lane, south_lane)
+    sign = jnp.where(north_lane, -1.0, jnp.where(south_lane, 1.0, 0.0))
+    if later:
+        halo_depth = depth_ref[...]
+    else:
+        south, north = lat_sides(swap_a, swap_b, groups)
+        halo_depth = jnp.where(
+            north_lane, pltpu.roll(north, LANE - 1, 1), jnp.where(south_lane, pltpu.roll(south, 1, 1), 0.0)
+        ).astype(jnp.int32)
+        depth_ref[...] = halo_depth
+    for group in range(groups):
+        south, north = lat_sides(swap_a, swap_b, group)
+        merged_ref[group] = jnp.where(even, north, pltpu.roll(south, 2, 1))
+
+    def level_body(level, inner, halo, carry):
+        total, *prev = carry
+        sides = []
+        for field in range(FIELDS):
+            j = inner * FIELDS + field
+            sides.append(jnp.where(rim, pltpu.roll(halo, (LANE - 1 - 2 * j) % LANE, 1), 0.0))
+        total = total + (sides[1] - WARMTH * sides[0])
+        wet = level < halo_depth
+        v_part = (QUARTER * sign) * tile_at(x_ref, 3 * levels + level)
+        gain = tile_at(gain_ref, level)
+        down = tile_at(down_ref, level)
+        done = []
+        for field in range(FIELDS):
+            row = field * levels + level
+            value = tile_at(explicit_ref, row)
+            value = value + DIFFUSE * (sides[field] - jnp.where(wet, tile_at(x_ref, row), 0.0))
+            if field < 2:
+                value = value + v_part * sides[field]
+            elif field == 3:
+                value = value + (PUSH * sign) * jnp.where(wet, total, 0.0)
             value = value * gain + down * prev[field]
-            put_tile(out_ref, field * levels + level, value)
+            put_tile(out_ref, row, value)
             done.append(value)
-        return (sum_e, sum_w, sum_n, sum_s, *done)
+        return (total, *done)
 
     def forward_group(group, carry):
         halo = merged_ref[group]
         for inner in range(GROUP):
-            carry = forward_level(group * GROUP + inner, inner, halo, carry)
+            carry = level_body(group * GROUP + inner, inner, halo, carry)
         return carry
 
-    lax.fori_loop(0, groups, forward_group, (zeros(),) * 8)
+    lax.fori_loop(0, groups, forward_group, (zeros(),) * (1 + FIELDS))
 
     def backward_group(step, following):
         group = groups - 1 - step
@@ -270,35 +322,6 @@
         return following
 
     lax.fori_loop(0, groups, backward_group, (zeros(),) * FIELDS)
-
-
-def first_kernel(levels, x_ref, count_ref, gain_ref, down_ref, up_ref, swap_a, swap_b,
-                 out_ref, packed_ref, depth_ref, merged_ref):
-    sub = sublane_ids()
-    lane = lane_ids()
-    depth = count_ref[...]
-    count_f = depth.astype(jnp.float32)
-    side_s, side_n = lat_sides(swap_a, swap_b, levels // GROUP)
-    depths = []
-    for at, value in enumerate((
-        jnp.where(sub == SUB - 1, 0.0, pltpu.roll(count_f, SUB - 1, 0)),
-        jnp.where(sub == 0, 0.0, pltpu.roll(count_f, 1, 0)),
-        jnp.where(lane == LANE - 1, pltpu.roll(side_n, LANE - 1, 1), pltpu.roll(count_f, LANE - 1, 1)),
-        jnp.where(lane == 0, pltpu.roll(side_s, 1, 1), pltpu.roll(count_f, 1, 1)),
-    )):
-        value = value.astype(jnp.int32)
-        put_tile(depth_ref, at, value)
-        depths.append(value)
-    inner_step(levels, True, x_ref, depth, depths, gain_ref, down_ref, up_ref, swap_a, swap_b,
-               out_ref, merged_ref)
-    pack_edges(levels, FIELDS, out_ref, packed_ref)
-
-
-def second_kernel(levels, x_ref, depth_ref, gain_ref, down_ref, up_ref, swap_a, swap_b, force_ref,
-                  out_ref, packed_ref, merged_ref):
-    depths = [tile_at(depth_ref, at) for at in range(4)]
-    inner_step(levels, False, x_ref, None, depths, gain_ref, down_ref, up_ref, swap_a, swap_b,
-               out_ref, merged_ref, force_ref)
     pack_edges(levels, FIELDS, out_ref, packed_ref)
 
 
@@ -397,26 +420,33 @@
 
 
 def second_edge_kernel(levels, west_in, east_in, full_ref, packed_ref, gain_ref, down_ref, up_ref, depth_ref,
-                       inner_ref, result_ref, state_ref, change_ref, sems):
+                       inner_ref, result_ref, change_ref, columns, bulk_sems, sems):
     even = sublane_ids() % 2 == 0
-    sub = sublane_ids()
     copies = []
 
+    def bulk(group):
+        for field in range(FIELDS):
+            piece = pl.ds(field * levels + group * GROUP, GROUP)
+            yield pltpu.make_async_copy(inner_ref.at[piece], result_ref.at[piece], bulk_sems.at[group, field])
+
+    for group in range(levels // GROUP - 1, -1, -1):
+        for copy in bulk(group):
+            copy.start()
+
     def finish(level, change):
-        edge = tile_at(packed_ref, level) + change
-        for field in range(FIELDS):
-            side = pltpu.roll(edge, SUB - 1 - 2 * field, 0)
-            rim = jnp.logical_or(sub == 0, sub == SUB - 1)
-            row = field * levels + level
-            put_tile(state_ref, row, jnp.where(rim, side, tile_at(inner_ref, row)))
+        columns[level] = tile_at(packed_ref, level) + change
         if level % GROUP == 0:
+            for copy in bulk(level // GROUP):
+                copy.wait()
             for field in range(FIELDS):
-                piece = pl.ds((field * levels + level) * SUB, GROUP * SUB)
-                copy = pltpu.make_async_copy(
-                    state_ref.at[piece, :], result_ref.at[piece, :], sems.at[level // GROUP, field]
-                )
-                copy.start()
-                copies.append(copy)
+                for side, column in ((0, SUB - 1), (1, 0)):
+                    copy = pltpu.make_async_copy(
+                        columns.at[pl.ds(level, GROUP), 2 * field + side, :],
+                        result_ref.at[pl.ds(field * levels + level, GROUP), column, :],
+                        sems.at[level // GROUP, 2 * field + side],
+                    )
+                    copy.start()
+                    copies.append(copy)
 
     edge_change(
         levels,
@@ -519,11 +549,14 @@
         (x, count, rate),
     )
     swap_a, swap_b = lat_exchange(edge)
-    others = [ring_shift(parts[s], "lon", s) for s in range(2, lon_total - 1)]
-    inner, packed, depths = call(
-        bind(first_kernel, levels),
-        [state_shape, table, ((4 * SUB, LANE), i32)],
-        (x, count, gain, down, up, swap_a, swap_b),
+    others = []
+    for s in range(2, lon_total - 1):
+        others.append(ring_shift(parts[s], "lon", s))
+    (explicit,) = call(bind(explicit_kernel, levels, False), [state_shape], (x, count))
+    inner, packed, lat_depth = call(
+        bind(solve_kernel, levels, False),
+        [state_shape, table, ((SUB, LANE), i32)],
+        (x, explicit, gain, down, up, swap_a, swap_b),
         scratch=[merged],
     )
     east_next, west_next, full, change, force, halo_depth = call(
@@ -539,17 +572,20 @@
         (inner, reply, change, force),
     )
     swap_a, swap_b = lat_exchange(edge)
+    (explicit,) = call(bind(explicit_kernel, levels, True), [state_shape], (state, count, force))
     inner, packed = call(
-        bind(second_kernel, levels),
+        bind(solve_kernel, levels, True),
         [state_shape, table],
-        (state, depths, gain, down, up, swap_a, swap_b, force),
+        (state, explicit, gain, down, up, swap_a, swap_b, lat_depth),
         scratch=[merged],
     )
     (result,) = call(
         bind(second_edge_kernel, levels),
-        [state_shape],
-        (from_west, from_east, full, packed, edge_gain, edge_down, edge_up, halo_depth, inner),
-        scratch=[pltpu.VMEM(*state_shape), pltpu.VMEM(*table), dma((groups, FIELDS))],
+        [((rows, lon_dev, lat_dev), f32)],
+        (from_west, from_east, full, packed, edge_gain, edge_down, edge_up, halo_depth,
+         inner.reshape(rows, lon_dev, lat_dev)),
+        scratch=[pltpu.VMEM(*table), pltpu.VMEM((levels, SUB, LANE), f32), dma((groups, FIELDS)),
+                 dma((groups, 2 * FIELDS))],
         hbm_out=(0,),
     )
     return result.reshape(ocean_state.shape)

time: 28.6 us -> 29.1 us (1.017)
  Pallas kernels: 9.09 us -> 11.1 us
  waiting for transfers between devices: 6.8 us -> 5.31 us
    pallas_call x7 -> x9, Pallas kernels: 9.09 us -> 11.1 us  [call(): pl.pallas_call(kernel, out_shape=[(pltpu.HBM if at in hbm_out else pltpu....]
    ppermute x2, waiting for transfers between devices: 2.31 us -> 1.05 us  [lat_exchange(): swap_b = lax.ppermute(edge, ('lon',) + LAT_AXES, between)]
  transfers between devices with their start and end apart: 9 -> 9, of which waited for: 4 -> 4; matrix products, arithmetic and copies ran while one was open for 0% -> 0% of each run, Pallas kernels for 15% -> 19%
where the time goes in v7:
time: 29.1 us; the launch traced here: 29 us
  starting transfers between devices  12.4 us (43%)
  Pallas kernels  11.1 us (38%)
  waiting for transfers between devices  5.31 us (18%)
    pallas_call x9, Pallas kernels, call(): pl.pallas_call(kernel, out_shape=[(pltpu.HBM if at in hbm_out else pltpu....  11.1 us
    ppermute x5, starting transfers between devices, ring_shift(): lax.ppermute(value, axis, [(i, (i + amount) % count) for i in range(count)])  7.42 us
    ppermute x5, waiting for transfers between devices, ring_shift(): lax.ppermute(value, axis, [(i, (i + amount) % count) for i in range(count)])  4.26 us
    ppermute x2, starting transfers between devices, lat_exchange(): swap_b = lax.ppermute(edge, ('lon',) + LAT_AXES, between)  3.97 us
    ppermute x2, waiting for transfers between devices, lat_exchange(): swap_b = lax.ppermute(edge, ('lon',) + LAT_AXES, between)  1.05 us
    ppermute x2, starting transfers between devices, lat_exchange(): swap_a = lax.ppermute(edge, ('lon',) + LAT_AXES, inside)  1.02 us
  transfers between devices with their start and end apart: 9, of which 4 were waited for; matrix products, arithmetic and copies ran while one was open for 0% of the time, Pallas kernels for 19%

profile of v7, /device:TPU:0, one launch (start us, length us, event | category | flops | bytes accessed | tf_op | source)
XLA Modules:
  0.0 29.0 jit_solution(3523114801249975499)
XLA Ops:
  0.0 0.0 copy-start
  0.0 1.6 %shard_map.73 = (f32[328,128]{1,0:T(8,128)S(1)}, f32[328,128]{1,0:T(8,128)S(1)}, f32[4,8,128]{2,1,0:T(8,128)S(1)}, s32[8,128]{1,0:T(8,128)S(1)}, f32[640,128]{1,0:T(8,128)S(1)}) custom-call(f32[320,8,128]{2,1,0:T(8,128)} %bitcast.9, s32[8,128]{1,0:T(8,128)} %refs_1_.1, bf16[4,4,256]{2,1,0:T(4,128)(2,1)} %bitcast.16, bf16[4,256,128]{2,1,0:T(8,128)(2,1)} %bitcast.15, ...), custom_call_target="tpu_custom_call" | custom-call | tf_op jit(solution)/shard_map/pallas_call | solution.py:470
  1.6 0.1 copy-done
  1.7 1.2 %shard_map.75 = (f32[48,128]{1,0:T(8,128)S(1)}, f32[640,128]{1,0:T(8,128)S(1)}, f32[640,128]{1,0:T(8,128)S(1)}, f32[640,128]{1,0:T(8,128)S(1)}, f32[640,128]{1,0...) custom-call(f32[2560,128]{1,0:T(8,128)S(1)} %bitcast.10, ...), custom_call_target="tpu_custom_call" | custom-call | tf_op jit(solution)/shard_map/pallas_call | solution.py:470
  2.9 3.1 %collective-permute-start.3 = (f32[48,128]{1,0:T(8,128)S(1)}, f32[48,128]{1,0:T(8,128)S(1)}, u32[]{:S(2)}, u32[]{:S(2)}) collective-permute-start(f32[48,128]{1,0:T(8,128)S(1)} %get-tuple-element.38), channel_id=1, source_target_pairs={{1,2},{2,1},{3,4},{4,3},{5,6},{6,5},{0,16},{7,23},{9,10},{10,9},{1... | collective-permute-start | bytes 73736 | tf_op jit(solution)/shard_map/ppermute | solution.py:503
  6.0 0.2 collective-permute-start.2
  6.2 1.5 %collective-permute-start = (f32[328,128]{1,0:T(8,128)S(1)}, f32[328,128]{1,0:T(8,128)S(1)}, u32[]{:S(2)}, u32[]{:S(2)}) collective-permute-start(f32[328,128]{1,0:T(8,128)S(1)} %get-tuple-element.31.refs_2_), channel_id=1, source_target_pairs={{0,8},{8,16},{16,24},{24,0},{1,9},{9,17},{17,25},{25,1},{2,10},{10... | collective-permute-start | bytes 503816 | tf_op jit(solution)/shard_map/ppermute | solution.py:486
  7.6 1.4 %collective-permute-start.1 = (f32[328,128]{1,0:T(8,128)S(1)}, f32[328,128]{1,0:T(8,128)S(1)}, u32[]{:S(2)}, u32[]{:S(2)}) collective-permute-start(f32[328,128]{1,0:T(8,128)S(1)} %get-tuple-element.32.refs_3_), channel_id=1, source_target_pairs={{0,24},{8,0},{16,8},{24,16},{1,25},{9,1},{17,9},{25,17},{2,26},{10... | collective-permute-start | bytes 503816 | tf_op jit(solution)/shard_map/ppermute | solution.py:486
  9.1 1.5 %collective-permute-start.4 = (f32[8,128]{1,0:T(8,128)S(1)}, f32[8,128]{1,0:T(8,128)S(1)}, u32[]{:S(2)}, u32[]{:S(2)}) collective-permute-start(f32[8,128]{1,0:T(8,128)S(1)} %slice_bitcast_fusion), channel_id=1, source_target_pairs={{0,16},{8,24},{16,0},{24,8},{1,17},{9,25},{17,1},{25,9},{2,18},{10... | collective-permute-start | bytes 12296 | tf_op jit(solution)/shard_map/ppermute | solution.py:486
  10.6 1.3 %shard_map.74.refs_1_ = f32[2560,128]{1,0:T(8,128)S(1)} custom-call(f32[2560,128]{1,0:T(8,128)S(1)} %bitcast.11, s32[8,128]{1,0:T(8,128)S(1)} %get-tuple-element.33.refs_1_), custom_call_target="tpu_custom_call" | custom-call | tf_op jit(solution)/shard_map/pallas_call | solution.py:470
  11.9 0.0 collective-permute-done.3.refs_6_
  11.9 0.0 collective-permute-done.2.refs_5_
  11.9 1.2 %shard_map.76 = (f32[2560,128]{1,0:T(8,128)S(1)}, f32[640,128]{1,0:T(8,128)S(1)}, s32[8,128]{1,0:T(8,128)S(1)}) custom-call(f32[2560,128]{1,0:T(8,128)S(1)} %bitcast.12, f32[2560,128]{1,0:T(8,128)S(1)} %shard_map.74.refs_1_, f32[640,128]{1,0:T(8,128)S(1)} %get-tuple-element.35.refs_2_, f32[640,128]{1,0:T(8,128)S(1)} %get-tuple-element.36.refs_3_, ...), custom_call_target="tpu_custom_call" | custom-call | tf_op jit(solution)/shard_map/pallas_call | solution.py:470
  13.1 0.0 collective-permute-done.4.refs_9_
  13.1 1.1 %collective-permute-done.refs_0_ = f32[328,128]{1,0:T(8,128)S(1)} collective-permute-done((f32[328,128]{1,0:T(8,128)S(1)}, f32[328,128]{1,0:T(8,128)S(1)}, u32[]{:S(2)}, u32[]{:S(2)}) %collective-permute-start) | collective-permute-done | bytes 167968 | tf_op jit(solution)/shard_map/ppermute | solution.py:486
  14.2 2.7 %collective-permute-done.1.refs_1_ = f32[328,128]{1,0:T(8,128)S(1)} collective-permute-done((f32[328,128]{1,0:T(8,128)S(1)}, f32[328,128]{1,0:T(8,128)S(1)}, u32[]{:S(2)}, u32[]{:S(2)}) %collective-permute-start.1) | collective-permute-done | bytes 167968 | tf_op jit(solution)/shard_map/ppermute | solution.py:486
  16.9 0.5 %shard_map.77 = (f32[320,128]{1,0:T(8,128)S(1)}, f32[320,128]{1,0:T(8,128)S(1)}, f32[640,128]{1,0:T(8,128)S(1)}, f32[640,128]{1,0:T(8,128)S(1)}, f32[64,128]{1,0:T(8,128)S(1)}, /*index=5*/s32[8,128]{1,0:T(8,128)S(1)}) custom-call(f32[328,128]{1,0:T(8,128)S(1)} %collective-permute-done.refs_0_, f32[328,128]{1,0:T(8,128)S(1)} %collective-permute-done.1.refs_1_, ...), custom_call_target="tpu_custom_call" | custom-call | tf_op jit(solution)/shard_map/pallas_call | solution.py:470
  17.4 1.5 %collective-permute-start.5 = (f32[320,128]{1,0:T(8,128)S(1)}, f32[320,128]{1,0:T(8,128)S(1)}, u32[]{:S(2)}, u32[]{:S(2)}) collective-permute-start(f32[320,128]{1,0:T(8,128)S(1)} %get-tuple-element.44), channel_id=1, source_target_pairs={{0,8},{8,16},{16,24},{24,0},{1,9},{9,17},{17,25},{25,1},{2,10},{10... | collective-permute-start | bytes 491528 | tf_op jit(solution)/shard_map/ppermute | solution.py:486
  18.9 1.4 %collective-permute-start.6 = (f32[320,128]{1,0:T(8,128)S(1)}, f32[320,128]{1,0:T(8,128)S(1)}, u32[]{:S(2)}, u32[]{:S(2)}) collective-permute-start(f32[320,128]{1,0:T(8,128)S(1)} %get-tuple-element.45), channel_id=1, source_target_pairs={{0,24},{8,0},{16,8},{24,16},{1,25},{9,1},{17,9},{25,17},{2,26},{10... | collective-permute-start | bytes 491528 | tf_op jit(solution)/shard_map/ppermute | solution.py:486
  20.4 0.7 %shard_map.78 = (f32[2560,128]{1,0:T(8,128)S(1)}, f32[40,128]{1,0:T(8,128)S(1)}) custom-call(f32[2560,128]{1,0:T(8,128)S(1)} %get-tuple-element.47.refs_0_, f32[640,128]{1,0:T(8,128)S(1)} %get-tuple-element.48.refs_1_, f32[640,128]{1,0:T(8,128)S(1)} %get-tuple-element.49.refs_2_, f32[64,128]{1,0:T(8,128)S(1)} %get-tuple-element.50.refs_3_.refs_2_), custom_call_target="tpu_custom_call" | custom-call | tf_op jit(solution)/shard_map/pallas_call | solution.py:470
  21.1 0.9 %collective-permute-start.8 = (f32[40,128]{1,0:T(8,128)S(1)}, f32[40,128]{1,0:T(8,128)S(1)}, u32[]{:S(2)}, u32[]{:S(2)}) collective-permute-start(f32[40,128]{1,0:T(8,128)S(1)} %get-tuple-element.52), channel_id=1, source_target_pairs={{1,2},{2,1},{3,4},{4,3},{5,6},{6,5},{0,16},{7,23},{9,10},{10,9},{1... | collective-permute-start | bytes 61448 | tf_op jit(solution)/shard_map/ppermute | solution.py:503
  22.0 0.8 %collective-permute-start.7 = (f32[40,128]{1,0:T(8,128)S(1)}, f32[40,128]{1,0:T(8,128)S(1)}, u32[]{:S(2)}, u32[]{:S(2)}) collective-permute-start(f32[40,128]{1,0:T(8,128)S(1)} %get-tuple-element.52), channel_id=1, source_target_pairs={{0,1},{1,0},{2,3},{3,2},{4,5},{5,4},{6,7},{7,6},{8,9},{9,8},{10,11... | collective-permute-start | bytes 61448 | tf_op jit(solution)/shard_map/ppermute | solution.py:502
  22.8 1.3 %shard_map.79.refs_1_ = f32[2560,128]{1,0:T(8,128)S(1)} custom-call(f32[2560,128]{1,0:T(8,128)S(1)} %get-tuple-element.51.refs_0_, s32[8,128]{1,0:T(8,128)S(1)} %get-tuple-element.33.refs_1_, f32[64,128]{1,0:T(8,128)S(1)} %get-tuple-element.50.refs_3_.refs_2_), custom_call_target="tpu_custom_call" | custom-call | tf_op jit(solution)/shard_map/pallas_call | solution.py:470
  24.1 1.0 %collective-permute-done.8.refs_6_ = f32[40,128]{1,0:T(8,128)S(1)} collective-permute-done((f32[40,128]{1,0:T(8,128)S(1)}, f32[40,128]{1,0:T(8,128)S(1)}, u32[]{:S(2)}, u32[]{:S(2)}) %collective-permute-start.8) | collective-permute-done | bytes 20512 | tf_op jit(solution)/shard_map/ppermute | solution.py:503
  25.1 0.0 collective-permute-done.7.refs_5_
  25.1 1.2 %shard_map.80 = (f32[2560,128]{1,0:T(8,128)S(1)}, f32[640,128]{1,0:T(8,128)S(1)}) custom-call(f32[2560,128]{1,0:T(8,128)S(1)} %get-tuple-element.51.refs_0_, f32[2560,128]{1,0:T(8,128)S(1)} %shard_map.79.refs_1_, f32[640,128]{1,0:T(8,128)S(1)} %get-tuple-element.35.refs_2_, f32[640,128]{1,0:T(8,128)S(1)} %get-tuple-element.36.refs_3_, ...), custom_call_target="tpu_custom_call" | custom-call | tf_op jit(solution)/shard_map/pallas_call | solution.py:470
  26.3 0.0 collective-permute-done.5.refs_0_
  26.3 0.5 %collective-permute-done.6.refs_1_ = f32[320,128]{1,0:T(8,128)S(1)} collective-permute-done((f32[320,128]{1,0:T(8,128)S(1)}, f32[320,128]{1,0:T(8,128)S(1)}, u32[]{:S(2)}, u32[]{:S(2)}) %collective-permute-start.6) | collective-permute-done | bytes 163872 | tf_op jit(solution)/shard_map/ppermute | solution.py:486
  26.8 2.2 %shard_map.81 = f32[320,8,128]{2,1,0:T(8,128)} custom-call(f32[320,128]{1,0:T(8,128)S(1)} %collective-permute-done.5.refs_0_, f32[320,128]{1,0:T(8,128)S(1)} %collective-permute-done.6.refs_1_, f32[640,128]{1,0:T(8,128)S(1)} %get-tuple-element.46.refs_2_, f32[640,128]{1,0:T(8,128)S(1)} %get-tuple-element.54.refs_3_, ...), custom_call_target="tpu_custom_call" | custom-call | tf_op jit(solution)/shard_map/pallas_call | solution.py:470
  (1 shorter events, 0.0 us)
Async XLA Ops:
  0.0 1.7 %copy-start = (f32[4,80,8,128]{3,2,1,0:T(8,128)S(1)}, f32[4,80,8,128]{3,2,1,0:T(8,128)}, u32[]{:S(2)}) copy-start(f32[4,80,8,128]{3,2,1,0:T(8,128)} %param.7) | copy-start | bytes 3932164
  2.9 8.9 %collective-permute-start.3 = (f32[48,128]{1,0:T(8,128)S(1)}, f32[48,128]{1,0:T(8,128)S(1)}, u32[]{:S(2)}, u32[]{:S(2)}) collective-permute-start(f32[48,128]{1,0:T(8,128)S(1)} %get-tuple-element.38), channel_id=1, source_target_pairs={{1,2},{2,1},{3,4},{4,3},{5,6},{6,5},{0,16},{7,23},{9,10},{10,9},{1... | collective-permute-start | bytes 73736 | tf_op jit(solution)/shard_map/ppermute | solution.py:503
  6.0 5.9 %collective-permute-start.2 = (f32[48,128]{1,0:T(8,128)S(1)}, f32[48,128]{1,0:T(8,128)S(1)}, u32[]{:S(2)}, u32[]{:S(2)}) collective-permute-start(f32[48,128]{1,0:T(8,128)S(1)} %get-tuple-element.38), channel_id=1, source_target_pairs={{0,1},{1,0},{2,3},{3,2},{4,5},{5,4},{6,7},{7,6},{8,9},{9,8},{10,11... | collective-permute-start | bytes 73736 | tf_op jit(solution)/shard_map/ppermute | solution.py:502
  6.2 8.1 %collective-permute-start = (f32[328,128]{1,0:T(8,128)S(1)}, f32[328,128]{1,0:T(8,128)S(1)}, u32[]{:S(2)}, u32[]{:S(2)}) collective-permute-start(f32[328,128]{1,0:T(8,128)S(1)} %get-tuple-element.31.refs_2_), channel_id=1, source_target_pairs={{0,8},{8,16},{16,24},{24,0},{1,9},{9,17},{17,25},{25,1},{2,10},{10... | collective-permute-start | bytes 503816 | tf_op jit(solution)/shard_map/ppermute | solution.py:486
  7.6 9.3 %collective-permute-start.1 = (f32[328,128]{1,0:T(8,128)S(1)}, f32[328,128]{1,0:T(8,128)S(1)}, u32[]{:S(2)}, u32[]{:S(2)}) collective-permute-start(f32[328,128]{1,0:T(8,128)S(1)} %get-tuple-element.32.refs_3_), channel_id=1, source_target_pairs={{0,24},{8,0},{16,8},{24,16},{1,25},{9,1},{17,9},{25,17},{2,26},{10... | collective-permute-start | bytes 503816 | tf_op jit(solution)/shard_map/ppermute | solution.py:486
  9.1 4.0 %collective-permute-start.4 = (f32[8,128]{1,0:T(8,128)S(1)}, f32[8,128]{1,0:T(8,128)S(1)}, u32[]{:S(2)}, u32[]{:S(2)}) collective-permute-start(f32[8,128]{1,0:T(8,128)S(1)} %slice_bitcast_fusion), channel_id=1, source_target_pairs={{0,16},{8,24},{16,0},{24,8},{1,17},{9,25},{17,1},{25,9},{2,18},{10... | collective-permute-start | bytes 12296 | tf_op jit(solution)/shard_map/ppermute | solution.py:486
  17.4 9.0 %collective-permute-start.5 = (f32[320,128]{1,0:T(8,128)S(1)}, f32[320,128]{1,0:T(8,128)S(1)}, u32[]{:S(2)}, u32[]{:S(2)}) collective-permute-start(f32[320,128]{1,0:T(8,128)S(1)} %get-tuple-element.44), channel_id=1, source_target_pairs={{0,8},{8,16},{16,24},{24,0},{1,9},{9,17},{17,25},{25,1},{2,10},{10... | collective-permute-start | bytes 491528 | tf_op jit(solution)/shard_map/ppermute | solution.py:486
  18.9 7.9 %collective-permute-start.6 = (f32[320,128]{1,0:T(8,128)S(1)}, f32[320,128]{1,0:T(8,128)S(1)}, u32[]{:S(2)}, u32[]{:S(2)}) collective-permute-start(f32[320,128]{1,0:T(8,128)S(1)} %get-tuple-element.45), channel_id=1, source_target_pairs={{0,24},{8,0},{16,8},{24,16},{1,25},{9,1},{17,9},{25,17},{2,26},{10... | collective-permute-start | bytes 491528 | tf_op jit(solution)/shard_map/ppermute | solution.py:486
  21.1 4.1 %collective-permute-start.8 = (f32[40,128]{1,0:T(8,128)S(1)}, f32[40,128]{1,0:T(8,128)S(1)}, u32[]{:S(2)}, u32[]{:S(2)}) collective-permute-start(f32[40,128]{1,0:T(8,128)S(1)} %get-tuple-element.52), channel_id=1, source_target_pairs={{1,2},{2,1},{3,4},{4,3},{5,6},{6,5},{0,16},{7,23},{9,10},{10,9},{1... | collective-permute-start | bytes 61448 | tf_op jit(solution)/shard_map/ppermute | solution.py:503
  22.0 3.2 %collective-permute-start.7 = (f32[40,128]{1,0:T(8,128)S(1)}, f32[40,128]{1,0:T(8,128)S(1)}, u32[]{:S(2)}, u32[]{:S(2)}) collective-permute-start(f32[40,128]{1,0:T(8,128)S(1)} %get-tuple-element.52), channel_id=1, source_target_pairs={{0,1},{1,0},{2,3},{3,2},{4,5},{5,4},{6,7},{7,6},{8,9},{9,8},{10,11... | collective-permute-start | bytes 61448 | tf_op jit(solution)/shard_map/ppermute | solution.py:502

commit v8 on v7

--- a/solution.py
+++ b/solution.py
@@ -420,33 +420,26 @@
 
 
 def second_edge_kernel(levels, west_in, east_in, full_ref, packed_ref, gain_ref, down_ref, up_ref, depth_ref,
-                       inner_ref, result_ref, change_ref, columns, bulk_sems, sems):
+                       inner_ref, result_ref, state_ref, change_ref, sems):
     even = sublane_ids() % 2 == 0
+    sub = sublane_ids()
     copies = []
 
-    def bulk(group):
+    def finish(level, change):
+        edge = tile_at(packed_ref, level) + change
         for field in range(FIELDS):
-            piece = pl.ds(field * levels + group * GROUP, GROUP)
-            yield pltpu.make_async_copy(inner_ref.at[piece], result_ref.at[piece], bulk_sems.at[group, field])
-
-    for group in range(levels // GROUP - 1, -1, -1):
-        for copy in bulk(group):
-            copy.start()
-
-    def finish(level, change):
-        columns[level] = tile_at(packed_ref, level) + change
+            side = pltpu.roll(edge, SUB - 1 - 2 * field, 0)
+            rim = jnp.logical_or(sub == 0, sub == SUB - 1)
+            row = field * levels + level
+            put_tile(state_ref, row, jnp.where(rim, side, tile_at(inner_ref, row)))
         if level % GROUP == 0:
-            for copy in bulk(level // GROUP):
-                copy.wait()
             for field in range(FIELDS):
-                for side, column in ((0, SUB - 1), (1, 0)):
-                    copy = pltpu.make_async_copy(
-                        columns.at[pl.ds(level, GROUP), 2 * field + side, :],
-                        result_ref.at[pl.ds(field * levels + level, GROUP), column, :],
-                        sems.at[level // GROUP, 2 * field + side],
-                    )
-                    copy.start()
-                    copies.append(copy)
+                piece = pl.ds((field * levels + level) * SUB, GROUP * SUB)
+                copy = pltpu.make_async_copy(
+                    state_ref.at[piece, :], result_ref.at[piece, :], sems.at[level // GROUP, field]
+                )
+                copy.start()
+                copies.append(copy)
 
     edge_change(
         levels,
@@ -524,7 +517,6 @@
     table = ((levels * lon_dev, lat_dev), f32)
     dma = pltpu.SemaphoreType.DMA
     merged = pltpu.VMEM((groups, SUB, LANE), f32)
-    x = in_vmem(ocean_state.reshape(rows * lon_dev, lat_dev))
 
     east, west, parts, count, rate = call(
         bind(column_kernel, levels, lon_total),
@@ -541,6 +533,7 @@
         ],
         hbm_in=range(7),
     )
+    x = in_vmem(ocean_state.reshape(rows * lon_dev, lat_dev))
     from_west = ring_shift(east, "lon", 1)
     from_east = ring_shift(west, "lon", -1)
     edge, gain, down, up, reply, edge_gain, edge_down, edge_up = call(
@@ -581,11 +574,9 @@
     )
     (result,) = call(
         bind(second_edge_kernel, levels),
-        [((rows, lon_dev, lat_dev), f32)],
-        (from_west, from_east, full, packed, edge_gain, edge_down, edge_up, halo_depth,
-         inner.reshape(rows, lon_dev, lat_dev)),
-        scratch=[pltpu.VMEM(*table), pltpu.VMEM((levels, SUB, LANE), f32), dma((groups, FIELDS)),
-                 dma((groups, 2 * FIELDS))],
+        [state_shape],
+        (from_west, from_east, full, packed, edge_gain, edge_down, edge_up, halo_depth, inner),
+        scratch=[pltpu.VMEM(*state_shape), pltpu.VMEM(*table), dma((groups, FIELDS))],
         hbm_out=(0,),
     )
     return result.reshape(ocean_state.shape)

time: 29.1 us -> 28.5 us (0.979)
  Pallas kernels: 11.1 us -> 10.4 us
    pallas_call x9, Pallas kernels: 11.1 us -> 10.4 us  [call(): pl.pallas_call(kernel, out_shape=[(pltpu.HBM if at in hbm_out else pltpu....]
  transfers between devices with their start and end apart: 9 -> 9, of which waited for: 4 -> 4; matrix products, arithmetic and copies ran while one was open for 0% -> 0% of each run, Pallas kernels for 19% -> 20%
where the time goes in v8:
time: 28.5 us; the launch traced here: 28.3 us
  starting transfers between devices  12.4 us (44%)
  Pallas kernels  10.4 us (36%)
  waiting for transfers between devices  5.31 us (19%)
    pallas_call x9, Pallas kernels, call(): pl.pallas_call(kernel, out_shape=[(pltpu.HBM if at in hbm_out else pltpu....  10.4 us
    ppermute x5, starting transfers between devices, ring_shift(): lax.ppermute(value, axis, [(i, (i + amount) % count) for i in range(count)])  7.42 us
    ppermute x5, waiting for transfers between devices, ring_shift(): lax.ppermute(value, axis, [(i, (i + amount) % count) for i in range(count)])  4.26 us
    ppermute x2, starting transfers between devices, lat_exchange(): swap_b = lax.ppermute(edge, ('lon',) + LAT_AXES, between)  3.97 us
    ppermute x2, waiting for transfers between devices, lat_exchange(): swap_b = lax.ppermute(edge, ('lon',) + LAT_AXES, between)  1.05 us
    ppermute x2, starting transfers between devices, lat_exchange(): swap_a = lax.ppermute(edge, ('lon',) + LAT_AXES, inside)  1.02 us
  transfers between devices with their start and end apart: 9, of which 4 were waited for; matrix products, arithmetic and copies ran while one was open for 0% of the time, Pallas kernels for 20%

profile of v8, /device:TPU:0, one launch (start us, length us, event | category | flops | bytes accessed | tf_op | source)
XLA Modules:
  0.0 28.3 jit_solution(11959003756215096333)
XLA Ops:
  0.0 0.0 copy-start
  0.0 1.6 %shard_map.73 = (f32[328,128]{1,0:T(8,128)S(1)}, f32[328,128]{1,0:T(8,128)S(1)}, f32[4,8,128]{2,1,0:T(8,128)S(1)}, s32[8,128]{1,0:T(8,128)S(1)}, f32[640,128]{1,0:T(8,128)S(1)}) custom-call(f32[320,8,128]{2,1,0:T(8,128)} %bitcast.8, s32[8,128]{1,0:T(8,128)} %refs_1_.1, bf16[4,4,256]{2,1,0:T(4,128)(2,1)} %bitcast.14, bf16[4,256,128]{2,1,0:T(8,128)(2,1)} %bitcast.13, ...), custom_call_target="tpu_custom_call" | custom-call | tf_op jit(solution)/shard_map/pallas_call | solution.py:463
  1.6 0.1 copy-done
  1.7 1.2 %shard_map.75 = (f32[48,128]{1,0:T(8,128)S(1)}, f32[640,128]{1,0:T(8,128)S(1)}, f32[640,128]{1,0:T(8,128)S(1)}, f32[640,128]{1,0:T(8,128)S(1)}, f32[640,128]{1,0...) custom-call(f32[2560,128]{1,0:T(8,128)S(1)} %bitcast.9, ...), custom_call_target="tpu_custom_call" | custom-call | tf_op jit(solution)/shard_map/pallas_call | solution.py:463
  2.9 3.1 %collective-permute-start.3 = (f32[48,128]{1,0:T(8,128)S(1)}, f32[48,128]{1,0:T(8,128)S(1)}, u32[]{:S(2)}, u32[]{:S(2)}) collective-permute-start(f32[48,128]{1,0:T(8,128)S(1)} %get-tuple-element.38), channel_id=1, source_target_pairs={{1,2},{2,1},{3,4},{4,3},{5,6},{6,5},{0,16},{7,23},{9,10},{10,9},{1... | collective-permute-start | bytes 73736 | tf_op jit(solution)/shard_map/ppermute | solution.py:496
  6.0 0.2 collective-permute-start.2
  6.2 1.5 %collective-permute-start = (f32[328,128]{1,0:T(8,128)S(1)}, f32[328,128]{1,0:T(8,128)S(1)}, u32[]{:S(2)}, u32[]{:S(2)}) collective-permute-start(f32[328,128]{1,0:T(8,128)S(1)} %get-tuple-element.31.refs_2_), channel_id=1, source_target_pairs={{0,8},{8,16},{16,24},{24,0},{1,9},{9,17},{17,25},{25,1},{2,10},{10... | collective-permute-start | bytes 503816 | tf_op jit(solution)/shard_map/ppermute | solution.py:479
  7.6 1.4 %collective-permute-start.1 = (f32[328,128]{1,0:T(8,128)S(1)}, f32[328,128]{1,0:T(8,128)S(1)}, u32[]{:S(2)}, u32[]{:S(2)}) collective-permute-start(f32[328,128]{1,0:T(8,128)S(1)} %get-tuple-element.32.refs_3_), channel_id=1, source_target_pairs={{0,24},{8,0},{16,8},{24,16},{1,25},{9,1},{17,9},{25,17},{2,26},{10... | collective-permute-start | bytes 503816 | tf_op jit(solution)/shard_map/ppermute | solution.py:479
  9.1 1.5 %collective-permute-start.4 = (f32[8,128]{1,0:T(8,128)S(1)}, f32[8,128]{1,0:T(8,128)S(1)}, u32[]{:S(2)}, u32[]{:S(2)}) collective-permute-start(f32[8,128]{1,0:T(8,128)S(1)} %slice_bitcast_fusion), channel_id=1, source_target_pairs={{0,16},{8,24},{16,0},{24,8},{1,17},{9,25},{17,1},{25,9},{2,18},{10... | collective-permute-start | bytes 12296 | tf_op jit(solution)/shard_map/ppermute | solution.py:479
  10.6 1.3 %shard_map.74.refs_1_ = f32[2560,128]{1,0:T(8,128)S(1)} custom-call(f32[2560,128]{1,0:T(8,128)S(1)} %bitcast.10, s32[8,128]{1,0:T(8,128)S(1)} %get-tuple-element.33.refs_1_), custom_call_target="tpu_custom_call" | custom-call | tf_op jit(solution)/shard_map/pallas_call | solution.py:463
  11.9 0.0 collective-permute-done.3.refs_6_
  11.9 0.0 collective-permute-done.2.refs_5_
  11.9 1.2 %shard_map.76 = (f32[2560,128]{1,0:T(8,128)S(1)}, f32[640,128]{1,0:T(8,128)S(1)}, s32[8,128]{1,0:T(8,128)S(1)}) custom-call(f32[2560,128]{1,0:T(8,128)S(1)} %bitcast.11, f32[2560,128]{1,0:T(8,128)S(1)} %shard_map.74.refs_1_, f32[640,128]{1,0:T(8,128)S(1)} %get-tuple-element.35.refs_2_, f32[640,128]{1,0:T(8,128)S(1)} %get-tuple-element.36.refs_3_, ...), custom_call_target="tpu_custom_call" | custom-call | tf_op jit(solution)/shard_map/pallas_call | solution.py:463
  13.1 0.0 collective-permute-done.4.refs_9_
  13.1 1.1 %collective-permute-done.refs_0_ = f32[328,128]{1,0:T(8,128)S(1)} collective-permute-done((f32[328,128]{1,0:T(8,128)S(1)}, f32[328,128]{1,0:T(8,128)S(1)}, u32[]{:S(2)}, u32[]{:S(2)}) %collective-permute-start) | collective-permute-done | bytes 167968 | tf_op jit(solution)/shard_map/ppermute | solution.py:479
  14.2 2.7 %collective-permute-done.1.refs_1_ = f32[328,128]{1,0:T(8,128)S(1)} collective-permute-done((f32[328,128]{1,0:T(8,128)S(1)}, f32[328,128]{1,0:T(8,128)S(1)}, u32[]{:S(2)}, u32[]{:S(2)}) %collective-permute-start.1) | collective-permute-done | bytes 167968 | tf_op jit(solution)/shard_map/ppermute | solution.py:479
  16.9 0.5 %shard_map.77 = (f32[320,128]{1,0:T(8,128)S(1)}, f32[320,128]{1,0:T(8,128)S(1)}, f32[640,128]{1,0:T(8,128)S(1)}, f32[640,128]{1,0:T(8,128)S(1)}, f32[64,128]{1,0:T(8,128)S(1)}, /*index=5*/s32[8,128]{1,0:T(8,128)S(1)}) custom-call(f32[328,128]{1,0:T(8,128)S(1)} %collective-permute-done.refs_0_, f32[328,128]{1,0:T(8,128)S(1)} %collective-permute-done.1.refs_1_, ...), custom_call_target="tpu_custom_call" | custom-call | tf_op jit(solution)/shard_map/pallas_call | solution.py:463
  17.4 1.5 %collective-permute-start.5 = (f32[320,128]{1,0:T(8,128)S(1)}, f32[320,128]{1,0:T(8,128)S(1)}, u32[]{:S(2)}, u32[]{:S(2)}) collective-permute-start(f32[320,128]{1,0:T(8,128)S(1)} %get-tuple-element.44), channel_id=1, source_target_pairs={{0,8},{8,16},{16,24},{24,0},{1,9},{9,17},{17,25},{25,1},{2,10},{10... | collective-permute-start | bytes 491528 | tf_op jit(solution)/shard_map/ppermute | solution.py:479
  18.9 1.4 %collective-permute-start.6 = (f32[320,128]{1,0:T(8,128)S(1)}, f32[320,128]{1,0:T(8,128)S(1)}, u32[]{:S(2)}, u32[]{:S(2)}) collective-permute-start(f32[320,128]{1,0:T(8,128)S(1)} %get-tuple-element.45), channel_id=1, source_target_pairs={{0,24},{8,0},{16,8},{24,16},{1,25},{9,1},{17,9},{25,17},{2,26},{10... | collective-permute-start | bytes 491528 | tf_op jit(solution)/shard_map/ppermute | solution.py:479
  20.4 0.7 %shard_map.78 = (f32[2560,128]{1,0:T(8,128)S(1)}, f32[40,128]{1,0:T(8,128)S(1)}) custom-call(f32[2560,128]{1,0:T(8,128)S(1)} %get-tuple-element.47.refs_0_, f32[640,128]{1,0:T(8,128)S(1)} %get-tuple-element.48.refs_1_, f32[640,128]{1,0:T(8,128)S(1)} %get-tuple-element.49.refs_2_, f32[64,128]{1,0:T(8,128)S(1)} %get-tuple-element.50.refs_3_.refs_2_), custom_call_target="tpu_custom_call" | custom-call | tf_op jit(solution)/shard_map/pallas_call | solution.py:463
  21.1 0.9 %collective-permute-start.8 = (f32[40,128]{1,0:T(8,128)S(1)}, f32[40,128]{1,0:T(8,128)S(1)}, u32[]{:S(2)}, u32[]{:S(2)}) collective-permute-start(f32[40,128]{1,0:T(8,128)S(1)} %get-tuple-element.52), channel_id=1, source_target_pairs={{1,2},{2,1},{3,4},{4,3},{5,6},{6,5},{0,16},{7,23},{9,10},{10,9},{1... | collective-permute-start | bytes 61448 | tf_op jit(solution)/shard_map/ppermute | solution.py:496
  22.0 0.8 %collective-permute-start.7 = (f32[40,128]{1,0:T(8,128)S(1)}, f32[40,128]{1,0:T(8,128)S(1)}, u32[]{:S(2)}, u32[]{:S(2)}) collective-permute-start(f32[40,128]{1,0:T(8,128)S(1)} %get-tuple-element.52), channel_id=1, source_target_pairs={{0,1},{1,0},{2,3},{3,2},{4,5},{5,4},{6,7},{7,6},{8,9},{9,8},{10,11... | collective-permute-start | bytes 61448 | tf_op jit(solution)/shard_map/ppermute | solution.py:495
  22.8 1.3 %shard_map.79.refs_1_ = f32[2560,128]{1,0:T(8,128)S(1)} custom-call(f32[2560,128]{1,0:T(8,128)S(1)} %get-tuple-element.51.refs_0_, s32[8,128]{1,0:T(8,128)S(1)} %get-tuple-element.33.refs_1_, f32[64,128]{1,0:T(8,128)S(1)} %get-tuple-element.50.refs_3_.refs_2_), custom_call_target="tpu_custom_call" | custom-call | tf_op jit(solution)/shard_map/pallas_call | solution.py:463
  24.1 1.0 %collective-permute-done.8.refs_6_ = f32[40,128]{1,0:T(8,128)S(1)} collective-permute-done((f32[40,128]{1,0:T(8,128)S(1)}, f32[40,128]{1,0:T(8,128)S(1)}, u32[]{:S(2)}, u32[]{:S(2)}) %collective-permute-start.8) | collective-permute-done | bytes 20512 | tf_op jit(solution)/shard_map/ppermute | solution.py:496
  25.1 0.0 collective-permute-done.7.refs_5_
  25.1 1.2 %shard_map.80 = (f32[2560,128]{1,0:T(8,128)S(1)}, f32[640,128]{1,0:T(8,128)S(1)}) custom-call(f32[2560,128]{1,0:T(8,128)S(1)} %get-tuple-element.51.refs_0_, f32[2560,128]{1,0:T(8,128)S(1)} %shard_map.79.refs_1_, f32[640,128]{1,0:T(8,128)S(1)} %get-tuple-element.35.refs_2_, f32[640,128]{1,0:T(8,128)S(1)} %get-tuple-element.36.refs_3_, ...), custom_call_target="tpu_custom_call" | custom-call | tf_op jit(solution)/shard_map/pallas_call | solution.py:463
  26.3 0.0 collective-permute-done.5.refs_0_
  26.3 0.5 %collective-permute-done.6.refs_1_ = f32[320,128]{1,0:T(8,128)S(1)} collective-permute-done((f32[320,128]{1,0:T(8,128)S(1)}, f32[320,128]{1,0:T(8,128)S(1)}, u32[]{:S(2)}, u32[]{:S(2)}) %collective-permute-start.6) | collective-permute-done | bytes 163872 | tf_op jit(solution)/shard_map/ppermute | solution.py:479
  26.8 1.5 %shard_map.81 = f32[2560,128]{1,0:T(8,128)} custom-call(f32[320,128]{1,0:T(8,128)S(1)} %collective-permute-done.5.refs_0_, f32[320,128]{1,0:T(8,128)S(1)} %collective-permute-done.6.refs_1_, f32[640,128]{1,0:T(8,128)S(1)} %get-tuple-element.46.refs_2_, f32[640,128]{1,0:T(8,128)S(1)} %get-tuple-element.54.refs_3_, ...), custom_call_target="tpu_custom_call" | custom-call | tf_op jit(solution)/shard_map/pallas_call | solution.py:463
  (1 shorter events, 0.0 us)
Async XLA Ops:
  0.0 1.7 %copy-start = (f32[4,80,8,128]{3,2,1,0:T(8,128)S(1)}, f32[4,80,8,128]{3,2,1,0:T(8,128)}, u32[]{:S(2)}) copy-start(f32[4,80,8,128]{3,2,1,0:T(8,128)} %param.7) | copy-start | bytes 3932164
  2.9 8.9 %collective-permute-start.3 = (f32[48,128]{1,0:T(8,128)S(1)}, f32[48,128]{1,0:T(8,128)S(1)}, u32[]{:S(2)}, u32[]{:S(2)}) collective-permute-start(f32[48,128]{1,0:T(8,128)S(1)} %get-tuple-element.38), channel_id=1, source_target_pairs={{1,2},{2,1},{3,4},{4,3},{5,6},{6,5},{0,16},{7,23},{9,10},{10,9},{1... | collective-permute-start | bytes 73736 | tf_op jit(solution)/shard_map/ppermute | solution.py:496
  6.0 5.9 %collective-permute-start.2 = (f32[48,128]{1,0:T(8,128)S(1)}, f32[48,128]{1,0:T(8,128)S(1)}, u32[]{:S(2)}, u32[]{:S(2)}) collective-permute-start(f32[48,128]{1,0:T(8,128)S(1)} %get-tuple-element.38), channel_id=1, source_target_pairs={{0,1},{1,0},{2,3},{3,2},{4,5},{5,4},{6,7},{7,6},{8,9},{9,8},{10,11... | collective-permute-start | bytes 73736 | tf_op jit(solution)/shard_map/ppermute | solution.py:495
  6.2 8.1 %collective-permute-start = (f32[328,128]{1,0:T(8,128)S(1)}, f32[328,128]{1,0:T(8,128)S(1)}, u32[]{:S(2)}, u32[]{:S(2)}) collective-permute-start(f32[328,128]{1,0:T(8,128)S(1)} %get-tuple-element.31.refs_2_), channel_id=1, source_target_pairs={{0,8},{8,16},{16,24},{24,0},{1,9},{9,17},{17,25},{25,1},{2,10},{10... | collective-permute-start | bytes 503816 | tf_op jit(solution)/shard_map/ppermute | solution.py:479
  7.6 9.3 %collective-permute-start.1 = (f32[328,128]{1,0:T(8,128)S(1)}, f32[328,128]{1,0:T(8,128)S(1)}, u32[]{:S(2)}, u32[]{:S(2)}) collective-permute-start(f32[328,128]{1,0:T(8,128)S(1)} %get-tuple-element.32.refs_3_), channel_id=1, source_target_pairs={{0,24},{8,0},{16,8},{24,16},{1,25},{9,1},{17,9},{25,17},{2,26},{10... | collective-permute-start | bytes 503816 | tf_op jit(solution)/shard_map/ppermute | solution.py:479
  9.1 4.0 %collective-permute-start.4 = (f32[8,128]{1,0:T(8,128)S(1)}, f32[8,128]{1,0:T(8,128)S(1)}, u32[]{:S(2)}, u32[]{:S(2)}) collective-permute-start(f32[8,128]{1,0:T(8,128)S(1)} %slice_bitcast_fusion), channel_id=1, source_target_pairs={{0,16},{8,24},{16,0},{24,8},{1,17},{9,25},{17,1},{25,9},{2,18},{10... | collective-permute-start | bytes 12296 | tf_op jit(solution)/shard_map/ppermute | solution.py:479
  17.4 9.0 %collective-permute-start.5 = (f32[320,128]{1,0:T(8,128)S(1)}, f32[320,128]{1,0:T(8,128)S(1)}, u32[]{:S(2)}, u32[]{:S(2)}) collective-permute-start(f32[320,128]{1,0:T(8,128)S(1)} %get-tuple-element.44), channel_id=1, source_target_pairs={{0,8},{8,16},{16,24},{24,0},{1,9},{9,17},{17,25},{25,1},{2,10},{10... | collective-permute-start | bytes 491528 | tf_op jit(solution)/shard_map/ppermute | solution.py:479
  18.9 7.9 %collective-permute-start.6 = (f32[320,128]{1,0:T(8,128)S(1)}, f32[320,128]{1,0:T(8,128)S(1)}, u32[]{:S(2)}, u32[]{:S(2)}) collective-permute-start(f32[320,128]{1,0:T(8,128)S(1)} %get-tuple-element.45), channel_id=1, source_target_pairs={{0,24},{8,0},{16,8},{24,16},{1,25},{9,1},{17,9},{25,17},{2,26},{10... | collective-permute-start | bytes 491528 | tf_op jit(solution)/shard_map/ppermute | solution.py:479
  21.1 4.1 %collective-permute-start.8 = (f32[40,128]{1,0:T(8,128)S(1)}, f32[40,128]{1,0:T(8,128)S(1)}, u32[]{:S(2)}, u32[]{:S(2)}) collective-permute-start(f32[40,128]{1,0:T(8,128)S(1)} %get-tuple-element.52), channel_id=1, source_target_pairs={{1,2},{2,1},{3,4},{4,3},{5,6},{6,5},{0,16},{7,23},{9,10},{10,9},{1... | collective-permute-start | bytes 61448 | tf_op jit(solution)/shard_map/ppermute | solution.py:496
  22.0 3.2 %collective-permute-start.7 = (f32[40,128]{1,0:T(8,128)S(1)}, f32[40,128]{1,0:T(8,128)S(1)}, u32[]{:S(2)}, u32[]{:S(2)}) collective-permute-start(f32[40,128]{1,0:T(8,128)S(1)} %get-tuple-element.52), channel_id=1, source_target_pairs={{0,1},{1,0},{2,3},{3,2},{4,5},{5,4},{6,7},{7,6},{8,9},{9,8},{10,11... | collective-permute-start | bytes 61448 | tf_op jit(solution)/shard_map/ppermute | solution.py:495

commit v9 on v8

--- a/solution.py
+++ b/solution.py
@@ -131,8 +131,7 @@
     later.wait()
 
 
-def prepare_kernel(levels, x_ref, count_ref, rate_ref, edge_ref, gain_ref, down_ref, up_ref, reply_ref,
-                   edge_gain_ref, edge_down_ref, edge_up_ref):
+def prepare_kernel(levels, x_ref, count_ref, rate_ref, edge_ref, gain_ref, down_ref, up_ref, reply_ref):
     pair = ((lane_ids() + 1) % LANE) // 2
     count = count_ref[...]
 
@@ -164,16 +163,6 @@
     lax.fori_loop(0, levels // GROUP, group_body, (zeros(), zeros(), zeros()))
     put_tile(edge_ref, levels // GROUP, count.astype(jnp.float32))
 
-    def back_body(step, following):
-        level = levels - 1 - step
-        value = tile_at(reply_ref, level) + tile_at(up_ref, level) * following
-        put_tile(reply_ref, level, value)
-        return value
-
-    lax.fori_loop(0, levels, back_body, zeros(), unroll=16)
-    for source_ref, out_ref in ((gain_ref, edge_gain_ref), (down_ref, edge_down_ref), (up_ref, edge_up_ref)):
-        pack_edges(levels, 1, source_ref, out_ref)
-
 
 def pack_edges(levels, fields, source_ref, out_ref):
     for side, column in ((0, SUB - 1), (1, 0)):
@@ -185,8 +174,23 @@
                 out_ref[pl.ds(start * SUB + 2 * field + side, SUB, stride=SUB), :] = value
 
 
+def finish_tables(levels, gain_ref, down_ref, up_ref, start_ref, reply_ref, edge_gain_ref, edge_down_ref, edge_up_ref):
+    def back_body(step, following):
+        level = levels - 1 - step
+        value = tile_at(start_ref, level) + tile_at(up_ref, level) * following
+        put_tile(reply_ref, level, value)
+        return value
+
+    lax.fori_loop(0, levels, back_body, zeros(), unroll=16)
+    for source_ref, out_ref in ((gain_ref, edge_gain_ref), (down_ref, edge_down_ref), (up_ref, edge_up_ref)):
+        pack_edges(levels, 1, source_ref, out_ref)
+
+
 def explicit_kernel(levels, later, x_ref, count_ref, *rest):
-    force_ref, out_ref = rest if later else (None, rest[0])
+    if later:
+        force_ref, out_ref = rest
+    else:
+        tables, (out_ref, *finished) = rest[:4], rest[4:]
     sub = sublane_ids()
     lane = lane_ids()
     lat_total = LANE * lax.axis_size("lat") * lax.axis_size("comp")
@@ -250,6 +254,8 @@
         return carry
 
     lax.fori_loop(0, levels // GROUP, group_body, (zeros(),) * 4)
+    if not later:
+        finish_tables(levels, *tables, *finished)
 
 
 def solve_kernel(levels, later, x_ref, explicit_ref, gain_ref, down_ref, up_ref, swap_a, swap_b, *rest):
@@ -536,16 +542,18 @@
     x = in_vmem(ocean_state.reshape(rows * lon_dev, lat_dev))
     from_west = ring_shift(east, "lon", 1)
     from_east = ring_shift(west, "lon", -1)
-    edge, gain, down, up, reply, edge_gain, edge_down, edge_up = call(
+    edge, gain, down, up, start = call(
         bind(prepare_kernel, levels),
-        [(((groups + 1) * SUB, lat_dev), f32)] + [table] * 7,
+        [(((groups + 1) * SUB, lat_dev), f32)] + [table] * 4,
         (x, count, rate),
     )
     swap_a, swap_b = lat_exchange(edge)
     others = []
     for s in range(2, lon_total - 1):
         others.append(ring_shift(parts[s], "lon", s))
-    (explicit,) = call(bind(explicit_kernel, levels, False), [state_shape], (x, count))
+    explicit, reply, edge_gain, edge_down, edge_up = call(
+        bind(explicit_kernel, levels, False), [state_shape] + [table] * 4, (x, count, gain, down, up, start)
+    )
     inner, packed, lat_depth = call(
         bind(solve_kernel, levels, False),
         [state_shape, table, ((SUB, LANE), i32)],

time: 28.5 us -> 28 us (0.982)
  waiting for transfers between devices: 5.31 us -> 4.98 us
    ppermute x5, waiting for transfers between devices: 4.26 us -> 3.93 us  [ring_shift(): lax.ppermute(value, axis, [(i, (i + amount) % count) for i in range(count)])]
  transfers between devices with their start and end apart: 9 -> 9, of which waited for: 4 -> 4; matrix products, arithmetic and copies ran while one was open for 0% -> 0% of each run, Pallas kernels for 20% -> 21%
where the time goes in v9:
time: 28 us; the launch traced here: 27.8 us
  starting transfers between devices  12.4 us (44%)
  Pallas kernels  10.2 us (36%)
  waiting for transfers between devices  4.98 us (18%)
    pallas_call x9, Pallas kernels, call(): pl.pallas_call(kernel, out_shape=[(pltpu.HBM if at in hbm_out else pltpu....  10.2 us
    ppermute x5, starting transfers between devices, ring_shift(): lax.ppermute(value, axis, [(i, (i + amount) % count) for i in range(count)])  7.42 us
    ppermute x2, starting transfers between devices, lat_exchange(): swap_b = lax.ppermute(edge, ('lon',) + LAT_AXES, between)  3.97 us
    ppermute x5, waiting for transfers between devices, ring_shift(): lax.ppermute(value, axis, [(i, (i + amount) % count) for i in range(count)])  3.93 us
    ppermute x2, waiting for transfers between devices, lat_exchange(): swap_b = lax.ppermute(edge, ('lon',) + LAT_AXES, between)  1.05 us
    ppermute x2, starting transfers between devices, lat_exchange(): swap_a = lax.ppermute(edge, ('lon',) + LAT_AXES, inside)  1.02 us
  transfers between devices with their start and end apart: 9, of which 4 were waited for; matrix products, arithmetic and copies ran while one was open for 0% of the time, Pallas kernels for 21%

profile of v9, /device:TPU:0, one launch (start us, length us, event | category | flops | bytes accessed | tf_op | source)
XLA Modules:
  0.0 27.8 jit_solution(18430034682501916822)
XLA Ops:
  0.0 0.0 copy-start
  0.0 1.6 %shard_map.73 = (f32[328,128]{1,0:T(8,128)S(1)}, f32[328,128]{1,0:T(8,128)S(1)}, f32[4,8,128]{2,1,0:T(8,128)S(1)}, s32[8,128]{1,0:T(8,128)S(1)}, f32[640,128]{1,0:T(8,128)S(1)}) custom-call(f32[320,8,128]{2,1,0:T(8,128)} %bitcast.8, s32[8,128]{1,0:T(8,128)} %refs_1_.1, bf16[4,4,256]{2,1,0:T(4,128)(2,1)} %bitcast.14, bf16[4,256,128]{2,1,0:T(8,128)(2,1)} %bitcast.13, ...), custom_call_target="tpu_custom_call" | custom-call | tf_op jit(solution)/shard_map/pallas_call | solution.py:469
  1.6 0.1 copy-done
  1.7 0.8 %shard_map.74 = (f32[48,128]{1,0:T(8,128)S(1)}, f32[640,128]{1,0:T(8,128)S(1)}, f32[640,128]{1,0:T(8,128)S(1)}, f32[640,128]{1,0:T(8,128)S(1)}, f32[640,128]{1,0:T(8,128)S(1)}) custom-call(f32[2560,128]{1,0:T(8,128)S(1)} %bitcast.9, s32[8,128]{1,0:T(8,128)S(1)} %get-tuple-element.35.refs_1_, f32[640,128]{1,0:T(8,128)S(1)} %get-tuple-element.36.refs_2_), custom_call_target="tpu_custom_call" | custom-call | tf_op jit(solution)/shard_map/pallas_call | solution.py:469
  2.4 3.1 %collective-permute-start.3 = (f32[48,128]{1,0:T(8,128)S(1)}, f32[48,128]{1,0:T(8,128)S(1)}, u32[]{:S(2)}, u32[]{:S(2)}) collective-permute-start(f32[48,128]{1,0:T(8,128)S(1)} %get-tuple-element.42), channel_id=1, source_target_pairs={{1,2},{2,1},{3,4},{4,3},{5,6},{6,5},{0,16},{7,23},{9,10},{10,9},{1... | collective-permute-start | bytes 73736 | tf_op jit(solution)/shard_map/ppermute | solution.py:502
  5.5 0.2 collective-permute-start.2
  5.7 1.5 %collective-permute-start = (f32[328,128]{1,0:T(8,128)S(1)}, f32[328,128]{1,0:T(8,128)S(1)}, u32[]{:S(2)}, u32[]{:S(2)}) collective-permute-start(f32[328,128]{1,0:T(8,128)S(1)} %get-tuple-element.33.refs_2_), channel_id=1, source_target_pairs={{0,8},{8,16},{16,24},{24,0},{1,9},{9,17},{17,25},{25,1},{2,10},{10... | collective-permute-start | bytes 503816 | tf_op jit(solution)/shard_map/ppermute | solution.py:485
  7.2 1.4 %collective-permute-start.1 = (f32[328,128]{1,0:T(8,128)S(1)}, f32[328,128]{1,0:T(8,128)S(1)}, u32[]{:S(2)}, u32[]{:S(2)}) collective-permute-start(f32[328,128]{1,0:T(8,128)S(1)} %get-tuple-element.34.refs_3_), channel_id=1, source_target_pairs={{0,24},{8,0},{16,8},{24,16},{1,25},{9,1},{17,9},{25,17},{2,26},{10... | collective-permute-start | bytes 503816 | tf_op jit(solution)/shard_map/ppermute | solution.py:485
  8.6 1.5 %collective-permute-start.4 = (f32[8,128]{1,0:T(8,128)S(1)}, f32[8,128]{1,0:T(8,128)S(1)}, u32[]{:S(2)}, u32[]{:S(2)}) collective-permute-start(f32[8,128]{1,0:T(8,128)S(1)} %slice_bitcast_fusion), channel_id=1, source_target_pairs={{0,16},{8,24},{16,0},{24,8},{1,17},{9,25},{17,1},{25,9},{2,18},{10... | collective-permute-start | bytes 12296 | tf_op jit(solution)/shard_map/ppermute | solution.py:485
  10.1 1.6 %shard_map.75 = (f32[2560,128]{1,0:T(8,128)S(1)}, f32[640,128]{1,0:T(8,128)S(1)}, f32[640,128]{1,0:T(8,128)S(1)}, f32[640,128]{1,0:T(8,128)S(1)}, f32[640,128]{1,0:T(8,128)S(1)}) custom-call(f32[2560,128]{1,0:T(8,128)S(1)} %bitcast.10, s32[8,128]{1,0:T(8,128)S(1)} %get-tuple-element.35.refs_1_, f32[640,128]{1,0:T(8,128)S(1)} %get-tuple-element.37.refs_2_, ...), custom_call_target="tpu_custom_call" | custom-call | tf_op jit(solution)/shard_map/pallas_call | solution.py:469
  11.7 0.0 collective-permute-done.3.refs_6_
  11.7 0.0 collective-permute-done.2.refs_5_
  11.7 1.2 %shard_map.76 = (f32[2560,128]{1,0:T(8,128)S(1)}, f32[640,128]{1,0:T(8,128)S(1)}, s32[8,128]{1,0:T(8,128)S(1)}) custom-call(f32[2560,128]{1,0:T(8,128)S(1)} %bitcast.11, f32[2560,128]{1,0:T(8,128)S(1)} %get-tuple-element.41.refs_1_, f32[640,128]{1,0:T(8,128)S(1)} %get-tuple-element.37.refs_2_, f32[640,128]{1,0:T(8,128)S(1)} %get-tuple-element.38.refs_3_, ...), custom_call_target="tpu_custom_call" | custom-call | tf_op jit(solution)/shard_map/pallas_call | solution.py:469
  13.0 0.0 collective-permute-done.4.refs_9_
  13.0 0.8 %collective-permute-done.refs_0_ = f32[328,128]{1,0:T(8,128)S(1)} collective-permute-done((f32[328,128]{1,0:T(8,128)S(1)}, f32[328,128]{1,0:T(8,128)S(1)}, u32[]{:S(2)}, u32[]{:S(2)}) %collective-permute-start) | collective-permute-done | bytes 167968 | tf_op jit(solution)/shard_map/ppermute | solution.py:485
  13.7 2.7 %collective-permute-done.1.refs_1_ = f32[328,128]{1,0:T(8,128)S(1)} collective-permute-done((f32[328,128]{1,0:T(8,128)S(1)}, f32[328,128]{1,0:T(8,128)S(1)}, u32[]{:S(2)}, u32[]{:S(2)}) %collective-permute-start.1) | collective-permute-done | bytes 167968 | tf_op jit(solution)/shard_map/ppermute | solution.py:485
  16.4 0.5 %shard_map.77 = (f32[320,128]{1,0:T(8,128)S(1)}, f32[320,128]{1,0:T(8,128)S(1)}, f32[640,128]{1,0:T(8,128)S(1)}, f32[640,128]{1,0:T(8,128)S(1)}, f32[64,128]{1,0:T(8,128)S(1)}, /*index=5*/s32[8,128]{1,0:T(8,128)S(1)}) custom-call(f32[328,128]{1,0:T(8,128)S(1)} %collective-permute-done.refs_0_, f32[328,128]{1,0:T(8,128)S(1)} %collective-permute-done.1.refs_1_, ...), custom_call_target="tpu_custom_call" | custom-call | tf_op jit(solution)/shard_map/pallas_call | solution.py:469
  16.9 1.5 %collective-permute-start.5 = (f32[320,128]{1,0:T(8,128)S(1)}, f32[320,128]{1,0:T(8,128)S(1)}, u32[]{:S(2)}, u32[]{:S(2)}) collective-permute-start(f32[320,128]{1,0:T(8,128)S(1)} %get-tuple-element.48), channel_id=1, source_target_pairs={{0,8},{8,16},{16,24},{24,0},{1,9},{9,17},{17,25},{25,1},{2,10},{10... | collective-permute-start | bytes 491528 | tf_op jit(solution)/shard_map/ppermute | solution.py:485
  18.4 1.4 %collective-permute-start.6 = (f32[320,128]{1,0:T(8,128)S(1)}, f32[320,128]{1,0:T(8,128)S(1)}, u32[]{:S(2)}, u32[]{:S(2)}) collective-permute-start(f32[320,128]{1,0:T(8,128)S(1)} %get-tuple-element.49), channel_id=1, source_target_pairs={{0,24},{8,0},{16,8},{24,16},{1,25},{9,1},{17,9},{25,17},{2,26},{10... | collective-permute-start | bytes 491528 | tf_op jit(solution)/shard_map/ppermute | solution.py:485
  19.9 0.7 %shard_map.78 = (f32[2560,128]{1,0:T(8,128)S(1)}, f32[40,128]{1,0:T(8,128)S(1)}) custom-call(f32[2560,128]{1,0:T(8,128)S(1)} %get-tuple-element.51.refs_0_, f32[640,128]{1,0:T(8,128)S(1)} %get-tuple-element.52.refs_1_, f32[640,128]{1,0:T(8,128)S(1)} %get-tuple-element.53.refs_2_, f32[64,128]{1,0:T(8,128)S(1)} %get-tuple-element.54.refs_3_.refs_2_), custom_call_target="tpu_custom_call" | custom-call | tf_op jit(solution)/shard_map/pallas_call | solution.py:469
  20.6 0.9 %collective-permute-start.8 = (f32[40,128]{1,0:T(8,128)S(1)}, f32[40,128]{1,0:T(8,128)S(1)}, u32[]{:S(2)}, u32[]{:S(2)}) collective-permute-start(f32[40,128]{1,0:T(8,128)S(1)} %get-tuple-element.56), channel_id=1, source_target_pairs={{1,2},{2,1},{3,4},{4,3},{5,6},{6,5},{0,16},{7,23},{9,10},{10,9},{1... | collective-permute-start | bytes 61448 | tf_op jit(solution)/shard_map/ppermute | solution.py:502
  21.5 0.8 %collective-permute-start.7 = (f32[40,128]{1,0:T(8,128)S(1)}, f32[40,128]{1,0:T(8,128)S(1)}, u32[]{:S(2)}, u32[]{:S(2)}) collective-permute-start(f32[40,128]{1,0:T(8,128)S(1)} %get-tuple-element.56), channel_id=1, source_target_pairs={{0,1},{1,0},{2,3},{3,2},{4,5},{5,4},{6,7},{7,6},{8,9},{9,8},{10,11... | collective-permute-start | bytes 61448 | tf_op jit(solution)/shard_map/ppermute | solution.py:501
  22.3 1.3 %shard_map.79.refs_1_ = f32[2560,128]{1,0:T(8,128)S(1)} custom-call(f32[2560,128]{1,0:T(8,128)S(1)} %get-tuple-element.55.refs_0_, s32[8,128]{1,0:T(8,128)S(1)} %get-tuple-element.35.refs_1_, f32[64,128]{1,0:T(8,128)S(1)} %get-tuple-element.54.refs_3_.refs_2_), custom_call_target="tpu_custom_call" | custom-call | tf_op jit(solution)/shard_map/pallas_call | solution.py:469
  23.6 1.0 %collective-permute-done.8.refs_6_ = f32[40,128]{1,0:T(8,128)S(1)} collective-permute-done((f32[40,128]{1,0:T(8,128)S(1)}, f32[40,128]{1,0:T(8,128)S(1)}, u32[]{:S(2)}, u32[]{:S(2)}) %collective-permute-start.8) | collective-permute-done | bytes 20512 | tf_op jit(solution)/shard_map/ppermute | solution.py:502
  24.6 0.0 collective-permute-done.7.refs_5_
  24.7 1.2 %shard_map.80 = (f32[2560,128]{1,0:T(8,128)S(1)}, f32[640,128]{1,0:T(8,128)S(1)}) custom-call(f32[2560,128]{1,0:T(8,128)S(1)} %get-tuple-element.55.refs_0_, f32[2560,128]{1,0:T(8,128)S(1)} %shard_map.79.refs_1_, f32[640,128]{1,0:T(8,128)S(1)} %get-tuple-element.37.refs_2_, f32[640,128]{1,0:T(8,128)S(1)} %get-tuple-element.38.refs_3_, ...), custom_call_target="tpu_custom_call" | custom-call | tf_op jit(solution)/shard_map/pallas_call | solution.py:469
  25.9 0.0 collective-permute-done.5.refs_0_
  25.9 0.5 %collective-permute-done.6.refs_1_ = f32[320,128]{1,0:T(8,128)S(1)} collective-permute-done((f32[320,128]{1,0:T(8,128)S(1)}, f32[320,128]{1,0:T(8,128)S(1)}, u32[]{:S(2)}, u32[]{:S(2)}) %collective-permute-start.6) | collective-permute-done | bytes 163872 | tf_op jit(solution)/shard_map/ppermute | solution.py:485
  26.3 1.5 %shard_map.81 = f32[2560,128]{1,0:T(8,128)} custom-call(f32[320,128]{1,0:T(8,128)S(1)} %collective-permute-done.5.refs_0_, f32[320,128]{1,0:T(8,128)S(1)} %collective-permute-done.6.refs_1_, f32[640,128]{1,0:T(8,128)S(1)} %get-tuple-element.50.refs_2_, f32[640,128]{1,0:T(8,128)S(1)} %get-tuple-element.58.refs_3_, ...), custom_call_target="tpu_custom_call" | custom-call | tf_op jit(solution)/shard_map/pallas_call | solution.py:469
  (1 shorter events, 0.0 us)
Async XLA Ops:
  0.0 1.7 %copy-start = (f32[4,80,8,128]{3,2,1,0:T(8,128)S(1)}, f32[4,80,8,128]{3,2,1,0:T(8,128)}, u32[]{:S(2)}) copy-start(f32[4,80,8,128]{3,2,1,0:T(8,128)} %param.7) | copy-start | bytes 3932164
  2.4 9.3 %collective-permute-start.3 = (f32[48,128]{1,0:T(8,128)S(1)}, f32[48,128]{1,0:T(8,128)S(1)}, u32[]{:S(2)}, u32[]{:S(2)}) collective-permute-start(f32[48,128]{1,0:T(8,128)S(1)} %get-tuple-element.42), channel_id=1, source_target_pairs={{1,2},{2,1},{3,4},{4,3},{5,6},{6,5},{0,16},{7,23},{9,10},{10,9},{1... | collective-permute-start | bytes 73736 | tf_op jit(solution)/shard_map/ppermute | solution.py:502
  5.5 6.2 %collective-permute-start.2 = (f32[48,128]{1,0:T(8,128)S(1)}, f32[48,128]{1,0:T(8,128)S(1)}, u32[]{:S(2)}, u32[]{:S(2)}) collective-permute-start(f32[48,128]{1,0:T(8,128)S(1)} %get-tuple-element.42), channel_id=1, source_target_pairs={{0,1},{1,0},{2,3},{3,2},{4,5},{5,4},{6,7},{7,6},{8,9},{9,8},{10,11... | collective-permute-start | bytes 73736 | tf_op jit(solution)/shard_map/ppermute | solution.py:501
  5.7 8.1 %collective-permute-start = (f32[328,128]{1,0:T(8,128)S(1)}, f32[328,128]{1,0:T(8,128)S(1)}, u32[]{:S(2)}, u32[]{:S(2)}) collective-permute-start(f32[328,128]{1,0:T(8,128)S(1)} %get-tuple-element.33.refs_2_), channel_id=1, source_target_pairs={{0,8},{8,16},{16,24},{24,0},{1,9},{9,17},{17,25},{25,1},{2,10},{10... | collective-permute-start | bytes 503816 | tf_op jit(solution)/shard_map/ppermute | solution.py:485
  7.2 9.3 %collective-permute-start.1 = (f32[328,128]{1,0:T(8,128)S(1)}, f32[328,128]{1,0:T(8,128)S(1)}, u32[]{:S(2)}, u32[]{:S(2)}) collective-permute-start(f32[328,128]{1,0:T(8,128)S(1)} %get-tuple-element.34.refs_3_), channel_id=1, source_target_pairs={{0,24},{8,0},{16,8},{24,16},{1,25},{9,1},{17,9},{25,17},{2,26},{10... | collective-permute-start | bytes 503816 | tf_op jit(solution)/shard_map/ppermute | solution.py:485
  8.6 4.4 %collective-permute-start.4 = (f32[8,128]{1,0:T(8,128)S(1)}, f32[8,128]{1,0:T(8,128)S(1)}, u32[]{:S(2)}, u32[]{:S(2)}) collective-permute-start(f32[8,128]{1,0:T(8,128)S(1)} %slice_bitcast_fusion), channel_id=1, source_target_pairs={{0,16},{8,24},{16,0},{24,8},{1,17},{9,25},{17,1},{25,9},{2,18},{10... | collective-permute-start | bytes 12296 | tf_op jit(solution)/shard_map/ppermute | solution.py:485
  16.9 9.0 %collective-permute-start.5 = (f32[320,128]{1,0:T(8,128)S(1)}, f32[320,128]{1,0:T(8,128)S(1)}, u32[]{:S(2)}, u32[]{:S(2)}) collective-permute-start(f32[320,128]{1,0:T(8,128)S(1)} %get-tuple-element.48), channel_id=1, source_target_pairs={{0,8},{8,16},{16,24},{24,0},{1,9},{9,17},{17,25},{25,1},{2,10},{10... | collective-permute-start | bytes 491528 | tf_op jit(solution)/shard_map/ppermute | solution.py:485
  18.4 7.9 %collective-permute-start.6 = (f32[320,128]{1,0:T(8,128)S(1)}, f32[320,128]{1,0:T(8,128)S(1)}, u32[]{:S(2)}, u32[]{:S(2)}) collective-permute-start(f32[320,128]{1,0:T(8,128)S(1)} %get-tuple-element.49), channel_id=1, source_target_pairs={{0,24},{8,0},{16,8},{24,16},{1,25},{9,1},{17,9},{25,17},{2,26},{10... | collective-permute-start | bytes 491528 | tf_op jit(solution)/shard_map/ppermute | solution.py:485
  20.6 4.1 %collective-permute-start.8 = (f32[40,128]{1,0:T(8,128)S(1)}, f32[40,128]{1,0:T(8,128)S(1)}, u32[]{:S(2)}, u32[]{:S(2)}) collective-permute-start(f32[40,128]{1,0:T(8,128)S(1)} %get-tuple-element.56), channel_id=1, source_target_pairs={{1,2},{2,1},{3,4},{4,3},{5,6},{6,5},{0,16},{7,23},{9,10},{10,9},{1... | collective-permute-start | bytes 61448 | tf_op jit(solution)/shard_map/ppermute | solution.py:502
  21.5 3.2 %collective-permute-start.7 = (f32[40,128]{1,0:T(8,128)S(1)}, f32[40,128]{1,0:T(8,128)S(1)}, u32[]{:S(2)}, u32[]{:S(2)}) collective-permute-start(f32[40,128]{1,0:T(8,128)S(1)} %get-tuple-element.56), channel_id=1, source_target_pairs={{0,1},{1,0},{2,3},{3,2},{4,5},{5,4},{6,7},{7,6},{8,9},{9,8},{10,11... | collective-permute-start | bytes 61448 | tf_op jit(solution)/shard_map/ppermute | solution.py:501

commit v10 on v9

--- a/solution.py
+++ b/solution.py
@@ -98,24 +98,11 @@
         pltpu.make_async_copy(x_ref.at[:, 0, :], columns.at[1], sems.at[1]),
     ]
     later = pltpu.make_async_copy(rate_hbm, rate_ref, sems.at[7])
-    for copy in sides + copies + [later]:
+    for copy in copies[:1] + sides + copies[1:] + [later]:
         copy.start()
-    for copy in copies:
-        copy.wait()
-
-    blocks = flux_ref.shape[0]
-    for block in range(blocks):
-        partial = jnp.dot(flux_ref[block], weight_ref[block], preferred_element_type=jnp.float32)
-        slot = slot_ref[0, block].astype(jnp.float32)
-        tile = jnp.concatenate([partial, jnp.full((SUB - FIELDS, LANE), slot, jnp.float32)], axis=0)
-        shift = lax.rem(target_ref[0, block] - me + lon_total, lon_total)
-        parts_ref[shift] = tile
-
+    copies[0].wait()
     count = count_ref[...]
-    count_f = count.astype(jnp.float32)
-    for side, (out_ref, column, shift) in enumerate(
-        ((east_ref, SUB - 1, 1), (west_ref, 0, lon_total - 1))
-    ):
+    for side, (out_ref, column) in enumerate(((east_ref, SUB - 1), (west_ref, 0))):
         sides[side].wait()
         depth = spread(count[column:column + 1, :])
         for field in range(FIELDS):
@@ -125,6 +112,19 @@
                 upper = start // half
                 row = (start - upper * half) * SUB + 2 * field + upper
                 out_ref[pl.ds(row, SUB, stride=SUB), :] = value
+    for copy in copies[1:]:
+        copy.wait()
+
+    blocks = flux_ref.shape[0]
+    for block in range(blocks):
+        partial = jnp.dot(flux_ref[block], weight_ref[block], preferred_element_type=jnp.float32)
+        slot = slot_ref[0, block].astype(jnp.float32)
+        tile = jnp.concatenate([partial, jnp.full((SUB - FIELDS, LANE), slot, jnp.float32)], axis=0)
+        shift = lax.rem(target_ref[0, block] - me + lon_total, lon_total)
+        parts_ref[shift] = tile
+
+    count_f = count.astype(jnp.float32)
+    for out_ref, column, shift in ((east_ref, SUB - 1, 1), (west_ref, 0, lon_total - 1)):
         out_ref[pl.ds(half * SUB, EXTRA), :] = jnp.where(
             sub == COUNT_ROW, spread(count_f[column:column + 1, :]), parts_ref[shift]
         )

time: 28 us -> 28 us (level)
  no operation moved by 1% of the time
where the time goes in v10:
time: 28 us; the launch traced here: 27.8 us
  starting transfers between devices  12.4 us (44%)
  Pallas kernels  10.2 us (36%)
  waiting for transfers between devices  4.98 us (18%)
    pallas_call x9, Pallas kernels, call(): pl.pallas_call(kernel, out_shape=[(pltpu.HBM if at in hbm_out else pltpu....  10.2 us
    ppermute x5, starting transfers between devices, ring_shift(): lax.ppermute(value, axis, [(i, (i + amount) % count) for i in range(count)])  7.42 us
    ppermute x2, starting transfers between devices, lat_exchange(): swap_b = lax.ppermute(edge, ('lon',) + LAT_AXES, between)  3.97 us
    ppermute x5, waiting for transfers between devices, ring_shift(): lax.ppermute(value, axis, [(i, (i + amount) % count) for i in range(count)])  3.93 us
    ppermute x2, waiting for transfers between devices, lat_exchange(): swap_b = lax.ppermute(edge, ('lon',) + LAT_AXES, between)  1.05 us
    ppermute x2, starting transfers between devices, lat_exchange(): swap_a = lax.ppermute(edge, ('lon',) + LAT_AXES, inside)  1.02 us
  transfers between devices with their start and end apart: 9, of which 4 were waited for; matrix products, arithmetic and copies ran while one was open for 0% of the time, Pallas kernels for 21%

profile of v10, /device:TPU:0, one launch (start us, length us, event | category | flops | bytes accessed | tf_op | source)
XLA Modules:
  0.0 27.8 jit_solution(2172859337844308633)
XLA Ops:
  0.0 0.0 copy-start
  0.0 1.5 %shard_map.73 = (f32[328,128]{1,0:T(8,128)S(1)}, f32[328,128]{1,0:T(8,128)S(1)}, f32[4,8,128]{2,1,0:T(8,128)S(1)}, s32[8,128]{1,0:T(8,128)S(1)}, f32[640,128]{1,0:T(8,128)S(1)}) custom-call(f32[320,8,128]{2,1,0:T(8,128)} %bitcast.8, s32[8,128]{1,0:T(8,128)} %refs_1_.1, bf16[4,4,256]{2,1,0:T(4,128)(2,1)} %bitcast.14, bf16[4,256,128]{2,1,0:T(8,128)(2,1)} %bitcast.13, ...), custom_call_target="tpu_custom_call" | custom-call | tf_op jit(solution)/shard_map/pallas_call | solution.py:469
  1.5 0.2 copy-done
  1.7 0.8 %shard_map.74 = (f32[48,128]{1,0:T(8,128)S(1)}, f32[640,128]{1,0:T(8,128)S(1)}, f32[640,128]{1,0:T(8,128)S(1)}, f32[640,128]{1,0:T(8,128)S(1)}, f32[640,128]{1,0:T(8,128)S(1)}) custom-call(f32[2560,128]{1,0:T(8,128)S(1)} %bitcast.9, s32[8,128]{1,0:T(8,128)S(1)} %get-tuple-element.35.refs_1_, f32[640,128]{1,0:T(8,128)S(1)} %get-tuple-element.36.refs_2_), custom_call_target="tpu_custom_call" | custom-call | tf_op jit(solution)/shard_map/pallas_call | solution.py:469
  2.4 3.1 %collective-permute-start.3 = (f32[48,128]{1,0:T(8,128)S(1)}, f32[48,128]{1,0:T(8,128)S(1)}, u32[]{:S(2)}, u32[]{:S(2)}) collective-permute-start(f32[48,128]{1,0:T(8,128)S(1)} %get-tuple-element.42), channel_id=1, source_target_pairs={{1,2},{2,1},{3,4},{4,3},{5,6},{6,5},{0,16},{7,23},{9,10},{10,9},{1... | collective-permute-start | bytes 73736 | tf_op jit(solution)/shard_map/ppermute | solution.py:502
  5.5 0.2 collective-permute-start.2
  5.7 1.5 %collective-permute-start = (f32[328,128]{1,0:T(8,128)S(1)}, f32[328,128]{1,0:T(8,128)S(1)}, u32[]{:S(2)}, u32[]{:S(2)}) collective-permute-start(f32[328,128]{1,0:T(8,128)S(1)} %get-tuple-element.33.refs_2_), channel_id=1, source_target_pairs={{0,8},{8,16},{16,24},{24,0},{1,9},{9,17},{17,25},{25,1},{2,10},{10... | collective-permute-start | bytes 503816 | tf_op jit(solution)/shard_map/ppermute | solution.py:485
  7.2 1.4 %collective-permute-start.1 = (f32[328,128]{1,0:T(8,128)S(1)}, f32[328,128]{1,0:T(8,128)S(1)}, u32[]{:S(2)}, u32[]{:S(2)}) collective-permute-start(f32[328,128]{1,0:T(8,128)S(1)} %get-tuple-element.34.refs_3_), channel_id=1, source_target_pairs={{0,24},{8,0},{16,8},{24,16},{1,25},{9,1},{17,9},{25,17},{2,26},{10... | collective-permute-start | bytes 503816 | tf_op jit(solution)/shard_map/ppermute | solution.py:485
  8.6 1.5 %collective-permute-start.4 = (f32[8,128]{1,0:T(8,128)S(1)}, f32[8,128]{1,0:T(8,128)S(1)}, u32[]{:S(2)}, u32[]{:S(2)}) collective-permute-start(f32[8,128]{1,0:T(8,128)S(1)} %slice_bitcast_fusion), channel_id=1, source_target_pairs={{0,16},{8,24},{16,0},{24,8},{1,17},{9,25},{17,1},{25,9},{2,18},{10... | collective-permute-start | bytes 12296 | tf_op jit(solution)/shard_map/ppermute | solution.py:485
  10.1 1.6 %shard_map.75 = (f32[2560,128]{1,0:T(8,128)S(1)}, f32[640,128]{1,0:T(8,128)S(1)}, f32[640,128]{1,0:T(8,128)S(1)}, f32[640,128]{1,0:T(8,128)S(1)}, f32[640,128]{1,0:T(8,128)S(1)}) custom-call(f32[2560,128]{1,0:T(8,128)S(1)} %bitcast.10, s32[8,128]{1,0:T(8,128)S(1)} %get-tuple-element.35.refs_1_, f32[640,128]{1,0:T(8,128)S(1)} %get-tuple-element.37.refs_2_, ...), custom_call_target="tpu_custom_call" | custom-call | tf_op jit(solution)/shard_map/pallas_call | solution.py:469
  11.7 0.0 collective-permute-done.3.refs_6_
  11.7 0.0 collective-permute-done.2.refs_5_
  11.7 1.2 %shard_map.76 = (f32[2560,128]{1,0:T(8,128)S(1)}, f32[640,128]{1,0:T(8,128)S(1)}, s32[8,128]{1,0:T(8,128)S(1)}) custom-call(f32[2560,128]{1,0:T(8,128)S(1)} %bitcast.11, f32[2560,128]{1,0:T(8,128)S(1)} %get-tuple-element.41.refs_1_, f32[640,128]{1,0:T(8,128)S(1)} %get-tuple-element.37.refs_2_, f32[640,128]{1,0:T(8,128)S(1)} %get-tuple-element.38.refs_3_, ...), custom_call_target="tpu_custom_call" | custom-call | tf_op jit(solution)/shard_map/pallas_call | solution.py:469
  13.0 0.0 collective-permute-done.4.refs_9_
  13.0 0.8 %collective-permute-done.refs_0_ = f32[328,128]{1,0:T(8,128)S(1)} collective-permute-done((f32[328,128]{1,0:T(8,128)S(1)}, f32[328,128]{1,0:T(8,128)S(1)}, u32[]{:S(2)}, u32[]{:S(2)}) %collective-permute-start) | collective-permute-done | bytes 167968 | tf_op jit(solution)/shard_map/ppermute | solution.py:485
  13.7 2.7 %collective-permute-done.1.refs_1_ = f32[328,128]{1,0:T(8,128)S(1)} collective-permute-done((f32[328,128]{1,0:T(8,128)S(1)}, f32[328,128]{1,0:T(8,128)S(1)}, u32[]{:S(2)}, u32[]{:S(2)}) %collective-permute-start.1) | collective-permute-done | bytes 167968 | tf_op jit(solution)/shard_map/ppermute | solution.py:485
  16.4 0.5 %shard_map.77 = (f32[320,128]{1,0:T(8,128)S(1)}, f32[320,128]{1,0:T(8,128)S(1)}, f32[640,128]{1,0:T(8,128)S(1)}, f32[640,128]{1,0:T(8,128)S(1)}, f32[64,128]{1,0:T(8,128)S(1)}, /*index=5*/s32[8,128]{1,0:T(8,128)S(1)}) custom-call(f32[328,128]{1,0:T(8,128)S(1)} %collective-permute-done.refs_0_, f32[328,128]{1,0:T(8,128)S(1)} %collective-permute-done.1.refs_1_, ...), custom_call_target="tpu_custom_call" | custom-call | tf_op jit(solution)/shard_map/pallas_call | solution.py:469
  16.9 1.5 %collective-permute-start.5 = (f32[320,128]{1,0:T(8,128)S(1)}, f32[320,128]{1,0:T(8,128)S(1)}, u32[]{:S(2)}, u32[]{:S(2)}) collective-permute-start(f32[320,128]{1,0:T(8,128)S(1)} %get-tuple-element.48), channel_id=1, source_target_pairs={{0,8},{8,16},{16,24},{24,0},{1,9},{9,17},{17,25},{25,1},{2,10},{10... | collective-permute-start | bytes 491528 | tf_op jit(solution)/shard_map/ppermute | solution.py:485
  18.4 1.4 %collective-permute-start.6 = (f32[320,128]{1,0:T(8,128)S(1)}, f32[320,128]{1,0:T(8,128)S(1)}, u32[]{:S(2)}, u32[]{:S(2)}) collective-permute-start(f32[320,128]{1,0:T(8,128)S(1)} %get-tuple-element.49), channel_id=1, source_target_pairs={{0,24},{8,0},{16,8},{24,16},{1,25},{9,1},{17,9},{25,17},{2,26},{10... | collective-permute-start | bytes 491528 | tf_op jit(solution)/shard_map/ppermute | solution.py:485
  19.9 0.7 %shard_map.78 = (f32[2560,128]{1,0:T(8,128)S(1)}, f32[40,128]{1,0:T(8,128)S(1)}) custom-call(f32[2560,128]{1,0:T(8,128)S(1)} %get-tuple-element.51.refs_0_, f32[640,128]{1,0:T(8,128)S(1)} %get-tuple-element.52.refs_1_, f32[640,128]{1,0:T(8,128)S(1)} %get-tuple-element.53.refs_2_, f32[64,128]{1,0:T(8,128)S(1)} %get-tuple-element.54.refs_3_.refs_2_), custom_call_target="tpu_custom_call" | custom-call | tf_op jit(solution)/shard_map/pallas_call | solution.py:469
  20.6 0.9 %collective-permute-start.8 = (f32[40,128]{1,0:T(8,128)S(1)}, f32[40,128]{1,0:T(8,128)S(1)}, u32[]{:S(2)}, u32[]{:S(2)}) collective-permute-start(f32[40,128]{1,0:T(8,128)S(1)} %get-tuple-element.56), channel_id=1, source_target_pairs={{1,2},{2,1},{3,4},{4,3},{5,6},{6,5},{0,16},{7,23},{9,10},{10,9},{1... | collective-permute-start | bytes 61448 | tf_op jit(solution)/shard_map/ppermute | solution.py:502
  21.5 0.8 %collective-permute-start.7 = (f32[40,128]{1,0:T(8,128)S(1)}, f32[40,128]{1,0:T(8,128)S(1)}, u32[]{:S(2)}, u32[]{:S(2)}) collective-permute-start(f32[40,128]{1,0:T(8,128)S(1)} %get-tuple-element.56), channel_id=1, source_target_pairs={{0,1},{1,0},{2,3},{3,2},{4,5},{5,4},{6,7},{7,6},{8,9},{9,8},{10,11... | collective-permute-start | bytes 61448 | tf_op jit(solution)/shard_map/ppermute | solution.py:501
  22.3 1.3 %shard_map.79.refs_1_ = f32[2560,128]{1,0:T(8,128)S(1)} custom-call(f32[2560,128]{1,0:T(8,128)S(1)} %get-tuple-element.55.refs_0_, s32[8,128]{1,0:T(8,128)S(1)} %get-tuple-element.35.refs_1_, f32[64,128]{1,0:T(8,128)S(1)} %get-tuple-element.54.refs_3_.refs_2_), custom_call_target="tpu_custom_call" | custom-call | tf_op jit(solution)/shard_map/pallas_call | solution.py:469
  23.6 1.0 %collective-permute-done.8.refs_6_ = f32[40,128]{1,0:T(8,128)S(1)} collective-permute-done((f32[40,128]{1,0:T(8,128)S(1)}, f32[40,128]{1,0:T(8,128)S(1)}, u32[]{:S(2)}, u32[]{:S(2)}) %collective-permute-start.8) | collective-permute-done | bytes 20512 | tf_op jit(solution)/shard_map/ppermute | solution.py:502
  24.6 0.0 collective-permute-done.7.refs_5_
  24.7 1.2 %shard_map.80 = (f32[2560,128]{1,0:T(8,128)S(1)}, f32[640,128]{1,0:T(8,128)S(1)}) custom-call(f32[2560,128]{1,0:T(8,128)S(1)} %get-tuple-element.55.refs_0_, f32[2560,128]{1,0:T(8,128)S(1)} %shard_map.79.refs_1_, f32[640,128]{1,0:T(8,128)S(1)} %get-tuple-element.37.refs_2_, f32[640,128]{1,0:T(8,128)S(1)} %get-tuple-element.38.refs_3_, ...), custom_call_target="tpu_custom_call" | custom-call | tf_op jit(solution)/shard_map/pallas_call | solution.py:469
  25.9 0.0 collective-permute-done.5.refs_0_
  25.9 0.5 %collective-permute-done.6.refs_1_ = f32[320,128]{1,0:T(8,128)S(1)} collective-permute-done((f32[320,128]{1,0:T(8,128)S(1)}, f32[320,128]{1,0:T(8,128)S(1)}, u32[]{:S(2)}, u32[]{:S(2)}) %collective-permute-start.6) | collective-permute-done | bytes 163872 | tf_op jit(solution)/shard_map/ppermute | solution.py:485
  26.3 1.5 %shard_map.81 = f32[2560,128]{1,0:T(8,128)} custom-call(f32[320,128]{1,0:T(8,128)S(1)} %collective-permute-done.5.refs_0_, f32[320,128]{1,0:T(8,128)S(1)} %collective-permute-done.6.refs_1_, f32[640,128]{1,0:T(8,128)S(1)} %get-tuple-element.50.refs_2_, f32[640,128]{1,0:T(8,128)S(1)} %get-tuple-element.58.refs_3_, ...), custom_call_target="tpu_custom_call" | custom-call | tf_op jit(solution)/shard_map/pallas_call | solution.py:469
  (1 shorter events, 0.0 us)
Async XLA Ops:
  0.0 1.7 %copy-start = (f32[4,80,8,128]{3,2,1,0:T(8,128)S(1)}, f32[4,80,8,128]{3,2,1,0:T(8,128)}, u32[]{:S(2)}) copy-start(f32[4,80,8,128]{3,2,1,0:T(8,128)} %param.7) | copy-start | bytes 3932164
  2.4 9.3 %collective-permute-start.3 = (f32[48,128]{1,0:T(8,128)S(1)}, f32[48,128]{1,0:T(8,128)S(1)}, u32[]{:S(2)}, u32[]{:S(2)}) collective-permute-start(f32[48,128]{1,0:T(8,128)S(1)} %get-tuple-element.42), channel_id=1, source_target_pairs={{1,2},{2,1},{3,4},{4,3},{5,6},{6,5},{0,16},{7,23},{9,10},{10,9},{1... | collective-permute-start | bytes 73736 | tf_op jit(solution)/shard_map/ppermute | solution.py:502
  5.5 6.2 %collective-permute-start.2 = (f32[48,128]{1,0:T(8,128)S(1)}, f32[48,128]{1,0:T(8,128)S(1)}, u32[]{:S(2)}, u32[]{:S(2)}) collective-permute-start(f32[48,128]{1,0:T(8,128)S(1)} %get-tuple-element.42), channel_id=1, source_target_pairs={{0,1},{1,0},{2,3},{3,2},{4,5},{5,4},{6,7},{7,6},{8,9},{9,8},{10,11... | collective-permute-start | bytes 73736 | tf_op jit(solution)/shard_map/ppermute | solution.py:501
  5.7 8.1 %collective-permute-start = (f32[328,128]{1,0:T(8,128)S(1)}, f32[328,128]{1,0:T(8,128)S(1)}, u32[]{:S(2)}, u32[]{:S(2)}) collective-permute-start(f32[328,128]{1,0:T(8,128)S(1)} %get-tuple-element.33.refs_2_), channel_id=1, source_target_pairs={{0,8},{8,16},{16,24},{24,0},{1,9},{9,17},{17,25},{25,1},{2,10},{10... | collective-permute-start | bytes 503816 | tf_op jit(solution)/shard_map/ppermute | solution.py:485
  7.2 9.3 %collective-permute-start.1 = (f32[328,128]{1,0:T(8,128)S(1)}, f32[328,128]{1,0:T(8,128)S(1)}, u32[]{:S(2)}, u32[]{:S(2)}) collective-permute-start(f32[328,128]{1,0:T(8,128)S(1)} %get-tuple-element.34.refs_3_), channel_id=1, source_target_pairs={{0,24},{8,0},{16,8},{24,16},{1,25},{9,1},{17,9},{25,17},{2,26},{10... | collective-permute-start | bytes 503816 | tf_op jit(solution)/shard_map/ppermute | solution.py:485
  8.6 4.4 %collective-permute-start.4 = (f32[8,128]{1,0:T(8,128)S(1)}, f32[8,128]{1,0:T(8,128)S(1)}, u32[]{:S(2)}, u32[]{:S(2)}) collective-permute-start(f32[8,128]{1,0:T(8,128)S(1)} %slice_bitcast_fusion), channel_id=1, source_target_pairs={{0,16},{8,24},{16,0},{24,8},{1,17},{9,25},{17,1},{25,9},{2,18},{10... | collective-permute-start | bytes 12296 | tf_op jit(solution)/shard_map/ppermute | solution.py:485
  16.9 9.0 %collective-permute-start.5 = (f32[320,128]{1,0:T(8,128)S(1)}, f32[320,128]{1,0:T(8,128)S(1)}, u32[]{:S(2)}, u32[]{:S(2)}) collective-permute-start(f32[320,128]{1,0:T(8,128)S(1)} %get-tuple-element.48), channel_id=1, source_target_pairs={{0,8},{8,16},{16,24},{24,0},{1,9},{9,17},{17,25},{25,1},{2,10},{10... | collective-permute-start | bytes 491528 | tf_op jit(solution)/shard_map/ppermute | solution.py:485
  18.4 7.9 %collective-permute-start.6 = (f32[320,128]{1,0:T(8,128)S(1)}, f32[320,128]{1,0:T(8,128)S(1)}, u32[]{:S(2)}, u32[]{:S(2)}) collective-permute-start(f32[320,128]{1,0:T(8,128)S(1)} %get-tuple-element.49), channel_id=1, source_target_pairs={{0,24},{8,0},{16,8},{24,16},{1,25},{9,1},{17,9},{25,17},{2,26},{10... | collective-permute-start | bytes 491528 | tf_op jit(solution)/shard_map/ppermute | solution.py:485
  20.6 4.1 %collective-permute-start.8 = (f32[40,128]{1,0:T(8,128)S(1)}, f32[40,128]{1,0:T(8,128)S(1)}, u32[]{:S(2)}, u32[]{:S(2)}) collective-permute-start(f32[40,128]{1,0:T(8,128)S(1)} %get-tuple-element.56), channel_id=1, source_target_pairs={{1,2},{2,1},{3,4},{4,3},{5,6},{6,5},{0,16},{7,23},{9,10},{10,9},{1... | collective-permute-start | bytes 61448 | tf_op jit(solution)/shard_map/ppermute | solution.py:502
  21.5 3.2 %collective-permute-start.7 = (f32[40,128]{1,0:T(8,128)S(1)}, f32[40,128]{1,0:T(8,128)S(1)}, u32[]{:S(2)}, u32[]{:S(2)}) collective-permute-start(f32[40,128]{1,0:T(8,128)S(1)} %get-tuple-element.56), channel_id=1, source_target_pairs={{0,1},{1,0},{2,3},{3,2},{4,5},{5,4},{6,7},{7,6},{8,9},{9,8},{10,11... | collective-permute-start | bytes 61448 | tf_op jit(solution)/shard_map/ppermute | solution.py:501
